TPU v7x, 32 devices: a whole 2x2x4 slice. The times are simulated.
32 devices in a mesh: row: 4 (over y, x), seq: 8 (over z, core).
Axes of the slice: x: 2, y: 2, z: 4, core: 2. Of those that a mesh axis runs over, the one named last changes fastest.
Arguments:
- tokens: bfloat16 [8, 1024, 1024], P('row', 'seq'), may hold values from -6 to 6
- segment_ids: int32 [8, 1024], P('row'), may hold values from 0 to 7, never falling along the last dimension, each value on 1 to 512 neighbouring positions
- expert_ids: int32 [8, 8, 128, 8], P('seq', 'row'), may hold values from 0 to 15, as said below
- norm1_gain: bfloat16 [1024], P(('row', 'seq')), may hold values from 0.5 to 1.5
- w_query: bfloat16 [1024, 1024], P(('row', 'seq')), may hold values from -0.75 to 0.75
- w_key: bfloat16 [1024, 512], P(('row', 'seq')), may hold values from -0.75 to 0.75
- w_value: bfloat16 [1024, 512], P(('row', 'seq')), may hold values from -0.1875 to 0.1875
- w_out: bfloat16 [1024, 1024], P(None, ('row', 'seq')), may hold values from -2 to 2
- norm2_gain: bfloat16 [1024], P(('row', 'seq')), may hold values from 0.5 to 1.5
- w_router: bfloat16 [1024, 16], P(('row', 'seq')), may hold values from -0.09375 to 0.09375
- w_gate: bfloat16 [16, 1024, 512], P(None, ('row', 'seq')), may hold values from -0.1875 to 0.1875
- w_up: bfloat16 [16, 1024, 512], P(None, ('row', 'seq')), may hold values from -0.1875 to 0.1875
- w_down: bfloat16 [16, 512, 1024], P(None, None, ('row', 'seq')), may hold values from -4 to 4
- out_grad: bfloat16 [8, 1024, 1024], P('row', 'seq'), may hold values from -6 to 6
Outputs:
- layer_out: bfloat16 [8, 1024, 1024], P('row', 'seq')
- input_grad: float32 [8, 1024, 1024], P('row', 'seq')
- grad_norm1_gain: float32 [1024], P(('row', 'seq'))
- grad_w_query: float32 [1024, 1024], P(('row', 'seq'))
- grad_w_key: float32 [1024, 512], P(('row', 'seq'))
- grad_w_value: float32 [1024, 512], P(('row', 'seq'))
- grad_w_out: float32 [1024, 1024], P(None, ('row', 'seq'))
- grad_norm2_gain: float32 [1024], P(('row', 'seq'))
- grad_w_router: float32 [1024, 16], P(('row', 'seq'))
- grad_w_gate: float32 [16, 1024, 512], P(None, ('row', 'seq'))
- grad_w_up: float32 [16, 1024, 512], P(None, ('row', 'seq'))
- grad_w_down: float32 [16, 512, 1024], P(None, None, ('row', 'seq'))
- expert_counts: int32 [16], replicated
Inputs may be any that keep to these rules, and one draw needn't show every extreme that they name: `segment_ids`: along a row segment ids never fall; each of the 8 ids covers 1 to 512 consecutive tokens, and one covers exactly that many. `expert_ids`: A token names 8 different experts. Among the tokens of one device (one index of seq and of row), no expert is named by more than 192 tokens, and in every draw some expert is named by exactly 192 of them; every expert is named by some token of each device.
All inputs are finite; a program needn't handle non-finite values.
Results may differ from a plain program's by a relative error of at most 0.015.
Values may be sent and summed in bfloat16 or wider, within the bound.
A program may use at most 320 MiB of HBM per device.

v0:
```python
import jax
import jax.numpy as jnp
from jax import lax
from jax.sharding import PartitionSpec as P

HEADS = 16
KV_HEADS = 8
HEAD = 64
GROUP = 2
EXPERTS = 16
TOPK = 8
CAP = 192


EPSILON = 1e-06
SCORE_SCALE = 0.015625
RESIDUAL = 0.22
THETA = 10000.0
NEGATIVE = -1e30


def norm_scale(value):
    return lax.rsqrt(jnp.mean(value * value, axis=-1, keepdims=True) + EPSILON)


def positions_of(segments):
    length = segments.shape[-1]
    index = jnp.arange(length, dtype=jnp.int32)
    change = jnp.concatenate(
        [jnp.ones_like(segments[:, :1]), (segments[:, 1:] != segments[:, :-1]).astype(jnp.int32)],
        axis=1,
    )
    start = lax.cummax(jnp.where(change > 0, index[None, :], 0), axis=1)
    return index[None, :] - start


def rope_tables(positions, width):
    half = width // 2
    frequency = THETA ** (-2.0 * jnp.arange(half, dtype=jnp.float32) / width)
    angle = positions.astype(jnp.float32)[..., None] * frequency
    angle = jnp.concatenate([angle, angle], axis=-1)
    return (jnp.cos(angle), jnp.sin(angle))


def rotate(value, cosine, sine):
    half = value.shape[-1] // 2
    turned = jnp.concatenate([-value[..., half:], value[..., :half]], axis=-1)
    return value * cosine[..., None, :] + turned * sine[..., None, :]


def rotate_back(delta, cosine, sine):
    half = delta.shape[-1] // 2
    moved = delta * sine[..., None, :]
    turned = jnp.concatenate([moved[..., half:], -moved[..., :half]], axis=-1)
    return delta * cosine[..., None, :] + turned


def visible_keys(row_segments, query_segments, first):
    key_index = jnp.arange(row_segments.shape[0], dtype=jnp.int32)
    query_index = first + jnp.arange(query_segments.shape[0], dtype=jnp.int32)
    return (query_segments[:, None] == row_segments[None, :]) & (
        key_index[None, :] <= query_index[:, None]
    )


def row_scores(query_row, row_keys, visible):
    raw = jnp.einsum("ckgd,lkd->kgcl", query_row, row_keys, preferred_element_type=jnp.float32)
    return jnp.where(visible, SCORE_SCALE * raw, NEGATIVE)


def body(
    tokens,
    segment_ids,
    expert_ids,
    norm1_gain,
    w_query,
    w_key,
    w_value,
    w_out,
    norm2_gain,
    w_router,
    w_gate,
    w_up,
    w_down,
    out_grad,
):
    row_count, block_len, width = tokens.shape
    token_count = row_count * block_len
    length = segment_ids.shape[1]
    first = lax.axis_index("seq") * block_len
    gain_one, query_weight, key_weight, value_weight, out_weight, gain_two, router_weight = (
        lax.all_gather(norm1_gain, ("row", "seq"), axis=0, tiled=True),
        lax.all_gather(w_query, ("row", "seq"), axis=0, tiled=True),
        lax.all_gather(w_key, ("row", "seq"), axis=0, tiled=True),
        lax.all_gather(w_value, ("row", "seq"), axis=0, tiled=True),
        lax.all_gather(w_out, ("row", "seq"), axis=1, tiled=True),
        lax.all_gather(norm2_gain, ("row", "seq"), axis=0, tiled=True),
        lax.all_gather(w_router, ("row", "seq"), axis=0, tiled=True),
    )
    gate_all, up_all, down_all = (
        lax.all_gather(w_gate, ("row", "seq"), axis=1, tiled=True),
        lax.all_gather(w_up, ("row", "seq"), axis=1, tiled=True),
        lax.all_gather(w_down, ("row", "seq"), axis=2, tiled=True),
    )
    flat = tokens.reshape(token_count, width).astype(jnp.float32)
    scale_one = norm_scale(flat)
    normed = (flat * scale_one * gain_one.astype(jnp.float32)).astype(jnp.bfloat16)
    local_positions = lax.dynamic_slice_in_dim(
        positions_of(segment_ids), first, block_len, axis=1
    ).reshape(token_count)
    local_segments = lax.dynamic_slice_in_dim(segment_ids, first, block_len, axis=1)
    cosine, sine = rope_tables(local_positions, HEAD)
    query = jnp.dot(normed, query_weight, preferred_element_type=jnp.float32).reshape(
        token_count, HEADS, HEAD
    )
    query = (
        rotate(query, cosine, sine)
        .astype(jnp.bfloat16)
        .reshape(row_count, block_len, KV_HEADS, GROUP, HEAD)
    )
    keys = jnp.dot(normed, key_weight, preferred_element_type=jnp.float32).reshape(
        token_count, KV_HEADS, HEAD
    )
    keys = (
        rotate(keys, cosine, sine)
        .astype(jnp.bfloat16)
        .reshape(row_count, block_len, KV_HEADS * HEAD)
    )
    values = (
        jnp.dot(normed, value_weight, preferred_element_type=jnp.float32)
        .astype(jnp.bfloat16)
        .reshape(row_count, block_len, KV_HEADS * HEAD)
    )
    key_rows, value_rows = (
        lax.all_gather(keys, "seq", axis=1, tiled=True),
        lax.all_gather(values, "seq", axis=1, tiled=True),
    )

    def attend_forward(carry, items):
        query_row, row_keys, row_values, row_segments, query_segments = items
        row_keys = row_keys.reshape(length, KV_HEADS, HEAD)
        row_values = row_values.reshape(length, KV_HEADS, HEAD)
        scores = row_scores(query_row, row_keys, visible_keys(row_segments, query_segments, first))
        peak = jnp.max(scores, axis=-1, keepdims=True)
        raised = jnp.exp(scores - peak)
        denominator = jnp.sum(raised, axis=-1, keepdims=True)
        probs = (raised / denominator).astype(jnp.bfloat16)
        mixed_row = jnp.einsum(
            "kgcl,lkd->ckgd", probs, row_values, preferred_element_type=jnp.float32
        )
        return (
            carry,
            (
                mixed_row.astype(jnp.bfloat16).reshape(block_len, HEADS * HEAD),
                peak + jnp.log(denominator),
            ),
        )

    _, (mixed, log_total) = lax.scan(
        attend_forward, None, (query, key_rows, value_rows, segment_ids, local_segments)
    )
    mixed = mixed.reshape(token_count, HEADS * HEAD)
    hidden = flat + RESIDUAL * jnp.dot(mixed, out_weight, preferred_element_type=jnp.float32)
    scale_two = norm_scale(hidden)
    normed_two = (hidden * scale_two * gain_two.astype(jnp.float32)).astype(jnp.bfloat16)
    logits = jnp.dot(normed_two, router_weight, preferred_element_type=jnp.float32)
    routes = expert_ids.reshape(token_count, TOPK)
    chosen = routes[:, :, None] == jnp.arange(EXPERTS, dtype=jnp.int32)[None, None, :]
    chosen_float = chosen.astype(jnp.float32)
    gates = jax.nn.softmax(jnp.sum(chosen_float * logits[:, None, :], axis=-1), axis=-1)
    expert_counts = lax.psum(jnp.sum(chosen.astype(jnp.int32), axis=(0, 1)), ("row", "seq"))
    assignments = token_count * TOPK
    onehot = chosen.reshape(assignments, EXPERTS).astype(jnp.int32)
    before = jnp.cumsum(onehot, axis=0) - onehot
    target = routes.reshape(-1) * CAP + jnp.sum(before * onehot, axis=1)
    source = (
        jnp.zeros((EXPERTS * CAP,), jnp.int32)
        .at[target]
        .set(jnp.arange(assignments, dtype=jnp.int32))
    )
    filled = jnp.zeros((EXPERTS * CAP,), jnp.bool_).at[target].set(True)
    owner = source // TOPK
    empty_row = jnp.zeros((), jnp.bfloat16)
    expert_rows = jnp.where(filled[:, None], normed_two[owner], empty_row).reshape(
        EXPERTS, CAP, width
    )
    gate_part = jnp.einsum(
        "ecd,edf->ecf", expert_rows, gate_all, preferred_element_type=jnp.float32
    )
    up_part = jnp.einsum("ecd,edf->ecf", expert_rows, up_all, preferred_element_type=jnp.float32)
    inner = (jax.nn.silu(gate_part) * up_part).astype(jnp.bfloat16)
    result = jnp.einsum("ecf,efd->ecd", inner, down_all, preferred_element_type=jnp.float32)
    returned = result.reshape(EXPERTS * CAP, width)[target].reshape(token_count, TOPK, width)
    mixture = jnp.sum(gates[:, :, None] * returned, axis=1)
    layer_out = (
        (hidden + RESIDUAL * mixture).astype(jnp.bfloat16).reshape(row_count, block_len, width)
    )
    back_gain_one, back_query, back_key, back_value, back_out, back_gain_two, back_router = (
        lax.all_gather(norm1_gain, ("row", "seq"), axis=0, tiled=True),
        lax.all_gather(w_query, ("row", "seq"), axis=0, tiled=True),
        lax.all_gather(w_key, ("row", "seq"), axis=0, tiled=True),
        lax.all_gather(w_value, ("row", "seq"), axis=0, tiled=True),
        lax.all_gather(w_out, ("row", "seq"), axis=1, tiled=True),
        lax.all_gather(norm2_gain, ("row", "seq"), axis=0, tiled=True),
        lax.all_gather(w_router, ("row", "seq"), axis=0, tiled=True),
    )
    back_gate, back_up, back_down = (
        lax.all_gather(w_gate, ("row", "seq"), axis=1, tiled=True),
        lax.all_gather(w_up, ("row", "seq"), axis=1, tiled=True),
        lax.all_gather(w_down, ("row", "seq"), axis=2, tiled=True),
    )
    delta_out = out_grad.reshape(token_count, width).astype(jnp.float32)
    delta_mixture = RESIDUAL * delta_out
    delta_gates = jnp.sum(delta_mixture[:, None, :] * returned, axis=-1)
    delta_returned = (
        (gates[:, :, None] * delta_mixture[:, None, :])
        .astype(jnp.bfloat16)
        .reshape(assignments, width)
    )
    delta_result = jnp.where(filled[:, None], delta_returned[source], empty_row).reshape(
        EXPERTS, CAP, width
    )
    delta_down = jnp.einsum("ecf,ecd->efd", inner, delta_result, preferred_element_type=jnp.float32)
    delta_inner = jnp.einsum(
        "ecd,efd->ecf", delta_result, back_down, preferred_element_type=jnp.float32
    )
    sigma = jax.nn.sigmoid(gate_part)
    delta_gate_part = (delta_inner * up_part * sigma * (1.0 + gate_part * (1.0 - sigma))).astype(
        jnp.bfloat16
    )
    delta_up_part = (delta_inner * gate_part * sigma).astype(jnp.bfloat16)
    delta_gate = jnp.einsum(
        "ecd,ecf->edf", expert_rows, delta_gate_part, preferred_element_type=jnp.float32
    )
    delta_up = jnp.einsum(
        "ecd,ecf->edf", expert_rows, delta_up_part, preferred_element_type=jnp.float32
    )
    delta_rows = jnp.einsum(
        "ecf,edf->ecd", delta_gate_part, back_gate, preferred_element_type=jnp.float32
    ) + jnp.einsum("ecf,edf->ecd", delta_up_part, back_up, preferred_element_type=jnp.float32)
    from_experts = jnp.sum(
        delta_rows.reshape(EXPERTS * CAP, width)[target].reshape(token_count, TOPK, width), axis=1
    )
    delta_picked = gates * (delta_gates - jnp.sum(gates * delta_gates, axis=-1, keepdims=True))
    delta_logits = jnp.sum(chosen_float * delta_picked[:, :, None], axis=1).astype(jnp.bfloat16)
    delta_router = jnp.dot(normed_two.T, delta_logits, preferred_element_type=jnp.float32)
    delta_normed_two = from_experts + jnp.dot(
        delta_logits, back_router.T, preferred_element_type=jnp.float32
    )
    weighted_two = back_gain_two.astype(jnp.float32) * delta_normed_two
    delta_gain_two = jnp.sum(delta_normed_two * hidden * scale_two, axis=0)
    delta_hidden = (
        delta_out
        + scale_two * weighted_two
        - hidden
        * (scale_two * scale_two * scale_two)
        * jnp.mean(weighted_two * hidden, axis=-1, keepdims=True)
    )
    delta_branch = (RESIDUAL * delta_hidden).astype(jnp.bfloat16)
    delta_out_weight = jnp.dot(mixed.T, delta_branch, preferred_element_type=jnp.float32)
    delta_mixed = (
        jnp.dot(delta_branch, back_out.T, preferred_element_type=jnp.float32)
        .astype(jnp.bfloat16)
        .reshape(row_count, block_len, KV_HEADS, GROUP, HEAD)
    )

    def score_grads(
        query_row, row_keys, row_values, row_segments, query_segments, delta_row, log_row
    ):
        scores = row_scores(query_row, row_keys, visible_keys(row_segments, query_segments, first))
        probs = jnp.exp(scores - log_row)
        delta_probs = jnp.einsum(
            "ckgd,lkd->kgcl", delta_row, row_values, preferred_element_type=jnp.float32
        )
        inner_sum = jnp.sum(probs * delta_probs, axis=-1, keepdims=True)
        delta_scores = (probs * (delta_probs - inner_sum)).astype(jnp.bfloat16)
        return (probs, delta_scores, inner_sum)

    def attend_backward(carry, items):
        query_row, row_keys, row_values, row_segments, query_segments, delta_row, log_row = items
        row_keys = row_keys.reshape(length, KV_HEADS, HEAD)
        row_values = row_values.reshape(length, KV_HEADS, HEAD)
        probs, delta_scores, inner_sum = score_grads(
            query_row, row_keys, row_values, row_segments, query_segments, delta_row, log_row
        )
        delta_query = (
            jnp.einsum("kgcl,lkd->ckgd", delta_scores, row_keys, preferred_element_type=jnp.float32)
            * SCORE_SCALE
        )
        delta_keys = (
            jnp.einsum(
                "kgcl,ckgd->lkd", delta_scores, query_row, preferred_element_type=jnp.float32
            )
            * SCORE_SCALE
        )
        delta_values = jnp.einsum(
            "kgcl,ckgd->lkd",
            probs.astype(jnp.bfloat16),
            delta_row,
            preferred_element_type=jnp.float32,
        )
        return (
            carry,
            (
                delta_query.reshape(block_len, HEADS * HEAD),
                delta_keys.reshape(length, KV_HEADS * HEAD),
                delta_values.reshape(length, KV_HEADS * HEAD),
            ),
        )

    _, (delta_query, delta_key_rows, delta_value_rows) = lax.scan(
        attend_backward,
        None,
        (query, key_rows, value_rows, segment_ids, local_segments, delta_mixed, log_total),
    )
    delta_keys, delta_values = (
        lax.psum_scatter(delta_key_rows, "seq", scatter_dimension=1, tiled=True),
        lax.psum_scatter(delta_value_rows, "seq", scatter_dimension=1, tiled=True),
    )
    delta_query = (
        rotate_back(delta_query.reshape(token_count, HEADS, HEAD), cosine, sine)
        .astype(jnp.bfloat16)
        .reshape(token_count, HEADS * HEAD)
    )
    delta_keys = (
        rotate_back(delta_keys.reshape(token_count, KV_HEADS, HEAD), cosine, sine)
        .astype(jnp.bfloat16)
        .reshape(token_count, KV_HEADS * HEAD)
    )
    delta_values = delta_values.reshape(token_count, KV_HEADS * HEAD).astype(jnp.bfloat16)
    delta_query_weight = jnp.dot(normed.T, delta_query, preferred_element_type=jnp.float32)
    delta_key_weight = jnp.dot(normed.T, delta_keys, preferred_element_type=jnp.float32)
    delta_value_weight = jnp.dot(normed.T, delta_values, preferred_element_type=jnp.float32)
    delta_normed = (
        jnp.dot(delta_query, back_query.T, preferred_element_type=jnp.float32)
        + jnp.dot(delta_keys, back_key.T, preferred_element_type=jnp.float32)
        + jnp.dot(delta_values, back_value.T, preferred_element_type=jnp.float32)
    )
    weighted_one = back_gain_one.astype(jnp.float32) * delta_normed
    delta_gain_one = jnp.sum(delta_normed * flat * scale_one, axis=0)
    input_grad = (
        delta_hidden
        + scale_one * weighted_one
        - flat
        * (scale_one * scale_one * scale_one)
        * jnp.mean(weighted_one * flat, axis=-1, keepdims=True)
    )
    dense = (
        lax.psum_scatter(delta_gain_one, ("row", "seq"), scatter_dimension=0, tiled=True),
        lax.psum_scatter(delta_query_weight, ("row", "seq"), scatter_dimension=0, tiled=True),
        lax.psum_scatter(delta_key_weight, ("row", "seq"), scatter_dimension=0, tiled=True),
        lax.psum_scatter(delta_value_weight, ("row", "seq"), scatter_dimension=0, tiled=True),
        lax.psum_scatter(delta_out_weight, ("row", "seq"), scatter_dimension=1, tiled=True),
        lax.psum_scatter(delta_gain_two, ("row", "seq"), scatter_dimension=0, tiled=True),
        lax.psum_scatter(delta_router, ("row", "seq"), scatter_dimension=0, tiled=True),
    )
    experts = (
        lax.psum_scatter(delta_gate, ("row", "seq"), scatter_dimension=1, tiled=True),
        lax.psum_scatter(delta_up, ("row", "seq"), scatter_dimension=1, tiled=True),
        lax.psum_scatter(delta_down, ("row", "seq"), scatter_dimension=2, tiled=True),
    )
    return (
        layer_out,
        input_grad.reshape(row_count, block_len, width),
        dense[0],
        dense[1],
        dense[2],
        dense[3],
        dense[4],
        dense[5],
        dense[6],
        experts[0],
        experts[1],
        experts[2],
        expert_counts,
    )


def solution(mesh):
    in_specs = (
        P("row", "seq", None),
        P("row", None),
        P("seq", "row", None, None),
        P(("row", "seq")),
        P(("row", "seq"), None),
        P(("row", "seq"), None),
        P(("row", "seq"), None),
        P(None, ("row", "seq")),
        P(("row", "seq")),
        P(("row", "seq"), None),
        P(None, ("row", "seq"), None),
        P(None, ("row", "seq"), None),
        P(None, None, ("row", "seq")),
        P("row", "seq", None),
    )
    out_specs = (
        P("row", "seq", None),
        P("row", "seq", None),
        P(("row", "seq")),
        P(("row", "seq"), None),
        P(("row", "seq"), None),
        P(("row", "seq"), None),
        P(None, ("row", "seq")),
        P(("row", "seq")),
        P(("row", "seq"), None),
        P(None, ("row", "seq"), None),
        P(None, ("row", "seq"), None),
        P(None, None, ("row", "seq")),
        P(),
    )
    return jax.shard_map(body, mesh=mesh, in_specs=in_specs, out_specs=out_specs, check_vma=False)
```

profile of v0, /device:TPU:0, one launch (start us, length us, event | category | flops | bytes accessed | tf_op | source)
XLA Modules:
  0.0 2709.3 jit_solution(6154057037551149125)
XLA Ops:
  13.2 42.1 %all-reduce.6 = (bf16[1024]{0:T(1024)(128)(2,1)S(1)}, bf16[1024]{0:T(1024)(128)(2,1)S(1)}) all-reduce(bf16[1024]{0:T(1024)(128)(2,1)S(1)} %dynamic-update-slice, bf16[1024]{0:T(1024)(128)(2,1)S(1)} %dynamic-update-slice.1), channel_id=1, replica_groups=mesh['row'=4,'seq'=8] {'row','seq'}, use_global_device_ids=true, to_apply=%add.1 | all-reduce | flops 2048 | bytes 8192
  58.0 9.6 all-gather.15.cloned.1.call-done
  70.9 52.5 %all-gather.11.cloned.1.call-done = bf16[1024,512]{1,0:T(8,128)(2,1)} async-done(((bf16[32,512]{1,0:T(8,128)(2,1)}), bf16[1024,512]{1,0:T(8,128)(2,1)}) %all-gather.11.cloned.1.call-update) | async-done | bytes 1048592 | tf_op jit(solution)/shard_map/all_gather | solution.py:95
  129.3 40.1 %all-gather = bf16[32,32,16]{1,2,0:T(8,128)(2,1)S(1)} all-gather(bf16[1,32,16]{1,2,0:T(8,128)(2,1)S(1)} %bitcast.394), channel_id=1, replica_groups=mesh['row'=4,'seq'=8] {'row','seq'}, dimensions={0}, use_global_device_ids=true | all-gather | bytes 33792 | tf_op jit(solution)/shard_map/all_gather | solution.py:98
  169.7 4.5 reduce-window.16
  175.3 8.1 scatter_custom_fusion.1
  183.4 9.3 scatter_custom_fusion
  194.6 2.9 copy.137
  198.8 15.0 all-gather.17.cloned.1.call-done
  213.8 31.9 %all-gather.13.cloned.1.call-done = bf16[2,1024,512]{1,2,0:T(8,128)(2,1)} async-done(((bf16[2,128,512]{1,2,0:T(8,128)(2,1)}), bf16[2,1024,512]{1,2,0:T(8,128)(2,1)}) %all-gather.13.cloned.1.call-update) | async-done | bytes 2097168 | tf_op jit(solution)/shard_map/all_gather | solution.py:136
  245.8 15.4 while.26
  250.9 2.3 fusion.192
  258.7 2.3 fusion.192
  261.2 43.0 %all-gather.21.cloned.1.call-done = bf16[1024,1024]{0,1:T(8,128)(2,1)} async-done(((bf16[1024,32]{0,1:T(8,128)(2,1)}), bf16[1024,1024]{0,1:T(8,128)(2,1)}) %all-gather.21.cloned.1.call-update) | async-done | bytes 2097168 | tf_op jit(solution)/shard_map/all_gather | solution.py:96
  304.2 2.5 multiply_reduce_fusion.2
  308.4 13.9 gather_fusion
  322.4 2.4 fusion.39
  324.8 18.9 gather_fusion.2
  343.7 77.5 %all-gather.25.cloned.1.call-done = bf16[16,1024,512]{2,1,0:T(8,128)(2,1)} async-done(((bf16[16,32,512]{2,1,0:T(8,128)(2,1)}), bf16[16,1024,512]{2,1,0:T(8,128)(2,1)}) %all-gather.25.cloned.1.call-update) | async-done | bytes 16777232 | tf_op jit(solution)/shard_map/all_gather | solution.py:102
  421.2 13.6 fusion.46
  434.8 102.9 %all-gather.23.cloned.1.call-done = bf16[16,1024,512]{2,1,0:T(8,128)(2,1)} async-done(((bf16[16,32,512]{2,1,0:T(8,128)(2,1)}), bf16[16,1024,512]{2,1,0:T(8,128)(2,1)}) %all-gather.23.cloned.1.call-update) | async-done | bytes 16777232 | tf_op jit(solution)/shard_map/all_gather | solution.py:101
  537.7 13.7 fusion.47
  551.4 102.9 %all-gather.27.cloned.1.call-done = bf16[16,512,1024]{1,2,0:T(8,128)(2,1)} async-done(((bf16[16,512,32]{1,2,0:T(8,128)(2,1)}), bf16[16,512,1024]{1,2,0:T(8,128)(2,1)}) %all-gather.27.cloned.1.call-update) | async-done | bytes 16777232 | tf_op jit(solution)/shard_map/all_gather | solution.py:103
  654.3 17.5 multiply_convert_fusion
  671.8 12.8 fusion.111
  684.6 16.3 gather_fusion.1
  701.0 6.8 fusion.41
  708.0 12.9 fusion.112
  720.8 15.5 convolution_add_fusion
  736.4 16.4 gather_fusion.3
  752.8 5.8 bitcast_reduce_fusion
  764.4 65.8 %while.27 = (s32[]{:T(128)}, f32[2,128,1024]{1,2,0:T(8,128)}, f32[2,1024,512]{2,1,0:T(8,128)}, f32[2,1024,512]{2,1,0:T(8,128)}, bf16[2,1024,512]{1,2,0:T(8,128)(...) while((s32[]{:T(128)}, f32[2,128,1024]{1,2,0:T(8,128)}, ...), condition=%wide.region_24.25_spmd, body=%wide.region_22.24_spmd.sunk | while | flops 1374681216 | bytes 184623536 | solution.py:311
  770.7 2.5 fusion.205
  773.3 2.5 fusion.206
  781.1 7.0 fusion.207
  788.0 2.9 copy.207
  790.9 4.2 constant_dynamic-update-slice_fusion.9
  798.8 2.3 fusion.202
  803.5 2.5 fusion.205
  806.1 2.5 fusion.206
  813.9 7.0 fusion.207
  820.8 2.9 copy.207
  823.7 4.2 constant_dynamic-update-slice_fusion.9
  837.9 2.7 fusion.114
  840.8 2.8 fusion.74
  843.7 35.0 %reduce-scatter.13.cloned.1.call-done = f32[2,128,512]{2,1,0:T(8,128)} async-done(((f32[2,1024,512]{2,1,0:T(8,128)}), f32[2,128,512]{2,1,0:T(8,128)}) %reduce-scatter.13.cloned.1.call-update) | async-done | bytes 524304 | tf_op jit(solution)/shard_map/reduce_scatter | solution.py:317
  883.3 2.8 fusion.115
  886.2 43.0 %reduce-scatter.15.cloned.1.call-done = f32[2,128,512]{2,1,0:T(8,128)} async-done(((f32[2,1024,512]{2,1,0:T(8,128)}), f32[2,128,512]{2,1,0:T(8,128)}) %reduce-scatter.15.cloned.1.call-update) | async-done | bytes 524304 | tf_op jit(solution)/shard_map/reduce_scatter | solution.py:318
  930.3 2.8 convolution_bitcast_fusion
  933.2 15.2 fusion.42
  950.3 15.2 fusion.45
  967.3 15.3 fusion.44
  983.4 38.0 %psum.7 = s32[16]{0:T(128)} all-reduce(s32[16]{0:T(128)S(1)} %convert_reduce_fusion), channel_id=1, replica_groups=mesh['row'=4,'seq'=8] {'row','seq'}, use_global_device_ids=true, to_apply=%region_41.42 | all-reduce | flops 16 | bytes 128 | tf_op jit(solution)/shard_map/psum | solution.py:171
  1025.1 2.6 copy.151
  1030.9 2.4 fusion.113
  1033.3 30.1 %reduce-scatter.31.cloned.1.call-done = f32[32,16]{1,0:T(8,128)} async-done(((f32[1024,16]{1,0:T(8,128)}), f32[32,16]{1,0:T(8,128)}) %reduce-scatter.31.cloned.1.call-update) | async-done | bytes 2064
  1071.0 37.9 %all-reduce.5 = (f32[1024]{0:T(1024)S(1)}, f32[1024]{0:T(1024)S(1)}) all-reduce(f32[1024]{0:T(1024)S(1)} %get-tuple-element.239, f32[1024]{0:T(1024)S(1)} %copy-done.59), channel_id=4, replica_groups=mesh['row'=4,'seq'=8] {'row','seq'}, use_global_device_ids=true, to_apply=%region_29.30.clone | all-reduce | flops 2048 | bytes 16384
  1111.3 93.9 %reduce-scatter.17.cloned.1.call-done = f32[32,1024]{1,0:T(8,128)} async-done(((f32[1024,1024]{1,0:T(8,128)}), f32[32,1024]{1,0:T(8,128)}) %reduce-scatter.17.cloned.1.call-update) | async-done | bytes 131088 | tf_op jit(solution)/shard_map/reduce_scatter | solution.py:350
  1205.2 143.1 %reduce-scatter.23.cloned.1.call-done = f32[1024,32]{0,1:T(8,128)} async-done(((f32[1024,1024]{0,1:T(8,128)}), f32[1024,32]{0,1:T(8,128)}) %reduce-scatter.23.cloned.1.call-update) | async-done | bytes 131088 | tf_op jit(solution)/shard_map/reduce_scatter | solution.py:353
  1348.3 136.8 %reduce-scatter.19.cloned.1.call-done = f32[32,512]{1,0:T(8,128)} async-done(((f32[1024,512]{1,0:T(8,128)}), f32[32,512]{1,0:T(8,128)}) %reduce-scatter.19.cloned.1.call-update) | async-done | bytes 65552 | tf_op jit(solution)/shard_map/reduce_scatter | solution.py:351
  1485.1 135.8 %reduce-scatter.21.cloned.1.call-done = f32[32,512]{1,0:T(8,128)} async-done(((f32[1024,512]{1,0:T(8,128)}), f32[32,512]{1,0:T(8,128)}) %reduce-scatter.21.cloned.1.call-update) | async-done | bytes 65552 | tf_op jit(solution)/shard_map/reduce_scatter | solution.py:352
  1620.8 360.4 %reduce-scatter.29.cloned.1.call-done = f32[16,512,32]{1,2,0:T(8,128)} async-done(((f32[16,512,1024]{1,2,0:T(8,128)}), f32[16,512,32]{1,2,0:T(8,128)}) %reduce-scatter.29.cloned.1.call-update) | async-done | bytes 1048592 | tf_op jit(solution)/shard_map/reduce_scatter | solution.py:360
  1981.2 360.5 %reduce-scatter.25.cloned.1.call-done = f32[16,32,512]{2,1,0:T(8,128)} async-done(((f32[16,1024,512]{2,1,0:T(8,128)}), f32[16,32,512]{2,1,0:T(8,128)}) %reduce-scatter.25.cloned.1.call-update) | async-done | bytes 1048592 | tf_op jit(solution)/shard_map/reduce_scatter | solution.py:358
  2341.7 360.6 %reduce-scatter.27.cloned.1.call-done = f32[16,32,512]{2,1,0:T(8,128)} async-done(((f32[16,1024,512]{2,1,0:T(8,128)}), f32[16,32,512]{2,1,0:T(8,128)}) %reduce-scatter.27.cloned.1.call-update) | async-done | bytes 1048592 | tf_op jit(solution)/shard_map/reduce_scatter | solution.py:359
  (345 shorter events, 100.1 us)
Async XLA Ops:
  7.2 63.5 %copy-start.18 = (bf16[2,128,1024]{2,1,0:T(8,128)(2,1)S(1)}, bf16[2,128,1024]{2,1,0:T(8,128)(2,1)}, u32[]{:S(2)}) copy-start(bf16[2,128,1024]{2,1,0:T(8,128)(2,1)} %param.18) | copy-start | bytes 1572868
  7.2 60.4 %all-gather.15.cloned.1.call-start = ((), (), s32[]{:S(2)}) async-start(), calls=%async_computation.12 | async-start | bytes 1081344 | tf_op jit(solution)/shard_map/all_gather | solution.py:94
  7.9 115.5 %all-gather.11.cloned.1.call-start = ((), (), s32[]{:S(2)}) async-start(), calls=%async_computation.10 | async-start | bytes 1081344 | tf_op jit(solution)/shard_map/all_gather | solution.py:95
  8.7 185.9 %all-gather.19.cloned.1.call-start = ((), (), s32[]{:S(2)}) async-start(), calls=%async_computation.14 | async-start | bytes 2162688 | tf_op jit(solution)/shard_map/all_gather | solution.py:93
  9.4 204.4 %all-gather.17.cloned.1.call-start = ((), (), s32[]{:S(2)}) async-start(), calls=%async_computation.13 | async-start | bytes 2359296 | tf_op jit(solution)/shard_map/all_gather | solution.py:135
  55.2 69.9 %copy-start.50 = (f32[1024]{0:T(1024)}, f32[1024]{0:T(1024)S(1)}, u32[]{:S(2)}) copy-start(f32[1024]{0:T(1024)S(1)} %convert_element_type.158) | copy-start | bytes 12292
  55.5 142.8 %copy-start.32 = (f32[256,64]{0,1:T(8,128)}, f32[256,64]{0,1:T(8,128)S(1)}, u32[]{:S(2)}) copy-start(f32[256,64]{0,1:T(8,128)S(1)} %get-tuple-element.312) | copy-start | bytes 196612
  55.5 142.8 %copy-start.37 = (f32[256,64]{0,1:T(8,128)}, f32[256,64]{0,1:T(8,128)S(1)}, u32[]{:S(2)}) copy-start(f32[256,64]{0,1:T(8,128)S(1)} %get-tuple-element.313) | copy-start | bytes 196612
  56.8 68.3 %copy-start.62 = (f32[2,128]{1,0:T(2,128)}, f32[2,128]{1,0:T(2,128)S(1)}, u32[]{:S(2)}) copy-start(f32[2,128]{1,0:T(2,128)S(1)} %fusion.60) | copy-start | bytes 3076
  56.8 68.3 %copy-start.57 = (f32[256]{0:T(256)}, f32[256]{0:T(256)S(1)}, u32[]{:S(2)}) copy-start(f32[256]{0:T(256)S(1)} %get-tuple-element.319) | copy-start | bytes 3076
  58.0 139.4 %copy-start.13 = (bf16[2,128,1024]{2,1,0:T(8,128)(2,1)}, bf16[2,128,1024]{2,1,0:T(8,128)(2,1)S(1)}, u32[]{:S(2)}) copy-start(bf16[2,128,1024]{2,1,0:T(8,128)(2,1)S(1)} %fusion.62) | copy-start | bytes 1572868
  69.1 59.7 %copy-start.48 = (s32[1,2,128,8]{2,3,1,0:T(8,128)S(1)}, s32[1,2,128,8]{2,3,1,0:T(8,128)}, u32[]{:S(2)}) copy-start(s32[1,2,128,8]{2,3,1,0:T(8,128)} %param.20) | copy-start | bytes 24580
  69.1 60.1 %copy-start.65 = (bf16[32,16]{0,1:T(8,128)(2,1)S(1)}, bf16[32,16]{0,1:T(8,128)(2,1)}, u32[]{:S(2)}) copy-start(bf16[32,16]{0,1:T(8,128)(2,1)} %param.27) | copy-start | bytes 3076
  69.6 123.1 %copy-start.42 = (s32[2,1024]{1,0:T(2,128)S(1)}, s32[2,1024]{1,0:T(2,128)}, u32[]{:S(2)}) copy-start(s32[2,1024]{1,0:T(2,128)} %param.19) | copy-start | bytes 24580
  69.6 123.8 %copy-start.34 = (bf16[2,128,1024]{2,1,0:T(8,128)(2,1)S(1)}, bf16[2,128,1024]{2,1,0:T(8,128)(2,1)}, u32[]{:S(2)}) copy-start(bf16[2,128,1024]{2,1,0:T(8,128)(2,1)} %param.31) | copy-start | bytes 1572868
  70.6 175.1 %all-gather.13.cloned.1.call-start = ((), (), s32[]{:S(2)}) async-start(), calls=%async_computation.11 | async-start | bytes 2359296 | tf_op jit(solution)/shard_map/all_gather | solution.py:136
  126.0 178.2 %all-gather.21.cloned.1.call-start = ((), (), s32[]{:S(2)}) async-start(), calls=%async_computation.15 | async-start | bytes 2162688 | tf_op jit(solution)/shard_map/all_gather | solution.py:96
  126.6 294.6 %all-gather.25.cloned.1.call-start = ((), (), s32[]{:S(2)}) async-start(), calls=%async_computation.17 | async-start | bytes 17301504 | tf_op jit(solution)/shard_map/all_gather | solution.py:102
  127.3 410.4 %all-gather.23.cloned.1.call-start = ((), (), s32[]{:S(2)}) async-start(), calls=%async_computation.16 | async-start | bytes 17301504 | tf_op jit(solution)/shard_map/all_gather | solution.py:101
  128.1 526.2 %all-gather.27.cloned.1.call-start = ((), (), s32[]{:S(2)}) async-start(), calls=%async_computation.18 | async-start | bytes 17301504 | tf_op jit(solution)/shard_map/all_gather | solution.py:103
  128.8 749.9 %reduce-scatter.13.cloned.1.call-start = ((), (), s32[]{:S(2)}) async-start(), calls=%async_computation.19 | async-start | bytes 4718592 | tf_op jit(solution)/shard_map/reduce_scatter | solution.py:317
  129.3 178.0 %copy-start.55 = (f32[1024]{0:T(1024)}, f32[1024]{0:T(1024)S(1)}, u32[]{:S(2)}) copy-start(f32[1024]{0:T(1024)S(1)} %convert_element_type.167) | copy-start | bytes 12292
  169.6 138.1 %copy-start.46 = (bf16[1024,16]{0,1:T(8,128)(2,1)}, bf16[1024,16]{0,1:T(8,128)(2,1)S(1)}, u32[]{:S(2)}) copy-start(bf16[1024,16]{0,1:T(8,128)(2,1)S(1)} %reshape.604) | copy-start | bytes 98308
  192.8 461.5 %copy-start.44 = (pred[16,192]{1,0:T(8,128)(4,1)}, pred[16,192]{1,0:T(8,128)(4,1)S(1)}, u32[]{:S(2)}) copy-start(pred[16,192]{1,0:T(8,128)(4,1)S(1)} %broadcast_in_dim.80) | copy-start | bytes 9220
  198.2 47.6 %copy-start.39 = (bf16[2,128,1024]{2,1,0:T(8,128)(2,1)S(1)}, bf16[2,128,1024]{2,1,0:T(8,128)(2,1)}, u32[]{:S(2)}) copy-start(bf16[2,128,1024]{2,1,0:T(8,128)(2,1)} %custom-call.8) | copy-start | bytes 1572868
  261.2 46.1 %copy-start.6 = (bf16[2,128,8,2,64]{1,4,3,2,0:T(8,128)(2,1)}, bf16[2,128,8,2,64]{1,4,3,2,0:T(8,128)(2,1)S(1)}, u32[]{:S(2)}) copy-start(bf16[2,128,8,2,64]{1,4,3,2,0:T(8,128)(2,1)S(1)} %get-tuple-element.569) | copy-start | bytes 1572868
  261.2 61.2 %copy-start.40 = (bf16[2,128,1024]{2,1,0:T(8,128)(2,1)}, bf16[2,128,1024]{2,1,0:T(8,128)(2,1)S(1)}, u32[]{:S(2)}) copy-start(bf16[2,128,1024]{2,1,0:T(8,128)(2,1)S(1)} %get-tuple-element.125) | copy-start | bytes 1572868
  261.2 61.2 %copy-start.52 = (f32[2,8,2,128,1]{3,2,1,4,0:T(2,128)}, f32[2,8,2,128,1]{3,2,1,4,0:T(2,128)S(1)}, u32[]{:S(2)}) copy-start(f32[2,8,2,128,1]{3,2,1,4,0:T(2,128)S(1)} %get-tuple-element.507) | copy-start | bytes 49156
  261.2 61.2 %copy-start.66 = (s32[2,128]{1,0:T(2,128)}, s32[2,128]{1,0:T(2,128)S(1)}, u32[]{:S(2)}) copy-start(s32[2,128]{1,0:T(2,128)S(1)} %get-tuple-element.610) | copy-start | bytes 3076
  307.3 15.1 copy-start.60
  307.8 14.6 copy-start
  308.4 14.0 copy-start.20
  671.8 12.8 copy-start.8
  671.8 12.8 copy-start.54
  684.6 16.4 copy-start.21
  707.9 12.9 copy-start.10
  752.7 5.8 copy-start.61
  752.7 7.0 copy-start.31
  752.7 7.0 copy-start.35
  752.8 7.0 copy-start.64
  764.5 6.1 copy-start.24
  781.1 9.8 copy-start.5
  797.4 6.1 copy-start.24
  813.9 9.8 copy-start.5
  830.2 6.3 copy-start.38
  830.2 99.0 %reduce-scatter.15.cloned.1.call-start = ((), (), s32[]{:S(2)}) async-start(), calls=%async_computation.20 | async-start | bytes 4718592 | tf_op jit(solution)/shard_map/reduce_scatter | solution.py:318
  830.3 6.4 copy-start.33
  830.9 232.5 %reduce-scatter.31.cloned.1.call-start = ((), (), s32[]{:S(2)}) async-start(), calls=%async_computation.28 | async-start | bytes 540672
  837.9 367.3 %reduce-scatter.17.cloned.1.call-start = ((), (), s32[]{:S(2)}) async-start(), calls=%async_computation.21 | async-start | bytes 4325376 | tf_op jit(solution)/shard_map/reduce_scatter | solution.py:350
  840.7 507.6 %reduce-scatter.23.cloned.1.call-start = ((), (), s32[]{:S(2)}) async-start(), calls=%async_computation.24 | async-start | bytes 4325376 | tf_op jit(solution)/shard_map/reduce_scatter | solution.py:353
  843.6 641.5 %reduce-scatter.19.cloned.1.call-start = ((), (), s32[]{:S(2)}) async-start(), calls=%async_computation.22 | async-start | bytes 2162688 | tf_op jit(solution)/shard_map/reduce_scatter | solution.py:351
  881.2 52.0 %copy-start.9 = (bf16[16,192,512]{2,1,0:T(8,128)(2,1)S(1)}, bf16[16,192,512]{2,1,0:T(8,128)(2,1)}, u32[]{:S(2)}) copy-start(bf16[16,192,512]{2,1,0:T(8,128)(2,1)} %copy-done.8) | copy-start | bytes 9437188
  881.2 52.0 %copy-start.45 = (pred[16,192]{1,0:T(8,128)(4,1)S(1)}, pred[16,192]{1,0:T(8,128)(4,1)}, u32[]{:S(2)}) copy-start(pred[16,192]{1,0:T(8,128)(4,1)} %copy-done.44) | copy-start | bytes 9220
  886.1 734.7 %reduce-scatter.21.cloned.1.call-start = ((), (), s32[]{:S(2)}) async-start(), calls=%async_computation.23 | async-start | bytes 2162688 | tf_op jit(solution)/shard_map/reduce_scatter | solution.py:352
  933.1 1048.1 %reduce-scatter.29.cloned.1.call-start = ((), (), s32[]{:S(2)}) async-start(), calls=%async_computation.27 | async-start | bytes 34603008 | tf_op jit(solution)/shard_map/reduce_scatter | solution.py:360
  948.4 1393.3 %reduce-scatter.25.cloned.1.call-start = ((), (), s32[]{:S(2)}) async-start(), calls=%async_computation.25 | async-start | bytes 34603008 | tf_op jit(solution)/shard_map/reduce_scatter | solution.py:358
  965.4 1736.9 %reduce-scatter.27.cloned.1.call-start = ((), (), s32[]{:S(2)}) async-start(), calls=%async_computation.26 | async-start | bytes 34603008 | tf_op jit(solution)/shard_map/reduce_scatter | solution.py:359
  982.6 42.5 %copy-start.63 = (f32[2,128]{1,0:T(2,128)S(1)}, f32[2,128]{1,0:T(2,128)}, u32[]{:S(2)}) copy-start(f32[2,128]{1,0:T(2,128)} %copy-done.62) | copy-start | bytes 3076
  983.3 44.4 %copy-start.27 = (f32[256,16,64]{0,2,1:T(8,128)S(1)}, f32[256,16,64]{0,2,1:T(8,128)}, u32[]{:S(2)}) copy-start(f32[256,16,64]{0,2,1:T(8,128)} %get-tuple-element.299) | copy-start | bytes 3145732
  1029.0 40.1 %copy-start.19 = (bf16[2,128,1024]{2,1,0:T(8,128)(2,1)S(1)}, bf16[2,128,1024]{2,1,0:T(8,128)(2,1)}, u32[]{:S(2)}) copy-start(bf16[2,128,1024]{2,1,0:T(8,128)(2,1)} %param.18) | copy-start | bytes 1572868
  1029.0 40.1 %copy-start.51 = (f32[1024]{0:T(1024)S(1)}, f32[1024]{0:T(1024)}, u32[]{:S(2)}) copy-start(f32[1024]{0:T(1024)} %copy-done.50) | copy-start | bytes 12292
  1029.0 40.1 %copy-start.58 = (f32[256]{0:T(256)S(1)}, f32[256]{0:T(256)}, u32[]{:S(2)}) copy-start(f32[256]{0:T(256)} %copy-done.57) | copy-start | bytes 3076
  1030.8 40.2 %copy-start.59 = (f32[1024]{0:T(1024)S(1)}, f32[1024]{0:T(1024)}, u32[]{:S(2)}) copy-start(f32[1024]{0:T(1024)} %get-tuple-element.237) | copy-start | bytes 12292
  1030.8 79.2 %copy-start.17 = (f32[256,1024]{1,0:T(8,128)S(1)}, f32[256,1024]{1,0:T(8,128)}, u32[]{:S(2)}) copy-start(f32[256,1024]{1,0:T(8,128)} %copy-done.15) | copy-start | bytes 3145732
  (32 other events, 100.7 us)
Sparse Core Ops, SparseCore 0:
  11.0 56.5 all-gather.14
  70.6 52.7 all-gather.10
  126.4 55.6 all-gather.18
  184.1 29.6 all-gather.16
  215.8 29.8 all-gather.12
  248.6 55.5 all-gather.20
  307.2 113.8 all-gather.24
  424.3 113.4 all-gather.22
  540.8 113.4 all-gather.26
  830.3 48.3 reduce-scatter.12
  881.0 48.1 reduce-scatter.14
  931.3 132.0 reduce-scatter.30
  1066.4 138.8 reduce-scatter.16
  1208.0 140.2 reduce-scatter.22
  1351.1 133.9 reduce-scatter.18
  1487.7 133.0 reduce-scatter.20
  1623.7 357.4 reduce-scatter.28
  1984.0 357.6 reduce-scatter.24
  2344.7 357.6 reduce-scatter.26
where the time goes:
time: 2720 us; the launch traced here: 2710 us
  waiting for transfers between devices  2140 us (79%)
  matrix products  193 us (7%)
  blocking collectives  158 us (6%)
  local copies, waits for them, and re-layouts  154 us (6%)
  other arithmetic  47.3 us (2%)
    reduce_scatter x1, waiting for transfers between devices, body(): lax.psum_scatter(delta_up, ('row', 'seq'), scatter_dimension=1, tiled=True)  361 us
    reduce_scatter x1, waiting for transfers between devices, body(): lax.psum_scatter(delta_gate, ('row', 'seq'), scatter_dimension=1, tiled=T...  360 us
    reduce_scatter x1, waiting for transfers between devices, body(): lax.psum_scatter(delta_down, ('row', 'seq'), scatter_dimension=2, tiled=T...  360 us
    reduce_scatter x1, waiting for transfers between devices, body(): lax.psum_scatter(delta_out_weight, ('row', 'seq'), scatter_dimension=1, t...  143 us
    reduce_scatter x1, waiting for transfers between devices, body(): lax.psum_scatter(delta_key_weight, ('row', 'seq'), scatter_dimension=0, t...  137 us
    reduce_scatter x1, waiting for transfers between devices, body(): lax.psum_scatter(delta_value_weight, ('row', 'seq'), scatter_dimension=0,...  136 us
    all_gather x1, waiting for transfers between devices, body(): lax.all_gather(w_gate, ('row', 'seq'), axis=1, tiled=True)  103 us
    all_gather x1, waiting for transfers between devices, body(): lax.all_gather(w_down, ('row', 'seq'), axis=2, tiled=True)  103 us
  transfers between devices with their start and end apart: 19, of which 18 were waited for; matrix products, arithmetic and copies ran while one was open for 8% of the time, Pallas kernels for 0%

commit v1 on v0

--- a/solution.py
+++ b/solution.py
@@ -1,6 +1,10 @@
+import functools
+
 import jax
 import jax.numpy as jnp
 from jax import lax
+from jax.experimental import pallas as pl
+from jax.experimental.pallas import tpu as pltpu
 from jax.sharding import PartitionSpec as P
 
 HEADS = 16
@@ -9,14 +13,16 @@
 GROUP = 2
 EXPERTS = 16
 TOPK = 8
-CAP = 192
-
 
 EPSILON = 1e-06
 SCORE_SCALE = 0.015625
 RESIDUAL = 0.22
 THETA = 10000.0
 NEGATIVE = -1e30
+
+MESH = pl.DeviceIdType.MESH
+ANY = pl.BlockSpec(memory_space=pl.ANY)
+VMEM = pl.BlockSpec(memory_space=pltpu.VMEM)
 
 
 def norm_scale(value):
@@ -68,7 +74,409 @@
     return jnp.where(visible, SCORE_SCALE * raw, NEGATIVE)
 
 
+def greet_all(n_row, n_seq):
+    row, seq = lax.axis_index("row"), lax.axis_index("seq")
+    me, total = row * n_seq + seq, n_row * n_seq
+    barrier = pltpu.get_barrier_semaphore()
+
+    def greet(step, carry):
+        other = (me + step) % total
+        pl.semaphore_signal(
+            barrier, inc=1, device_id=(other // n_seq, other % n_seq), device_id_type=MESH
+        )
+        return carry
+
+    lax.fori_loop(1, total, greet, 0)
+    pl.semaphore_wait(barrier, total - 1)
+
+
+def weights_kernel(n_row, n_seq, gate, up, down, held, send, recv, local, pass_send, pass_recv):
+    row, seq = lax.axis_index("row"), lax.axis_index("seq")
+    me, total = row * n_seq + seq, n_row * n_seq
+    core = seq % 2
+    rows = gate.shape[1]
+    greet_all(n_row, n_seq)
+
+    def transfer(kind, source, step):
+        other = (me + step) % total
+        other_row, other_seq = other // n_seq, other % n_seq
+        return pltpu.make_async_remote_copy(
+            src_ref=source.at[other_row * 4 + other_seq % 4],
+            dst_ref=held.at[other_seq % 2, kind, pl.ds(pl.multiple_of(me * rows, rows), rows)],
+            send_sem=send.at[kind, step],
+            recv_sem=recv.at[kind, step],
+            device_id=(other_row, other_seq),
+            device_id_type=MESH,
+        )
+
+    def arrival(kind, source, step):
+        other = (me + total - step) % total
+        return pltpu.make_async_remote_copy(
+            src_ref=source.at[0],
+            dst_ref=held.at[core, kind, pl.ds(pl.multiple_of(other * rows, rows), rows)],
+            send_sem=send.at[kind, step],
+            recv_sem=recv.at[kind, step],
+            device_id=(row, (seq + 1) % 2 + seq // 2 * 2),
+            device_id_type=MESH,
+        )
+
+    sources = (gate, up, down)
+    own = [
+        pltpu.make_async_copy(
+            source.at[row * 4 + seq % 4],
+            held.at[core, kind, pl.ds(pl.multiple_of(me * rows, rows), rows)],
+            local.at[kind],
+        )
+        for kind, source in enumerate(sources)
+    ]
+    for copy in own:
+        copy.start()
+
+    def start(step, carry):
+        for kind, source in enumerate(sources):
+            transfer(kind, source, step).start()
+        return carry
+
+    lax.fori_loop(1, total, start, 0)
+
+    def settle(step, carry):
+        for kind, source in enumerate(sources):
+            arrival(kind, source, step).wait_recv()
+        return carry
+
+    lax.fori_loop(1, total, settle, 0)
+    for copy in own:
+        copy.wait()
+    share = pltpu.make_async_remote_copy(
+        src_ref=held.at[core],
+        dst_ref=held.at[core],
+        send_sem=pass_send,
+        recv_sem=pass_recv,
+        device_id=(row, seq // 2 * 2 + (1 - core)),
+        device_id_type=MESH,
+    )
+    share.start()
+
+    def drain(step, carry):
+        for kind, source in enumerate(sources):
+            transfer(kind, source, step).wait_send()
+        return carry
+
+    lax.fori_loop(1, total, drain, 0)
+    share.wait_send()
+    pltpu.make_async_remote_copy(
+        src_ref=held.at[core],
+        dst_ref=held.at[1 - core],
+        send_sem=pass_send,
+        recv_sem=pass_recv,
+        device_id=(row, seq // 2 * 2 + (1 - core)),
+        device_id_type=MESH,
+    ).wait_recv()
+
+
+def gather_weights(n_row, n_seq, gate, up, down):
+    experts, rows, hidden = gate.shape
+    total = n_row * n_seq
+    return pl.pallas_call(
+        functools.partial(weights_kernel, n_row, n_seq),
+        out_shape=jax.ShapeDtypeStruct((2, 3, rows * total, hidden), jnp.bfloat16),
+        in_specs=[ANY] * 3,
+        out_specs=ANY,
+        scratch_shapes=[
+            pltpu.SemaphoreType.DMA((3, total)),
+            pltpu.SemaphoreType.DMA((3, total)),
+            pltpu.SemaphoreType.DMA((3,)),
+            pltpu.SemaphoreType.DMA,
+            pltpu.SemaphoreType.DMA,
+        ],
+        compiler_params=pltpu.CompilerParams(collective_id=1, has_side_effects=True),
+        name="weights",
+    )(gate, up, down)
+
+
+def grads_kernel(n_row, n_seq, grads, held, send, recv, local):
+    row, seq = lax.axis_index("row"), lax.axis_index("seq")
+    me, total = row * n_seq + seq, n_row * n_seq
+    rows = held.shape[3]
+    greet_all(n_row, n_seq)
+
+    def transfer(kind, step):
+        other = (me + step) % total
+        return pltpu.make_async_remote_copy(
+            src_ref=grads.at[kind, pl.ds(pl.multiple_of(other * rows, rows), rows)],
+            dst_ref=held.at[kind, seq // 4, row * 4 + seq % 4],
+            send_sem=send.at[kind, step],
+            recv_sem=recv.at[kind, step],
+            device_id=(other // n_seq, other % n_seq),
+            device_id_type=MESH,
+        )
+
+    def arrival(kind, step):
+        other = (me + total - step) % total
+        return pltpu.make_async_remote_copy(
+            src_ref=grads.at[kind, pl.ds(0, rows)],
+            dst_ref=held.at[kind, other % n_seq // 4, other // n_seq * 4 + other % 4],
+            send_sem=send.at[kind, step],
+            recv_sem=recv.at[kind, step],
+            device_id=(other // n_seq, other % n_seq),
+            device_id_type=MESH,
+        )
+
+    own = [
+        pltpu.make_async_copy(
+            grads.at[kind, pl.ds(pl.multiple_of(me * rows, rows), rows)],
+            held.at[kind, seq // 4, row * 4 + seq % 4],
+            local.at[kind],
+        )
+        for kind in range(3)
+    ]
+    for copy in own:
+        copy.start()
+
+    def start(step, carry):
+        for kind in range(3):
+            transfer(kind, step).start()
+        return carry
+
+    lax.fori_loop(1, total, start, 0)
+    for copy in own:
+        copy.wait()
+
+    def settle(step, carry):
+        for kind in range(3):
+            transfer(kind, step).wait_send()
+            arrival(kind, step).wait_recv()
+        return carry
+
+    lax.fori_loop(1, total, settle, 0)
+
+
+def scatter_grads(n_row, n_seq, grads):
+    _, width, hidden = grads.shape
+    total = n_row * n_seq
+    held = pl.pallas_call(
+        functools.partial(grads_kernel, n_row, n_seq),
+        out_shape=jax.ShapeDtypeStruct(
+            (3, n_seq // 4, n_row * 4, width // total, hidden), jnp.bfloat16
+        ),
+        in_specs=[ANY],
+        out_specs=ANY,
+        scratch_shapes=[
+            pltpu.SemaphoreType.DMA((3, total)),
+            pltpu.SemaphoreType.DMA((3, total)),
+            pltpu.SemaphoreType.DMA((3,)),
+        ],
+        compiler_params=pltpu.CompilerParams(collective_id=2, has_side_effects=True),
+        name="grads",
+    )(grads)
+    return jnp.sum(held.astype(jnp.float32), axis=1)
+
+
+NN = (((1,), (0,)), ((), ()))
+NT = (((1,), (1,)), ((), ()))
+TN = (((0,), (0,)), ((), ()))
+
+
+def mul(a, b, dims):
+    return lax.dot_general(a, b, dims, preferred_element_type=jnp.float32)
+
+
+def column(row_values):
+    return jnp.broadcast_to(row_values, (128, row_values.shape[1])).T
+
+
+def experts_kernel(
+    n_seq, x_in, g_in, gates_in, w_in, y_out, dx_out, dg_out, grad_out,
+    xs, gs, gates, w, acc, y_acc, dx_acc, dg_made, y_got, dx_got, dg_got, total_low,
+    in_send, in_recv, out_send, out_recv, w_sem, half_send, half_recv, ready, done_sem,
+):
+    row, seq = lax.axis_index("row"), lax.axis_index("seq")
+    core, chip_z, base = seq % 2, seq // 2 % 2, seq // 4 * 4
+    width = x_in.shape[1]
+    chunk = 256
+    mine = (row * 2 + chip_z) * 2
+
+    def peer(step):
+        other_row = (row // 2 + step // 4) % 2 * 2 + (row % 2 + step // 2 % 2) % 2
+        other_seq = base + (chip_z + step % 2) % 2 * 2 + core
+        return (other_row, other_seq)
+
+    sibling = (row, seq // 2 * 2 + (1 - core))
+    fetch = [pltpu.make_async_copy(w_in.at[j], w.at[j], w_sem.at[j]) for j in range(2)]
+    for copy in fetch:
+        copy.start()
+    barrier = pltpu.get_barrier_semaphore()
+
+    def greet(step, carry):
+        pl.semaphore_signal(barrier, inc=1, device_id=peer(step), device_id_type=MESH)
+        return carry
+
+    lax.fori_loop(1, 8, greet, 0)
+    pl.semaphore_signal(barrier, inc=1, device_id=sibling, device_id_type=MESH)
+    pl.semaphore_wait(barrier, 8)
+
+    def inward(step):
+        return [
+            pltpu.make_async_remote_copy(
+                src_ref=source, dst_ref=target.at[step], send_sem=in_send.at[i, step],
+                recv_sem=in_recv.at[i, step], device_id=peer(step), device_id_type=MESH,
+            )
+            for i, (source, target) in enumerate(((x_in, xs), (g_in, gs), (gates_in, gates)))
+        ]
+
+    def outward(step):
+        return [
+            pltpu.make_async_remote_copy(
+                src_ref=source.at[step], dst_ref=target.at[step], send_sem=out_send.at[i, step],
+                recv_sem=out_recv.at[i, step], device_id=peer(step), device_id_type=MESH,
+            )
+            for i, (source, target) in enumerate(((xs, y_got), (gs, dx_got), (dg_made, dg_got)))
+        ]
+
+    def send_in(step, carry):
+        for copy in inward(step):
+            copy.start()
+        return carry
+
+    lax.fori_loop(1, 8, send_in, 0)
+    xs[0] = x_in[...]
+    gs[0] = g_in[...]
+    gates[0] = gates_in[...]
+    acc[...] = jnp.zeros_like(acc)
+    for copy in fetch:
+        copy.wait()
+
+    def block(step, carry):
+        @pl.when(step > 0)
+        def _():
+            for copy in inward(step):
+                copy.wait_recv()
+
+        y_acc[...] = jnp.zeros_like(y_acc)
+        dx_acc[...] = jnp.zeros_like(dx_acc)
+
+        def expert(j, inner_carry):
+            gate = column(gates[step, pl.ds(mine + j, 1)])[:, :1]
+            x = xs[step]
+            a = mul(x, w[j, 0], NN)
+            b = mul(x, w[j, 1], NN)
+            sigma = jax.nn.sigmoid(a)
+            smooth = a * sigma
+            inner = (smooth * b).astype(jnp.bfloat16)
+            dgate = jnp.zeros((x.shape[0], 1), jnp.float32)
+            d_inner = jnp.zeros(a.shape, jnp.float32)
+            for lo in range(0, width, chunk):
+                part = slice(lo, lo + chunk)
+                delta = RESIDUAL * gs[step, :, part].astype(jnp.float32)
+                y = mul(inner, w[j, 2, part], NT)
+                y_acc[:, part] += gate * y
+                dgate += jnp.sum(delta * y, axis=1, keepdims=True)
+                dy = (gate * delta).astype(jnp.bfloat16)
+                d_inner += mul(dy, w[j, 2, part], NN)
+                acc[j, 2, part] += mul(dy, inner, TN)
+            da = (d_inner * b * sigma * (1.0 + a * (1.0 - sigma))).astype(jnp.bfloat16)
+            db = (d_inner * smooth).astype(jnp.bfloat16)
+            for lo in range(0, width, chunk):
+                part = slice(lo, lo + chunk)
+                x_part = xs[step, :, part]
+                acc[j, 0, part] += mul(x_part, da, TN)
+                acc[j, 1, part] += mul(x_part, db, TN)
+                dx_acc[:, part] += mul(da, w[j, 0, part], NT) + mul(db, w[j, 1, part], NT)
+            dg_made[step, j] = jnp.broadcast_to(dgate, (dgate.shape[0], 128)).T[:8]
+            return inner_carry
+
+        lax.fori_loop(0, 2, expert, 0)
+        xs[step] = y_acc[...].astype(jnp.bfloat16)
+        gs[step] = dx_acc[...].astype(jnp.bfloat16)
+
+        @pl.when(step > 0)
+        def _():
+            for copy in outward(step):
+                copy.start()
+
+        return carry
+
+    lax.fori_loop(0, 8, block, 0)
+
+    pl.semaphore_signal(ready, inc=1, device_id=sibling, device_id_type=MESH)
+    w[1 - core] = acc[1 - core].astype(jnp.bfloat16)
+    pl.semaphore_wait(ready, 1)
+    half = pltpu.make_async_remote_copy(
+        src_ref=w.at[1 - core], dst_ref=total_low, send_sem=half_send, recv_sem=half_recv,
+        device_id=sibling, device_id_type=MESH,
+    )
+    half.start()
+    y_got[0] = xs[0]
+    dx_got[0] = gs[0]
+    dg_got[0] = dg_made[0]
+    half.wait_recv()
+    total_low[...] = (acc[core] + total_low[...].astype(jnp.float32)).astype(jnp.bfloat16)
+    store = pltpu.make_async_copy(total_low, grad_out, done_sem)
+    store.start()
+
+    def settle(step, carry):
+        for copy in inward(step):
+            copy.wait_send()
+        for copy in outward(step):
+            copy.wait()
+        return carry
+
+    lax.fori_loop(1, 8, settle, 0)
+    y_out[...] = sum(y_got[i].astype(jnp.float32) for i in range(8))
+    dx_out[...] = sum(dx_got[i].astype(jnp.float32) for i in range(8))
+    dg_out[...] = dg_got[...]
+    half.wait_send()
+    store.wait()
+
+
+def run_experts(n_row, n_seq, x, g, gates, w):
+    tokens, width = x.shape
+    hidden = w.shape[3]
+    low, full = jnp.bfloat16, jnp.float32
+    dma = pltpu.SemaphoreType.DMA
+    return pl.pallas_call(
+        functools.partial(experts_kernel, n_seq),
+        out_shape=(
+            jax.ShapeDtypeStruct((tokens, width), full),
+            jax.ShapeDtypeStruct((tokens, width), full),
+            jax.ShapeDtypeStruct((8, 2, 8, tokens), full),
+            jax.ShapeDtypeStruct((3, width, hidden), low),
+        ),
+        in_specs=[VMEM, VMEM, VMEM, ANY],
+        out_specs=(VMEM, VMEM, VMEM, ANY),
+        scratch_shapes=[
+            pltpu.VMEM((8, tokens, width), low),
+            pltpu.VMEM((8, tokens, width), low),
+            pltpu.VMEM((8, EXPERTS, tokens), full),
+            pltpu.VMEM((2, 3, width, hidden), low),
+            pltpu.VMEM((2, 3, width, hidden), full),
+            pltpu.VMEM((tokens, width), full),
+            pltpu.VMEM((tokens, width), full),
+            pltpu.VMEM((8, 2, 8, tokens), full),
+            pltpu.VMEM((8, tokens, width), low),
+            pltpu.VMEM((8, tokens, width), low),
+            pltpu.VMEM((8, 2, 8, tokens), full),
+            pltpu.VMEM((3, width, hidden), low),
+            dma((3, 8)),
+            dma((3, 8)),
+            dma((3, 8)),
+            dma((3, 8)),
+            dma((2,)),
+            dma,
+            dma,
+            pltpu.SemaphoreType.REGULAR,
+            dma,
+        ],
+        compiler_params=pltpu.CompilerParams(
+            collective_id=3, has_side_effects=True, vmem_limit_bytes=60 << 20
+        ),
+        name="experts",
+    )(x, g, gates, w)
+
+
 def body(
+    n_row,
+    n_seq,
     tokens,
     segment_ids,
     expert_ids,
@@ -97,11 +505,7 @@
         lax.all_gather(norm2_gain, ("row", "seq"), axis=0, tiled=True),
         lax.all_gather(w_router, ("row", "seq"), axis=0, tiled=True),
     )
-    gate_all, up_all, down_all = (
-        lax.all_gather(w_gate, ("row", "seq"), axis=1, tiled=True),
-        lax.all_gather(w_up, ("row", "seq"), axis=1, tiled=True),
-        lax.all_gather(w_down, ("row", "seq"), axis=2, tiled=True),
-    )
+    expert_weights = gather_weights(n_row, n_seq, w_gate, w_up, jnp.swapaxes(w_down, 1, 2))
     flat = tokens.reshape(token_count, width).astype(jnp.float32)
     scale_one = norm_scale(flat)
     normed = (flat * scale_one * gain_one.astype(jnp.float32)).astype(jnp.bfloat16)
@@ -165,89 +569,36 @@
     normed_two = (hidden * scale_two * gain_two.astype(jnp.float32)).astype(jnp.bfloat16)
     logits = jnp.dot(normed_two, router_weight, preferred_element_type=jnp.float32)
     routes = expert_ids.reshape(token_count, TOPK)
-    chosen = routes[:, :, None] == jnp.arange(EXPERTS, dtype=jnp.int32)[None, None, :]
-    chosen_float = chosen.astype(jnp.float32)
-    gates = jax.nn.softmax(jnp.sum(chosen_float * logits[:, None, :], axis=-1), axis=-1)
-    expert_counts = lax.psum(jnp.sum(chosen.astype(jnp.int32), axis=(0, 1)), ("row", "seq"))
-    assignments = token_count * TOPK
-    onehot = chosen.reshape(assignments, EXPERTS).astype(jnp.int32)
-    before = jnp.cumsum(onehot, axis=0) - onehot
-    target = routes.reshape(-1) * CAP + jnp.sum(before * onehot, axis=1)
-    source = (
-        jnp.zeros((EXPERTS * CAP,), jnp.int32)
-        .at[target]
-        .set(jnp.arange(assignments, dtype=jnp.int32))
-    )
-    filled = jnp.zeros((EXPERTS * CAP,), jnp.bool_).at[target].set(True)
-    owner = source // TOPK
-    empty_row = jnp.zeros((), jnp.bfloat16)
-    expert_rows = jnp.where(filled[:, None], normed_two[owner], empty_row).reshape(
-        EXPERTS, CAP, width
-    )
-    gate_part = jnp.einsum(
-        "ecd,edf->ecf", expert_rows, gate_all, preferred_element_type=jnp.float32
-    )
-    up_part = jnp.einsum("ecd,edf->ecf", expert_rows, up_all, preferred_element_type=jnp.float32)
-    inner = (jax.nn.silu(gate_part) * up_part).astype(jnp.bfloat16)
-    result = jnp.einsum("ecf,efd->ecd", inner, down_all, preferred_element_type=jnp.float32)
-    returned = result.reshape(EXPERTS * CAP, width)[target].reshape(token_count, TOPK, width)
-    mixture = jnp.sum(gates[:, :, None] * returned, axis=1)
+    picks = jnp.sum(
+        (routes[:, :, None] == jnp.arange(EXPERTS, dtype=jnp.int32)[None, None, :]).astype(
+            jnp.int32
+        ),
+        axis=1,
+    )
+    expert_counts = lax.psum(jnp.sum(picks, axis=0), ("row", "seq"))
+    gates = jax.nn.softmax(jnp.where(picks > 0, logits, NEGATIVE), axis=-1)
+    gates = jnp.where(picks > 0, gates, 0.0)
+    flat_grad = out_grad.reshape(token_count, width)
+    mixture, from_experts, gate_grads, expert_grads = run_experts(
+        n_row, n_seq, normed_two, flat_grad, gates.T, expert_weights
+    )
     layer_out = (
         (hidden + RESIDUAL * mixture).astype(jnp.bfloat16).reshape(row_count, block_len, width)
     )
-    back_gain_one, back_query, back_key, back_value, back_out, back_gain_two, back_router = (
-        lax.all_gather(norm1_gain, ("row", "seq"), axis=0, tiled=True),
-        lax.all_gather(w_query, ("row", "seq"), axis=0, tiled=True),
-        lax.all_gather(w_key, ("row", "seq"), axis=0, tiled=True),
-        lax.all_gather(w_value, ("row", "seq"), axis=0, tiled=True),
-        lax.all_gather(w_out, ("row", "seq"), axis=1, tiled=True),
-        lax.all_gather(norm2_gain, ("row", "seq"), axis=0, tiled=True),
-        lax.all_gather(w_router, ("row", "seq"), axis=0, tiled=True),
-    )
-    back_gate, back_up, back_down = (
-        lax.all_gather(w_gate, ("row", "seq"), axis=1, tiled=True),
-        lax.all_gather(w_up, ("row", "seq"), axis=1, tiled=True),
-        lax.all_gather(w_down, ("row", "seq"), axis=2, tiled=True),
-    )
-    delta_out = out_grad.reshape(token_count, width).astype(jnp.float32)
-    delta_mixture = RESIDUAL * delta_out
-    delta_gates = jnp.sum(delta_mixture[:, None, :] * returned, axis=-1)
-    delta_returned = (
-        (gates[:, :, None] * delta_mixture[:, None, :])
-        .astype(jnp.bfloat16)
-        .reshape(assignments, width)
-    )
-    delta_result = jnp.where(filled[:, None], delta_returned[source], empty_row).reshape(
-        EXPERTS, CAP, width
-    )
-    delta_down = jnp.einsum("ecf,ecd->efd", inner, delta_result, preferred_element_type=jnp.float32)
-    delta_inner = jnp.einsum(
-        "ecd,efd->ecf", delta_result, back_down, preferred_element_type=jnp.float32
-    )
-    sigma = jax.nn.sigmoid(gate_part)
-    delta_gate_part = (delta_inner * up_part * sigma * (1.0 + gate_part * (1.0 - sigma))).astype(
-        jnp.bfloat16
-    )
-    delta_up_part = (delta_inner * gate_part * sigma).astype(jnp.bfloat16)
-    delta_gate = jnp.einsum(
-        "ecd,ecf->edf", expert_rows, delta_gate_part, preferred_element_type=jnp.float32
-    )
-    delta_up = jnp.einsum(
-        "ecd,ecf->edf", expert_rows, delta_up_part, preferred_element_type=jnp.float32
-    )
-    delta_rows = jnp.einsum(
-        "ecf,edf->ecd", delta_gate_part, back_gate, preferred_element_type=jnp.float32
-    ) + jnp.einsum("ecf,edf->ecd", delta_up_part, back_up, preferred_element_type=jnp.float32)
-    from_experts = jnp.sum(
-        delta_rows.reshape(EXPERTS * CAP, width)[target].reshape(token_count, TOPK, width), axis=1
-    )
+    grads = scatter_grads(n_row, n_seq, expert_grads)
+    row, chip_z = lax.axis_index("row"), lax.axis_index("seq") // 2 % 2
+    chip = jnp.arange(8)
+    slot = ((chip // 4 + row // 2) % 2) * 4 + ((chip // 2 % 2 + row % 2) % 2) * 2 + (chip + chip_z) % 2
+    delta_gates = gate_grads[:, :, 0][slot].reshape(EXPERTS, token_count).T
+
+    delta_out = flat_grad.astype(jnp.float32)
     delta_picked = gates * (delta_gates - jnp.sum(gates * delta_gates, axis=-1, keepdims=True))
-    delta_logits = jnp.sum(chosen_float * delta_picked[:, :, None], axis=1).astype(jnp.bfloat16)
+    delta_logits = delta_picked.astype(jnp.bfloat16)
     delta_router = jnp.dot(normed_two.T, delta_logits, preferred_element_type=jnp.float32)
     delta_normed_two = from_experts + jnp.dot(
-        delta_logits, back_router.T, preferred_element_type=jnp.float32
-    )
-    weighted_two = back_gain_two.astype(jnp.float32) * delta_normed_two
+        delta_logits, router_weight.T, preferred_element_type=jnp.float32
+    )
+    weighted_two = gain_two.astype(jnp.float32) * delta_normed_two
     delta_gain_two = jnp.sum(delta_normed_two * hidden * scale_two, axis=0)
     delta_hidden = (
         delta_out
@@ -259,7 +610,7 @@
     delta_branch = (RESIDUAL * delta_hidden).astype(jnp.bfloat16)
     delta_out_weight = jnp.dot(mixed.T, delta_branch, preferred_element_type=jnp.float32)
     delta_mixed = (
-        jnp.dot(delta_branch, back_out.T, preferred_element_type=jnp.float32)
+        jnp.dot(delta_branch, out_weight.T, preferred_element_type=jnp.float32)
         .astype(jnp.bfloat16)
         .reshape(row_count, block_len, KV_HEADS, GROUP, HEAD)
     )
@@ -332,11 +683,11 @@
     delta_key_weight = jnp.dot(normed.T, delta_keys, preferred_element_type=jnp.float32)
     delta_value_weight = jnp.dot(normed.T, delta_values, preferred_element_type=jnp.float32)
     delta_normed = (
-        jnp.dot(delta_query, back_query.T, preferred_element_type=jnp.float32)
-        + jnp.dot(delta_keys, back_key.T, preferred_element_type=jnp.float32)
-        + jnp.dot(delta_values, back_value.T, preferred_element_type=jnp.float32)
-    )
-    weighted_one = back_gain_one.astype(jnp.float32) * delta_normed
+        jnp.dot(delta_query, query_weight.T, preferred_element_type=jnp.float32)
+        + jnp.dot(delta_keys, key_weight.T, preferred_element_type=jnp.float32)
+        + jnp.dot(delta_values, value_weight.T, preferred_element_type=jnp.float32)
+    )
+    weighted_one = gain_one.astype(jnp.float32) * delta_normed
     delta_gain_one = jnp.sum(delta_normed * flat * scale_one, axis=0)
     input_grad = (
         delta_hidden
@@ -353,11 +704,6 @@
         lax.psum_scatter(delta_out_weight, ("row", "seq"), scatter_dimension=1, tiled=True),
         lax.psum_scatter(delta_gain_two, ("row", "seq"), scatter_dimension=0, tiled=True),
         lax.psum_scatter(delta_router, ("row", "seq"), scatter_dimension=0, tiled=True),
-    )
-    experts = (
-        lax.psum_scatter(delta_gate, ("row", "seq"), scatter_dimension=1, tiled=True),
-        lax.psum_scatter(delta_up, ("row", "seq"), scatter_dimension=1, tiled=True),
-        lax.psum_scatter(delta_down, ("row", "seq"), scatter_dimension=2, tiled=True),
     )
     return (
         layer_out,
@@ -369,9 +715,9 @@
         dense[4],
         dense[5],
         dense[6],
-        experts[0],
-        experts[1],
-        experts[2],
+        grads[0],
+        grads[1],
+        jnp.swapaxes(grads[2], 1, 2),
         expert_counts,
     )
 
@@ -408,4 +754,10 @@
         P(None, None, ("row", "seq")),
         P(),
     )
-    return jax.shard_map(body, mesh=mesh, in_specs=in_specs, out_specs=out_specs, check_vma=False)
+    return jax.shard_map(
+        functools.partial(body, mesh.shape["row"], mesh.shape["seq"]),
+        mesh=mesh,
+        in_specs=in_specs,
+        out_specs=out_specs,
+        check_vma=False,
+    )

time: 2720 us -> 1460 us (0.54)
  waiting for transfers between devices: 2140 us -> 726 us
  Pallas kernels: 0 us -> 403 us
  matrix products: 193 us -> 58.4 us
  local copies, waits for them, and re-layouts: 154 us -> 71.3 us
    reduce_scatter x3 -> x0, waiting for transfers between devices: 1080 us -> none  [the longest x1 361 us: body(): lax.psum_scatter(delta_up, ('row', 'seq'), scatter_dimension=1, tiled=True)]
    pallas_call x0 -> x3, Pallas kernels: none -> 403 us  [the longest x1 233 us: run_experts(): pl.pallas_call(functools.partial(experts_kernel, n_seq), out_shape=(jax.S...]
    all_gather x3 -> x0, waiting for transfers between devices: 283 us -> none  [the longest x1 103 us: body(): lax.all_gather(w_gate, ('row', 'seq'), axis=1, tiled=True)]
    dot_general x14 -> x5, matrix products: 140 us -> 7.54 us  [the longest x1 2.48 us: body(): jnp.dot(delta_logits, router_weight.T, preferred_element_type=jnp.float32)]
    gather x4 -> x1, local copies, waits for them, and re-layouts: 65.5 us -> 0.58 us  [body(): delta_gates = gate_grads[:, :, 0][slot].reshape(EXPERTS, token_count).T]
  transfers between devices with their start and end apart: 19 -> 13, of which waited for: 18 -> 11; matrix products, arithmetic and copies ran while one was open for 8% -> 5% of each run, Pallas kernels for 0% -> 12%
where the time goes in v1:
time: 1460 us
  waiting for transfers between devices  726 us (50%)
  Pallas kernels  403 us (28%)
  blocking collectives  158 us (11%)
  local copies, waits for them, and re-layouts  71.3 us (5%)
  matrix products  58.4 us (4%)
  other arithmetic  26.8 us (2%)
  between operations  14.9 us (1%)
    pallas_call x1, Pallas kernels, run_experts(): pl.pallas_call(functools.partial(experts_kernel, n_seq), out_shape=(jax.S...  233 us
    reduce_scatter x1, waiting for transfers between devices, body(): lax.psum_scatter(delta_out_weight, ('row', 'seq'), scatter_dimension=1, t...  142 us
    reduce_scatter x1, waiting for transfers between devices, body(): lax.psum_scatter(delta_value_weight, ('row', 'seq'), scatter_dimension=0,...  137 us
    reduce_scatter x1, waiting for transfers between devices, body(): lax.psum_scatter(delta_key_weight, ('row', 'seq'), scatter_dimension=0, t...  137 us
    pallas_call x1, Pallas kernels, gather_weights(): pl.pallas_call(functools.partial(weights_kernel, n_row, n_seq), out_shape...  96.6 us
    reduce_scatter x1, waiting for transfers between devices, body(): lax.psum_scatter(delta_query_weight, ('row', 'seq'), scatter_dimension=0,...  95.3 us
    unnamed x2, blocking collectives  79.6 us
    pallas_call x1, Pallas kernels, scatter_grads(): pl.pallas_call(functools.partial(grads_kernel, n_row, n_seq), out_shape=j...  73.2 us
  transfers between devices with their start and end apart: 13, of which 11 were waited for; matrix products, arithmetic and copies ran while one was open for 5% of the time, Pallas kernels for 12%

profile of v1, /device:TPU:0, one launch (start us, length us, event | category | flops | bytes accessed | tf_op | source)
XLA Modules:
  0.0 1460.3 jit_solution(13933618166222350436)
XLA Ops:
  13.2 42.1 %all-reduce.6 = (bf16[1024]{0:T(1024)(128)(2,1)S(1)}, bf16[1024]{0:T(1024)(128)(2,1)S(1)}) all-reduce(bf16[1024]{0:T(1024)(128)(2,1)S(1)} %dynamic-update-slice, bf16[1024]{0:T(1024)(128)(2,1)S(1)} %dynamic-update-slice.1), channel_id=1, replica_groups=mesh['row'=4,'seq'=8] {'row','seq'}, use_global_device_ids=true, to_apply=%add.1 | all-reduce | flops 2048 | bytes 8192
  58.6 9.1 all-gather.12.cloned.1.call-done
  67.6 1.5 copy.97
  71.0 52.5 %all-gather.8.cloned.1.call-done = bf16[1024,512]{1,0:T(8,128)(2,1)} async-done(((bf16[32,512]{1,0:T(8,128)(2,1)}), bf16[1024,512]{1,0:T(8,128)(2,1)}) %all-gather.8.cloned.1.call-update) | async-done | bytes 1048592 | tf_op jit(solution)/shard_map/all_gather | solution.py:503
  123.4 1.7 convolution_convert_fusion.1
  126.7 40.2 %all-gather = bf16[32,32,16]{1,2,0:T(8,128)(2,1)S(1)} all-gather(bf16[1,32,16]{1,2,0:T(8,128)(2,1)S(1)} %bitcast.359), channel_id=1, replica_groups=mesh['row'=4,'seq'=8] {'row','seq'}, dimensions={0}, use_global_device_ids=true | all-gather | bytes 33792 | tf_op jit(solution)/shard_map/all_gather | solution.py:506
  167.9 96.6 %weights.1.w_in = bf16[2,3,1024,512]{3,2,1,0:T(8,128)(2,1)} custom-call(bf16[16,32,512]{2,1,0:T(8,128)(2,1)} %gate.1, bf16[16,32,512]{2,1,0:T(8,128)(2,1)} %up.1, bf16[16,32,512]{2,1,0:T(8,128)(2,1)} %bitcast.352), custom_call_target="tpu_custom_call" | custom-call | tf_op jit(solution)/shard_map/weights/pallas_call | solution.py:180
  264.5 2.9 copy.99
  268.8 12.7 all-gather.10.cloned.1.call-done
  281.5 15.3 %while.26 = (s32[]{:T(128)}, bf16[2,128,1024]{2,1,0:T(8,128)(2,1)S(1)}, f32[2,8,2,128,1]{3,2,1,4,0:T(2,128)S(1)}, bf16[2,1024,512]{1,2,0:T(8,128)(2,1)}, s32[2,1...) while((s32[]{:T(128)}, ...), condition=%wide.region_6.7_spmd, body=%wide.region_3.6_spmd.sunk | while | flops 562559104 | bytes 33634944 | solution.py:563
  281.7 1.7 constant_dynamic-slice_fusion.14
  284.9 1.7 fusion.157
  286.6 2.3 fusion.158
  289.4 1.7 constant_dynamic-slice_fusion.14
  292.6 1.7 fusion.157
  294.3 2.3 fusion.158
  296.8 43.1 %all-gather.18.cloned.1.call-done = bf16[1024,1024]{0,1:T(8,128)(2,1)} async-done(((bf16[1024,32]{0,1:T(8,128)(2,1)}), bf16[1024,1024]{0,1:T(8,128)(2,1)}) %all-gather.18.cloned.1.call-update) | async-done | bytes 2097168 | tf_op jit(solution)/shard_map/all_gather | solution.py:504
  339.9 2.5 multiply_reduce_fusion.2
  343.5 233.4 %experts.1 = (f32[256,1024]{1,0:T(8,128)}, f32[256,1024]{1,0:T(8,128)}, f32[8,2,8,256]{3,2,1,0:T(8,128)}, bf16[3,1024,512]{2,1,0:T(8,128)(2,1)}) custom-call(bf16[256,1024]{1,0:T(8,128)(2,1)} %copy-done.12, bf16[256,1024]{1,0:T(8,128)(2,1)} %bitcast.342, f32[16,256]{1,0:T(8,128)} %fusion.67.gates_in, bf16[2,3,1024,512]{3,2,1,0:T(8,128)(2,1)} %weights.1.w_in), custom_call_target="tpu_custom_call" | custom-call | tf_op jit(solution)/shard_map/experts/pallas_call | solution.py:437
  578.4 2.5 multiply_reduce_fusion
  580.9 2.5 multiply_subtract_fusion
  586.7 66.1 %while.27 = (s32[]{:T(128)}, f32[2,128,1024]{1,2,0:T(8,128)}, f32[2,1024,512]{2,1,0:T(8,128)}, f32[2,1024,512]{2,1,0:T(8,128)}, bf16[2,1024,512]{1,2,0:T(8,128)(...) while((s32[]{:T(128)}, f32[2,128,1024]{1,2,0:T(8,128)}, ...), condition=%wide.region_15.16_spmd, body=%wide.region_13.15_spmd.sunk | while | flops 1374681216 | bytes 186720720 | solution.py:662
  587.1 1.7 constant_dynamic-slice_fusion.16
  590.4 2.1 constant_dynamic-slice_fusion.18
  592.5 2.5 fusion.171
  595.0 2.5 fusion.172
  597.5 1.9 copy-done.1
  599.5 2.3 bitcast_multiply_fusion.10
  601.8 1.8 copy.160
  603.6 6.8 fusion.173
  610.4 3.1 copy.159
  613.5 4.2 constant_dynamic-update-slice_fusion.9
  620.0 1.7 constant_dynamic-slice_fusion.16
  623.2 2.1 constant_dynamic-slice_fusion.18
  625.3 2.5 fusion.171
  627.9 2.5 fusion.172
  630.4 1.9 copy-done.1
  632.3 2.3 bitcast_multiply_fusion.10
  634.7 1.8 copy.160
  636.5 6.8 fusion.173
  643.3 3.1 copy.159
  646.3 4.2 constant_dynamic-update-slice_fusion.9
  657.9 2.7 fusion.92
  661.6 2.8 fusion.58
  664.5 38.5 %reduce-scatter.10.cloned.1.call-done = f32[2,128,512]{2,1,0:T(8,128)} async-done(((f32[2,1024,512]{2,1,0:T(8,128)}), f32[2,128,512]{2,1,0:T(8,128)}) %reduce-scatter.10.cloned.1.call-update) | async-done | bytes 524304 | tf_op jit(solution)/shard_map/reduce_scatter | solution.py:668
  702.9 2.0 copy.112
  707.4 1.8 fusion.93
  709.3 44.1 %reduce-scatter.12.cloned.1.call-done = f32[2,128,512]{2,1,0:T(8,128)} async-done(((f32[2,1024,512]{2,1,0:T(8,128)}), f32[2,128,512]{2,1,0:T(8,128)}) %reduce-scatter.12.cloned.1.call-update) | async-done | bytes 524304 | tf_op jit(solution)/shard_map/reduce_scatter | solution.py:669
  754.5 1.8 convolution_bitcast_fusion
  756.3 37.9 %psum.7 = s32[16]{0:T(128)} all-reduce(s32[16]{0:T(128)S(1)} %copy-done.43), channel_id=1, replica_groups=mesh['row'=4,'seq'=8] {'row','seq'}, use_global_device_ids=true, to_apply=%region_30.31 | all-reduce | flops 16 | bytes 128 | tf_op jit(solution)/shard_map/psum | solution.py:578
  796.3 2.5 copy.107
  798.8 2.5 copy.106
  802.7 73.2 %grads.1 = bf16[3,2,16,32,512]{4,3,2,1,0:T(8,128)(2,1)} custom-call(bf16[3,1024,512]{2,1,0:T(8,128)(2,1)} %get-tuple-element.137.grads), custom_call_target="tpu_custom_call" | custom-call | tf_op jit(solution)/shard_map/grads/pallas_call | solution.py:257
  875.9 3.1 convert_reduce_fusion
  880.2 1.8 slice_bitcast_fusion
  882.0 12.1 reduce-scatter.22.cloned.1.call-done
  895.5 2.0 copy.113
  898.8 1.7 convolution_add_fusion.2
  900.5 1.9 fusion.53
  902.5 37.6 %all-reduce.5 = (f32[1024]{0:T(1024)S(1)}, f32[1024]{0:T(1024)S(1)}) all-reduce(f32[1024]{0:T(1024)S(1)} %get-tuple-element.224, f32[1024]{0:T(1024)S(1)} %copy-done.38), channel_id=4, replica_groups=mesh['row'=4,'seq'=8] {'row','seq'}, use_global_device_ids=true, to_apply=%region_20.21.clone | all-reduce | flops 2048 | bytes 16384
  942.5 95.3 %reduce-scatter.14.cloned.1.call-done = f32[32,1024]{1,0:T(8,128)} async-done(((f32[1024,1024]{1,0:T(8,128)}), f32[32,1024]{1,0:T(8,128)}) %reduce-scatter.14.cloned.1.call-update) | async-done | bytes 131088 | tf_op jit(solution)/shard_map/reduce_scatter | solution.py:701
  1037.8 142.4 %reduce-scatter.20.cloned.1.call-done = f32[1024,32]{0,1:T(8,128)} async-done(((f32[1024,1024]{0,1:T(8,128)}), f32[1024,32]{0,1:T(8,128)}) %reduce-scatter.20.cloned.1.call-update) | async-done | bytes 131088 | tf_op jit(solution)/shard_map/reduce_scatter | solution.py:704
  1180.2 136.6 %reduce-scatter.16.cloned.1.call-done = f32[32,512]{1,0:T(8,128)} async-done(((f32[1024,512]{1,0:T(8,128)}), f32[32,512]{1,0:T(8,128)}) %reduce-scatter.16.cloned.1.call-update) | async-done | bytes 65552 | tf_op jit(solution)/shard_map/reduce_scatter | solution.py:702
  1316.8 136.8 %reduce-scatter.18.cloned.1.call-done = f32[32,512]{1,0:T(8,128)} async-done(((f32[1024,512]{1,0:T(8,128)}), f32[32,512]{1,0:T(8,128)}) %reduce-scatter.18.cloned.1.call-update) | async-done | bytes 65552 | tf_op jit(solution)/shard_map/reduce_scatter | solution.py:703
  (249 shorter events, 51.2 us)
Async XLA Ops:
  7.2 60.4 %all-gather.12.cloned.1.call-start = ((), (), s32[]{:S(2)}) async-start(), calls=%async_computation.9 | async-start | bytes 1081344 | tf_op jit(solution)/shard_map/all_gather | solution.py:502
  7.9 115.5 %all-gather.8.cloned.1.call-start = ((), (), s32[]{:S(2)}) async-start(), calls=%async_computation.7 | async-start | bytes 1081344 | tf_op jit(solution)/shard_map/all_gather | solution.py:503
  8.7 255.9 %all-gather.16.cloned.1.call-start = ((), (), s32[]{:S(2)}) async-start(), calls=%async_computation.11 | async-start | bytes 2162688 | tf_op jit(solution)/shard_map/all_gather | solution.py:501
  9.4 259.4 %all-gather.14.cloned.1.call-start = ((), (), s32[]{:S(2)}) async-start(), calls=%async_computation.10 | async-start | bytes 2359296 | tf_op jit(solution)/shard_map/all_gather | solution.py:539
  55.2 15.5 %copy-start.34 = (f32[1024]{0:T(1024)}, f32[1024]{0:T(1024)S(1)}, u32[]{:S(2)}) copy-start(f32[1024]{0:T(1024)S(1)} %convert_element_type.133) | copy-start | bytes 12292
  55.5 212.8 %copy-start.23 = (f32[256,64]{0,1:T(8,128)}, f32[256,64]{0,1:T(8,128)S(1)}, u32[]{:S(2)}) copy-start(f32[256,64]{0,1:T(8,128)S(1)} %get-tuple-element.301) | copy-start | bytes 196612
  55.5 212.8 %copy-start.28 = (f32[256,64]{0,1:T(8,128)}, f32[256,64]{0,1:T(8,128)S(1)}, u32[]{:S(2)}) copy-start(f32[256,64]{0,1:T(8,128)S(1)} %get-tuple-element.302) | copy-start | bytes 196612
  57.3 13.4 copy-start.36
  58.6 208.9 %copy-start.6 = (bf16[2,128,1024]{2,1,0:T(8,128)(2,1)}, bf16[2,128,1024]{2,1,0:T(8,128)(2,1)S(1)}, u32[]{:S(2)}) copy-start(bf16[2,128,1024]{2,1,0:T(8,128)(2,1)S(1)} %fusion.46) | copy-start | bytes 1572868
  67.6 3.1 copy-start.10
  69.7 56.9 %copy-start.33 = (s32[2,1024]{1,0:T(2,128)S(1)}, s32[2,1024]{1,0:T(2,128)}, u32[]{:S(2)}) copy-start(s32[2,1024]{1,0:T(2,128)} %param.19) | copy-start | bytes 24580
  69.7 57.0 %copy-start.42 = (bf16[32,16]{0,1:T(8,128)(2,1)S(1)}, bf16[32,16]{0,1:T(8,128)(2,1)}, u32[]{:S(2)}) copy-start(bf16[32,16]{0,1:T(8,128)(2,1)} %param.27) | copy-start | bytes 3076
  69.7 97.4 %copy-start.41 = (s32[1,2,128,8]{2,3,1,0:T(8,128)S(1)}, s32[1,2,128,8]{2,3,1,0:T(8,128)}, u32[]{:S(2)}) copy-start(s32[1,2,128,8]{2,3,1,0:T(8,128)} %param.20) | copy-start | bytes 24580
  70.7 210.8 %all-gather.10.cloned.1.call-start = ((), (), s32[]{:S(2)}) async-start(), calls=%async_computation.8 | async-start | bytes 2359296 | tf_op jit(solution)/shard_map/all_gather | solution.py:540
  125.9 213.9 %all-gather.18.cloned.1.call-start = ((), (), s32[]{:S(2)}) async-start(), calls=%async_computation.12 | async-start | bytes 2162688 | tf_op jit(solution)/shard_map/all_gather | solution.py:504
  126.5 576.4 %reduce-scatter.10.cloned.1.call-start = ((), (), s32[]{:S(2)}) async-start(), calls=%async_computation.13 | async-start | bytes 4718592 | tf_op jit(solution)/shard_map/reduce_scatter | solution.py:668
  268.2 13.3 copy-start.30
  296.8 280.0 %copy-start.31 = (bf16[2,128,1024]{2,1,0:T(8,128)(2,1)}, bf16[2,128,1024]{2,1,0:T(8,128)(2,1)S(1)}, u32[]{:S(2)}) copy-start(bf16[2,128,1024]{2,1,0:T(8,128)(2,1)S(1)} %get-tuple-element.129) | copy-start | bytes 1572868
  343.5 237.5 %copy-start.25 = (bf16[2,128,1024]{2,1,0:T(8,128)(2,1)S(1)}, bf16[2,128,1024]{2,1,0:T(8,128)(2,1)}, u32[]{:S(2)}) copy-start(bf16[2,128,1024]{2,1,0:T(8,128)(2,1)} %param.31) | copy-start | bytes 1572868
  578.4 5.9 copy-start.26
  587.1 3.0 copy-start.4
  587.1 5.4 copy-start.15
  590.1 4.9 copy-start
  597.5 1.9 copy-start.1
  610.4 3.1 copy-start.3
  613.5 4.2 copy-start.2
  617.7 1.2 copy-start.20
  617.7 2.2 copy-start.5
  617.7 2.2 copy-start.16
  619.0 1.0 copy-start.21
  620.0 3.0 copy-start.4
  620.0 5.4 copy-start.15
  623.0 4.9 copy-start
  630.4 1.9 copy-start.1
  643.3 3.1 copy-start.3
  646.3 4.2 copy-start.2
  650.5 1.2 copy-start.20
  650.5 2.2 copy-start.5
  650.5 2.2 copy-start.16
  651.8 1.0 copy-start.21
  652.8 1.2 copy-start.22
  652.8 100.6 %reduce-scatter.12.cloned.1.call-start = ((), (), s32[]{:S(2)}) async-start(), calls=%async_computation.14 | async-start | bytes 4718592 | tf_op jit(solution)/shard_map/reduce_scatter | solution.py:669
  652.8 2.8 copy-start.13
  652.9 4.0 copy-start.29
  653.5 240.5 %reduce-scatter.22.cloned.1.call-start = ((), (), s32[]{:S(2)}) async-start(), calls=%async_computation.19 | async-start | bytes 540672
  654.8 2.2 copy-start.24
  656.8 1.0 copy-start.7
  657.3 380.5 %reduce-scatter.14.cloned.1.call-start = ((), (), s32[]{:S(2)}) async-start(), calls=%async_computation.15 | async-start | bytes 4325376 | tf_op jit(solution)/shard_map/reduce_scatter | solution.py:701
  657.9 2.8 copy-start.9
  660.6 1.0 copy-start.32
  660.6 519.6 %reduce-scatter.20.cloned.1.call-start = ((), (), s32[]{:S(2)}) async-start(), calls=%async_computation.18 | async-start | bytes 4325376 | tf_op jit(solution)/shard_map/reduce_scatter | solution.py:704
  664.4 652.4 %reduce-scatter.16.cloned.1.call-start = ((), (), s32[]{:S(2)}) async-start(), calls=%async_computation.16 | async-start | bytes 2162688 | tf_op jit(solution)/shard_map/reduce_scatter | solution.py:702
  709.2 47.1 %copy-start.43 = (s32[16]{0:T(128)S(1)}, s32[16]{0:T(128)}, u32[]{:S(2)}) copy-start(s32[16]{0:T(128)} %get-tuple-element.226) | copy-start | bytes 196
  709.3 744.4 %reduce-scatter.18.cloned.1.call-start = ((), (), s32[]{:S(2)}) async-start(), calls=%async_computation.17 | async-start | bytes 2162688 | tf_op jit(solution)/shard_map/reduce_scatter | solution.py:703
  756.3 42.6 %copy-start.40 = (f32[2,128]{1,0:T(2,128)S(1)}, f32[2,128]{1,0:T(2,128)}, u32[]{:S(2)}) copy-start(f32[2,128]{1,0:T(2,128)} %copy-done.39) | copy-start | bytes 3076
  875.9 3.2 copy-start.17
  875.9 3.2 copy-start.18
  875.9 3.1 copy-start.19
  875.9 3.5 copy-start.14
  880.2 17.3 %copy-start.27 = (f32[2,128,512]{2,1,0:T(8,128)S(1)}, f32[2,128,512]{2,1,0:T(8,128)}, u32[]{:S(2)}) copy-start(f32[2,128,512]{2,1,0:T(8,128)} %reduce-scatter.10.cloned.1.call-done) | copy-start | bytes 1572868
  881.9 18.6 %copy-start.11 = (bf16[2,128,1024]{2,1,0:T(8,128)(2,1)S(1)}, bf16[2,128,1024]{2,1,0:T(8,128)(2,1)}, u32[]{:S(2)}) copy-start(bf16[2,128,1024]{2,1,0:T(8,128)(2,1)} %param.18) | copy-start | bytes 1572868
  881.9 18.6 %copy-start.35 = (f32[1024]{0:T(1024)S(1)}, f32[1024]{0:T(1024)}, u32[]{:S(2)}) copy-start(f32[1024]{0:T(1024)} %copy-done.34) | copy-start | bytes 12292
  882.0 18.6 %copy-start.37 = (f32[256]{0:T(256)S(1)}, f32[256]{0:T(256)}, u32[]{:S(2)}) copy-start(f32[256]{0:T(256)} %copy-done.36) | copy-start | bytes 3076
  897.5 5.0 copy-start.38
  (3 other events, 2.5 us)
Sparse Core Ops, SparseCore 0:
  11.0 56.5 all-gather.11
  70.6 52.7 all-gather.7
  126.4 62.9 all-gather.15
  191.4 55.7 all-gather.13
  249.2 32.2 all-gather.9
  284.3 55.5 all-gather.17
  652.9 49.9 reduce-scatter.9
  705.2 48.1 reduce-scatter.11
  755.6 138.3 reduce-scatter.21
  896.9 140.8 reduce-scatter.13
  1040.8 139.4 reduce-scatter.19
  1183.0 133.7 reduce-scatter.15
  1319.7 133.8 reduce-scatter.17

commit v2 on v1

v2 whole, which is shorter than its diff:
```python
import functools

import jax
import jax.numpy as jnp
from jax import lax
from jax.experimental import pallas as pl
from jax.experimental.pallas import tpu as pltpu
from jax.sharding import PartitionSpec as P

HEAD = 64
EXPERTS = 16
TOPK = 8

EPSILON = 1e-06
SCORE_SCALE = 0.015625
RESIDUAL = 0.22
THETA = 10000.0
NEGATIVE = -1e30

MESH = pl.DeviceIdType.MESH
ANY = pl.BlockSpec(memory_space=pl.ANY)
VMEM = pl.BlockSpec(memory_space=pltpu.VMEM)


def norm_scale(value):
    return lax.rsqrt(jnp.mean(value * value, axis=-1, keepdims=True) + EPSILON)


def rope_tables(positions, width):
    half = width // 2
    frequency = THETA ** (-2.0 * jnp.arange(half, dtype=jnp.float32) / width)
    angle = positions.astype(jnp.float32)[..., None] * frequency
    angle = jnp.concatenate([angle, angle], axis=-1)
    return (jnp.cos(angle), jnp.sin(angle))


def greet_all(n_row, n_seq):
    row, seq = lax.axis_index("row"), lax.axis_index("seq")
    me, total = row * n_seq + seq, n_row * n_seq
    barrier = pltpu.get_barrier_semaphore()

    def greet(step, carry):
        other = (me + step) % total
        pl.semaphore_signal(
            barrier, inc=1, device_id=(other // n_seq, other % n_seq), device_id_type=MESH
        )
        return carry

    lax.fori_loop(1, total, greet, 0)
    pl.semaphore_wait(barrier, total - 1)


NN = (((1,), (0,)), ((), ()))
NT = (((1,), (1,)), ((), ()))
TN = (((0,), (0,)), ((), ()))


def mul(a, b, dims):
    return lax.dot_general(a, b, dims, preferred_element_type=jnp.float32)


def column(row_values):
    return jnp.broadcast_to(row_values, (128, row_values.shape[1])).T


def peer_of(row, seq, step):
    other_row = (row // 2 + step // 4) % 2 * 2 + (row % 2 + step // 2 % 2) % 2
    other_seq = seq // 4 * 4 + (seq // 2 % 2 + step % 2) % 2 * 2 + seq % 2
    return (other_row, other_seq)


def row_of(row, step):
    return (row // 2 + step // 2) % 2 * 2 + (row % 2 + step % 2) % 2


def remote(source, target, send, recv, device):
    return pltpu.make_async_remote_copy(
        src_ref=source, dst_ref=target, send_sem=send, recv_sem=recv, device_id=device,
        device_id_type=MESH,
    )


def forward_kernel(
    n_row, n_seq, back,
    packed, x_in, g_in, cos_in, sin_in, start_in, picks_in, gate, up, down,
    xtwo_out, gates_out, counts_out, hidden_out, mixed_out, lse_out, normed_out, queries_out, kv_out, weights_out, g_out, held,
    wall, kv, queries, normed, mixed, hidden, lse,
    z_send, z_recv, p_send, p_recv, d_send, d_recv, kv_send, kv_recv, kvd_send, kvd_recv,
    g_send, g_recv, e_send, e_recv, e_local, pass_send, pass_recv, local, store,
):
    row, seq = lax.axis_index("row"), lax.axis_index("seq")
    core, deep, n_deep = seq % 2, seq // 2, n_seq // 2
    me, total = row * n_seq + seq, n_row * n_seq
    sibling = (row, deep * 2 + (1 - core))
    rows = packed.shape[0]
    tokens, width = x_in.shape
    block = tokens // 2
    low, full = jnp.bfloat16, jnp.float32
    slots = kv.shape[0]
    greet_all(n_row, n_seq)

    def part(of_row, of_deep, of_core):
        return wall.at[pl.ds(pl.multiple_of((of_row * n_seq + of_deep * 2 + of_core) * rows, rows), rows)]

    mine = part(row, deep, core)
    own_copy = pltpu.make_async_copy(packed, mine, local.at[0])
    own_copy.start()

    def z_copy(step, source):
        return remote(source, mine, z_send.at[step], z_recv.at[step],
                      (row, (deep + step) % n_deep * 2 + core))

    def plane_copy(step, hop, source):
        here = part(row, (deep + n_deep - hop) % n_deep, core)
        return remote(here if source is None else source, here, p_send.at[hop, step], p_recv.at[hop, step],
                      (row_of(row, step), seq))

    def core_copy(step, hop, source):
        here = part(row_of(row, step), (deep + n_deep - hop) % n_deep, core)
        return remote(here if source is None else source, here, d_send.at[hop, step], d_recv.at[hop, step], sibling)

    def start_z(step, carry):
        z_copy(step, packed).start()
        return carry

    lax.fori_loop(1, n_deep, start_z, 0)
    for step in range(1, 4):
        plane_copy(step, 0, packed).start()
    core_copy(0, 0, packed).start()

    x = x_in[...].astype(full)
    scale_one = norm_scale(x)

    def relay(hop, carry):
        there = part(row, (deep + n_deep - hop) % n_deep, core)
        remote(there, there, z_send.at[hop], z_recv.at[hop], sibling).wait_recv()
        for step in range(1, 4):
            plane_copy(step, hop, None).start()
        core_copy(0, hop, None).start()
        return carry

    lax.fori_loop(1, n_deep, relay, 0)

    def expert_copy(kind, source, step):
        other = (me + step) % total
        other_row, other_seq = other // n_seq, other % n_seq
        return remote(
            source.at[other_row * 4 + other_seq % 4],
            held.at[other_seq % 2, kind, pl.ds(pl.multiple_of(me * rows, rows), rows)],
            e_send.at[kind, step], e_recv.at[kind, step], (other_row, other_seq),
        )

    sources = (gate, up, down)
    expert_own = [
        pltpu.make_async_copy(
            source.at[row * 4 + seq % 4],
            held.at[core, kind, pl.ds(pl.multiple_of(me * rows, rows), rows)],
            e_local.at[kind],
        )
        for kind, source in enumerate(sources)
    ]
    for copy in expert_own:
        copy.start()

    def start_experts(step, carry):
        for kind, source in enumerate(sources):
            expert_copy(kind, source, step).start()
        return carry

    def spread(index, carry):
        hop, step = index // 3, index % 3 + 1
        there = part(row_of(row, step), (deep + n_deep - hop) % n_deep, core)
        remote(there, there, p_send.at[hop, step], p_recv.at[hop, step], sibling).wait_recv()
        core_copy(step, hop, None).start()
        return carry

    lax.fori_loop(0, n_deep * 3, spread, 0)
    lax.fori_loop(1, total, start_experts, 0)
    own_copy.wait()

    def gathered(index, carry):
        hop, step = index // 4, index % 4
        there = part(row_of(row, step), (deep + n_deep - hop) % n_deep, 1 - core)
        remote(there, there, d_send.at[hop, step], d_recv.at[hop, step], sibling).wait_recv()
        return carry

    lax.fori_loop(0, n_deep * 4, gathered, 0)

    small = wall[:, 3072:].astype(full).T
    gain_one, gain_two = small[16:17], small[17:18]
    normed[...] = (x * scale_one * gain_one).astype(low)
    counts_out[...] = jnp.broadcast_to(jnp.sum(wall[:, 3072:].astype(full), axis=0, keepdims=True), (8, 128))

    lane = lax.broadcasted_iota(jnp.int32, (tokens, 128), 1)
    cosine, sine = cos_in[...], sin_in[...]

    def turn(value):
        return value * cosine + jnp.where(lane % 64 < 32, pltpu.roll(value, 96, 1), pltpu.roll(value, 32, 1)) * sine

    for pair in range(4):
        lanes = slice(1024 + 128 * pair, 1152 + 128 * pair)
        key = turn(mul(normed[...], wall[:, lanes], NN)).astype(low)
        lanes = slice(1536 + 128 * pair, 1664 + 128 * pair)
        value = mul(normed[...], wall[:, lanes], NN).astype(low)
        for t in range(2):
            here = slice(block * t, block * (t + 1))
            kv[core, t, :, 128 * pair:128 * (pair + 1)] = key[here]
            kv[core, t, :, 512 + 128 * pair:640 + 128 * pair] = value[here]

    def kv_copy(hop):
        return remote(kv.at[core], kv.at[hop * 2 + core], kv_send.at[hop], kv_recv.at[hop],
                      (row, seq + 2 * hop))

    def kv_pass(hop, of_core):
        there = kv.at[hop * 2 + of_core]
        return remote(there, there, kvd_send.at[hop], kvd_recv.at[hop], sibling)

    for hop in range(1, back + 1):
        @pl.when(deep + hop < n_deep)
        def _():
            kv_copy(hop).start()

        @pl.when(deep < hop)
        def _():
            kv[2 * hop] = jnp.zeros(kv.shape[1:], low)
            kv[2 * hop + 1] = jnp.zeros(kv.shape[1:], low)

    kv_pass(0, core).start()

    def g_copy(step):
        return remote(g_in, g_out.at[step], g_send.at[step], g_recv.at[step], peer_of(row, seq, step))

    def start_g(step, carry):
        g_copy(step).start()
        return carry

    lax.fori_loop(1, 8, start_g, 0)
    g_own = pltpu.make_async_copy(g_in, g_out.at[0], g_send.at[0])
    g_own.start()

    half_lane = lax.broadcasted_iota(jnp.int32, (block, 128), 1) < 64
    for head in range(8):
        both = turn(mul(normed[...], wall[:, 128 * head:128 * (head + 1)], NN))
        for t in range(2):
            value = both[block * t:block * (t + 1)]
            other = pltpu.roll(value, 64, 1)
            if head % 2 == 0:
                first, second = jnp.where(half_lane, value, 0.0), jnp.where(half_lane, other, 0.0)
            else:
                first, second = jnp.where(half_lane, 0.0, other), jnp.where(half_lane, 0.0, value)
            queries[t * 8 + head, :block] = first.astype(low)
            queries[t * 8 + head, block:] = second.astype(low)

    for hop in range(1, back + 1):
        @pl.when(deep >= hop)
        def _():
            remote(kv.at[core], kv.at[hop * 2 + core], kv_send.at[hop], kv_recv.at[hop], sibling).wait_recv()
            kv_pass(hop, core).start()

    kv_pass(0, 1 - core).wait_recv()
    for hop in range(1, back + 1):
        @pl.when(deep >= hop)
        def _():
            kv_pass(hop, 1 - core).wait_recv()

    for t in range(2):
        visible = visibility(deep, seq, slots, block, start_in[block * t:block * (t + 1)])

        def attend(pair, carry):
            lanes = pl.ds(pl.multiple_of(128 * pair, 128), 128)
            value_lanes = pl.ds(pl.multiple_of(512 + 128 * pair, 128), 128)
            values = jnp.concatenate([kv[slot, t, :, value_lanes] for slot in range(slots)], axis=0)
            for half in range(2):
                head = 2 * pair + half
                query = queries[t * 8 + head]
                scores = jnp.concatenate(
                    [mul(query, kv[slot, t, :, lanes], NT) for slot in range(slots)], axis=1
                )
                scores = jnp.where(visible, SCORE_SCALE * scores, NEGATIVE)
                peak = jnp.max(scores, axis=1, keepdims=True)
                raised = jnp.exp(scores - peak)
                denominator = jnp.sum(raised, axis=1, keepdims=True)
                probs = (raised / denominator).astype(low)
                out = mul(probs, values, NN)
                if half == 0:
                    joined = jnp.where(half_lane, out[:block], pltpu.roll(out[block:], 64, 1))
                else:
                    joined = jnp.where(half_lane, pltpu.roll(out[:block], 64, 1), out[block:])
                mixed[block * t:block * (t + 1), pl.ds(pl.multiple_of(128 * head, 128), 128)] = joined.astype(low)
                lse[t] = jnp.where(lane == head, peak + jnp.log(denominator), lse[t])
            return carry

        lax.fori_loop(0, 4, attend, 0)

    for lo in range(0, width, 256):
        branch = mul(mixed[...], wall[lo:lo + 256, 2048:3072], NT)
        hidden[:, lo:lo + 256] = x_in[:, lo:lo + 256].astype(full) + RESIDUAL * branch
    scale_two = norm_scale(hidden[...])
    xtwo_out[...] = (hidden[...] * scale_two * gain_two).astype(low)
    logits = mul(xtwo_out[...], wall[:, 3072:], NN)
    picked = picks_in[...] > 0
    logits = jnp.where(picked, logits, NEGATIVE)
    raised = jnp.where(picked, jnp.exp(logits - jnp.max(logits, axis=1, keepdims=True)), 0.0)
    gates = raised / jnp.sum(raised, axis=1, keepdims=True)
    gates_out[...] = gates.T[:EXPERTS]

    stores = [
        pltpu.make_async_copy(source, target, store.at[i])
        for i, (source, target) in enumerate((
            (wall, weights_out), (kv, kv_out), (queries, queries_out), (normed, normed_out),
            (mixed, mixed_out), (hidden, hidden_out), (lse, lse_out),
        ))
    ]
    for copy in stores:
        copy.start()

    def arrived(step, carry):
        other = (me + total - step) % total
        for kind in range(3):
            there = held.at[core, kind, pl.ds(pl.multiple_of(other * rows, rows), rows)]
            remote(there, there, e_send.at[kind, step], e_recv.at[kind, step], sibling).wait_recv()
        return carry

    lax.fori_loop(1, total, arrived, 0)
    for copy in expert_own:
        copy.wait()
    remote(held.at[core], held.at[core], pass_send, pass_recv, sibling).start()

    def settle_experts(step, carry):
        for kind, source in enumerate(sources):
            expert_copy(kind, source, step).wait_send()
        return carry

    lax.fori_loop(1, total, settle_experts, 0)

    def settle_g(step, carry):
        g_copy(step).wait()
        return carry

    lax.fori_loop(1, 8, settle_g, 0)
    g_own.wait()

    def settle_z(step, carry):
        z_copy(step, packed).wait_send()
        return carry

    lax.fori_loop(1, n_deep, settle_z, 0)

    def settle_plane(index, carry):
        hop, step = index // 4, index % 4
        core_copy(step, hop, None).wait_send()

        @pl.when(step > 0)
        def _():
            plane_copy(step, hop, None).wait_send()

        return carry

    lax.fori_loop(0, n_deep * 4, settle_plane, 0)
    kv_pass(0, core).wait_send()
    for hop in range(1, back + 1):
        @pl.when(deep + hop < n_deep)
        def _():
            kv_copy(hop).wait_send()

        @pl.when(deep >= hop)
        def _():
            kv_pass(hop, core).wait_send()

    for copy in stores:
        copy.wait()
    share = remote(held.at[core], held.at[1 - core], pass_send, pass_recv, sibling)
    share.wait_recv()
    remote(held.at[core], held.at[core], pass_send, pass_recv, sibling).wait_send()


def visibility(deep, seq, slots, block, start):
    key = lax.broadcasted_iota(jnp.int32, (block, block), 1)
    query = lax.broadcasted_iota(jnp.int32, (block, block), 0) + seq * block
    tiles = []
    for slot in range(slots):
        position = key + ((deep - slot // 2) * 2 + slot % 2) * block
        seen = jnp.where((position >= start) & (position <= query), 1.0, 0.0)
        tiles.append(jnp.concatenate([seen, seen], axis=0))
    return jnp.concatenate(tiles, axis=1) > 0.5


def run_forward(n_row, n_seq, length, packed, x, g, cosine, sine, start, picks, gate, up, down):
    tokens, width = x.shape
    experts, rows, hidden = gate.shape
    total, n_deep = n_row * n_seq, n_seq // 2
    block = tokens // 2
    back = window_of(length, block, n_deep)
    slots = 2 * (back + 1)
    low, full = jnp.bfloat16, jnp.float32
    dma = pltpu.SemaphoreType.DMA
    kv = (slots, 2, block, 1024)
    shape = jax.ShapeDtypeStruct
    return pl.pallas_call(
        functools.partial(forward_kernel, n_row, n_seq, back),
        out_shape=(
            shape((tokens, width), low),
            shape((EXPERTS, tokens), full),
            shape((8, 128), full),
            shape((tokens, width), full),
            shape((tokens, 1024), low),
            shape((2, 2 * block, 128), full),
            shape((tokens, width), low),
            shape((16, 2 * block, 128), low),
            shape(kv, low),
            shape((width, packed.shape[1]), low),
            shape((8, tokens, width), low),
            shape((2, 3, width, hidden), low),
        ),
        in_specs=[ANY, VMEM, ANY, VMEM, VMEM, VMEM, VMEM, ANY, ANY, ANY],
        out_specs=(VMEM, VMEM, VMEM) + (ANY,) * 9,
        scratch_shapes=[
            pltpu.VMEM((width, packed.shape[1]), low),
            pltpu.VMEM(kv, low),
            pltpu.VMEM((16, 2 * block, 128), low),
            pltpu.VMEM((tokens, width), low),
            pltpu.VMEM((tokens, 1024), low),
            pltpu.VMEM((tokens, width), full),
            pltpu.VMEM((2, 2 * block, 128), full),
            dma((n_deep,)), dma((n_deep,)),
            dma((n_deep, 4)), dma((n_deep, 4)),
            dma((n_deep, 4)), dma((n_deep, 4)),
            dma((back + 1,)), dma((back + 1,)),
            dma((back + 1,)), dma((back + 1,)),
            dma((8,)), dma((8,)),
            dma((3, total)), dma((3, total)), dma((3,)),
            dma, dma, dma((1,)), dma((7,)),
        ],
        compiler_params=pltpu.CompilerParams(
            collective_id=1, has_side_effects=True, vmem_limit_bytes=60 << 20
        ),
        name="forward",
    )(packed, x, g, cosine, sine, start, picks, gate, up, down)


def experts_kernel(
    n_seq, x_in, gates_in, g_in, w_in, y_made, dx_out, dg_out, grad_out,
    xs, gs, gates, w, acc, y_acc, dx_acc, dg_made, dx_got, dg_got, total_low,
    in_send, in_recv, out_send, out_recv, y_store, w_sem, g_sem, half_send, half_recv, ready, done_sem,
):
    row, seq = lax.axis_index("row"), lax.axis_index("seq")
    core, chip_z = seq % 2, seq // 2 % 2
    width = x_in.shape[1]
    chunk = 256
    mine = (row * 2 + chip_z) * 2
    low, full = jnp.bfloat16, jnp.float32
    sibling = (row, seq // 2 * 2 + (1 - core))
    fetch = [pltpu.make_async_copy(w_in.at[j], w.at[j], w_sem.at[j]) for j in range(2)]
    fetch.append(pltpu.make_async_copy(g_in, gs, g_sem))
    for copy in fetch:
        copy.start()
    barrier = pltpu.get_barrier_semaphore()

    def greet(step, carry):
        pl.semaphore_signal(barrier, inc=1, device_id=peer_of(row, seq, step), device_id_type=MESH)
        return carry

    lax.fori_loop(1, 8, greet, 0)
    pl.semaphore_signal(barrier, inc=1, device_id=sibling, device_id_type=MESH)
    pl.semaphore_wait(barrier, 8)

    def inward(step):
        return [
            remote(source, target.at[step], in_send.at[i, step], in_recv.at[i, step], peer_of(row, seq, step))
            for i, (source, target) in enumerate(((x_in, xs), (gates_in, gates)))
        ]

    def outward(step):
        return [
            remote(source.at[step], target.at[step], out_send.at[i, step], out_recv.at[i, step], peer_of(row, seq, step))
            for i, (source, target) in enumerate(((gs, dx_got), (dg_made, dg_got)))
        ]

    def y_copy(step):
        return pltpu.make_async_copy(xs.at[step], y_made.at[step], y_store.at[step])

    def send_in(step, carry):
        for copy in inward(step):
            copy.start()
        return carry

    lax.fori_loop(1, 8, send_in, 0)
    xs[0] = x_in[...]
    gates[0] = gates_in[...]
    acc[...] = jnp.zeros_like(acc)
    for copy in fetch:
        copy.wait()

    def block(step, carry):
        @pl.when(step > 0)
        def _():
            for copy in inward(step):
                copy.wait_recv()

        y_acc[...] = jnp.zeros_like(y_acc)
        dx_acc[...] = jnp.zeros_like(dx_acc)

        def expert(j, inner_carry):
            gate = column(gates[step, pl.ds(mine + j, 1)])[:, :1]
            x = xs[step]
            a = mul(x, w[j, 0], NN)
            b = mul(x, w[j, 1], NN)
            sigma = jax.nn.sigmoid(a)
            smooth = a * sigma
            inner = (smooth * b).astype(low)
            dgate = jnp.zeros((x.shape[0], 1), full)
            d_inner = jnp.zeros(a.shape, full)
            for lo in range(0, width, chunk):
                part = slice(lo, lo + chunk)
                delta = RESIDUAL * gs[step, :, part].astype(full)
                y = mul(inner, w[j, 2, part], NT)
                y_acc[:, part] += gate * y
                dgate += jnp.sum(delta * y, axis=1, keepdims=True)
                dy = (gate * delta).astype(low)
                d_inner += mul(dy, w[j, 2, part], NN)
                acc[j, 2, part] += mul(dy, inner, TN)
            da = (d_inner * b * sigma * (1.0 + a * (1.0 - sigma))).astype(low)
            db = (d_inner * smooth).astype(low)
            for lo in range(0, width, chunk):
                part = slice(lo, lo + chunk)
                x_part = xs[step, :, part]
                acc[j, 0, part] += mul(x_part, da, TN)
                acc[j, 1, part] += mul(x_part, db, TN)
                dx_acc[:, part] += mul(da, w[j, 0, part], NT) + mul(db, w[j, 1, part], NT)
            dg_made[step, j] = jnp.broadcast_to(dgate, (dgate.shape[0], 128)).T[:8]
            return inner_carry

        lax.fori_loop(0, 2, expert, 0)
        xs[step] = y_acc[...].astype(low)
        y_copy(step).start()
        gs[step] = dx_acc[...].astype(low)

        @pl.when(step > 0)
        def _():
            for copy in outward(step):
                copy.start()

        return carry

    lax.fori_loop(0, 8, block, 0)

    pl.semaphore_signal(ready, inc=1, device_id=sibling, device_id_type=MESH)
    w[1 - core] = acc[1 - core].astype(low)
    pl.semaphore_wait(ready, 1)
    half = remote(w.at[1 - core], total_low, half_send, half_recv, sibling)
    half.start()
    dx_got[0] = gs[0]
    dg_got[0] = dg_made[0]
    half.wait_recv()
    total_low[...] = (acc[core] + total_low[...].astype(full)).astype(low)
    store = pltpu.make_async_copy(total_low, grad_out, done_sem)
    store.start()

    def settle(step, carry):
        for copy in inward(step):
            copy.wait_send()
        for copy in outward(step):
            copy.wait()
        return carry

    lax.fori_loop(1, 8, settle, 0)
    dx_out[...] = sum(dx_got[i].astype(full) for i in range(8))

    def place(step, carry):
        other_row, other_seq = peer_of(row, seq, step)
        chip = other_row * 2 + other_seq // 2 % 2
        for j in range(2):
            dg_out[pl.ds(chip * 2 + j, 1)] = dg_got[step, j, :1]
        y_copy(step).wait()
        return carry

    lax.fori_loop(0, 8, place, 0)
    half.wait_send()
    store.wait()


def run_experts(n_row, n_seq, x, gates, g, w):
    tokens, width = x.shape
    hidden = w.shape[3]
    low, full = jnp.bfloat16, jnp.float32
    dma, shape = pltpu.SemaphoreType.DMA, jax.ShapeDtypeStruct
    return pl.pallas_call(
        functools.partial(experts_kernel, n_seq),
        out_shape=(
            shape((8, tokens, width), low),
            shape((tokens, width), full),
            shape((EXPERTS, tokens), full),
            shape((3, width, hidden), low),
        ),
        in_specs=[VMEM, VMEM, ANY, ANY],
        out_specs=(ANY, VMEM, VMEM, ANY),
        scratch_shapes=[
            pltpu.VMEM((8, tokens, width), low),
            pltpu.VMEM((8, tokens, width), low),
            pltpu.VMEM((8, EXPERTS, tokens), full),
            pltpu.VMEM((2, 3, width, hidden), low),
            pltpu.VMEM((2, 3, width, hidden), full),
            pltpu.VMEM((tokens, width), full),
            pltpu.VMEM((tokens, width), full),
            pltpu.VMEM((8, 2, 8, tokens), full),
            pltpu.VMEM((8, tokens, width), low),
            pltpu.VMEM((8, 2, 8, tokens), full),
            pltpu.VMEM((3, width, hidden), low),
            dma((2, 8)),
            dma((2, 8)),
            dma((2, 8)),
            dma((2, 8)),
            dma((8,)),
            dma((2,)),
            dma,
            dma,
            dma,
            pltpu.SemaphoreType.REGULAR,
            dma,
        ],
        compiler_params=pltpu.CompilerParams(
            collective_id=3, has_side_effects=True, vmem_limit_bytes=60 << 20
        ),
        name="experts",
    )(x, gates, g, w)


def backward_kernel(
    n_row, n_seq, back,
    dense, kv_in, queries_in, normed_in, mixed_in, x_in, g_in, cos_in, sin_in, start_in,
    hidden_in, xtwo_in, gates_in, dgates_in, dx_in, lse_in, y_made, expert_grads,
    y_got, input_out, q_out, k_out, v_out, o_out, small_out, held,
    wall, kv, queries, outs, dq, dqkv, dkv_own, dkv_core, dkv_deep, grads, from_core, from_plane, from_deep,
    load, k_send, k_recv, kd_send, kd_recv, y_send, y_recv, e_send, e_recv, e_local,
    d_send, d_recv, p_send, p_recv, z_send, z_recv,
):
    row, seq = lax.axis_index("row"), lax.axis_index("seq")
    core, deep, n_deep = seq % 2, seq // 2, n_seq // 2
    me, total = row * n_seq + seq, n_row * n_seq
    sibling = (row, deep * 2 + (1 - core))
    rows = q_out.shape[0]
    tokens, width = x_in.shape
    block = tokens // 2
    low, full = jnp.bfloat16, jnp.float32
    slots = kv.shape[0]
    loads = [
        pltpu.make_async_copy(source, target, load.at[i])
        for i, (source, target) in enumerate(((dense, wall), (kv_in, kv), (queries_in, queries)))
    ]
    for copy in loads:
        copy.start()
    greet_all(n_row, n_seq)

    def y_copy(step):
        return remote(y_made.at[step], y_got.at[step], y_send.at[step], y_recv.at[step], peer_of(row, seq, step))

    def start_y(step, carry):
        y_copy(step).start()
        return carry

    lax.fori_loop(1, 8, start_y, 0)

    erows = held.shape[3]

    def expert_copy(kind, step):
        other = (me + step) % total
        return remote(
            expert_grads.at[kind, pl.ds(pl.multiple_of(other * erows, erows), erows)],
            held.at[kind, seq // 4, row * 4 + seq % 4],
            e_send.at[kind, step], e_recv.at[kind, step], (other // n_seq, other % n_seq),
        )

    expert_own = [
        pltpu.make_async_copy(
            expert_grads.at[kind, pl.ds(pl.multiple_of(me * erows, erows), erows)],
            held.at[kind, seq // 4, row * 4 + seq % 4], e_local.at[kind],
        )
        for kind in range(3)
    ]
    for copy in expert_own:
        copy.start()

    def start_experts(step, carry):
        for kind in range(3):
            expert_copy(kind, step).start()
        return carry

    lax.fori_loop(1, total, start_experts, 0)
    for copy in loads:
        copy.wait()

    def upright(value):
        return jnp.concatenate([value, jnp.zeros((128 - value.shape[0], tokens), full)], axis=0).T

    small = wall[:, 3072:].astype(full).T
    gain_one, gain_two = small[16:17], small[17:18]
    gates, dgates = upright(gates_in[...]), upright(dgates_in[...])
    dlogits = (gates * (dgates - jnp.sum(gates * dgates, axis=1, keepdims=True))).astype(low)
    dxtwo = dx_in[...] + mul(dlogits, wall[:, 3072:], NT)
    h = hidden_in[...]
    scale_two = norm_scale(h)
    weighted = gain_two * dxtwo
    dgain_two = jnp.sum(dxtwo * h * scale_two, axis=0, keepdims=True)
    input_out[...] = (
        g_in[...].astype(full)
        + scale_two * weighted
        - h * (scale_two * scale_two * scale_two) * jnp.mean(weighted * h, axis=1, keepdims=True)
    )
    dbranch = (RESIDUAL * input_out[...]).astype(low)
    drouter = mul(xtwo_in[...], dlogits, TN)
    for lo in range(0, width, 256):
        grads[lo:lo + 256, 2048:3072] = mul(dbranch[:, lo:lo + 256], mixed_in[...], TN).astype(low)

    half_lane = lax.broadcasted_iota(jnp.int32, (block, 128), 1) < 64
    for head in range(8):
        both = mul(dbranch, wall[:, 2048 + 128 * head:2176 + 128 * head], NN)
        for t in range(2):
            value = both[block * t:block * (t + 1)]
            other = pltpu.roll(value, 64, 1)
            if head % 2 == 0:
                first, second = jnp.where(half_lane, value, 0.0), jnp.where(half_lane, other, 0.0)
            else:
                first, second = jnp.where(half_lane, 0.0, other), jnp.where(half_lane, 0.0, value)
            outs[t * 8 + head, :block] = first.astype(low)
            outs[t * 8 + head, block:] = second.astype(low)

    lane = lax.broadcasted_iota(jnp.int32, (tokens, 128), 1)
    for t in range(2):
        visible = visibility(deep, seq, slots, block, start_in[block * t:block * (t + 1)])

        def attend(pair, carry):
            lanes = pl.ds(pl.multiple_of(128 * pair, 128), 128)
            value_lanes = pl.ds(pl.multiple_of(512 + 128 * pair, 128), 128)
            keys = jnp.concatenate([kv[slot, t, :, lanes] for slot in range(slots)], axis=0)
            values = jnp.concatenate([kv[slot, t, :, value_lanes] for slot in range(slots)], axis=0)
            dk, dv = 0.0, 0.0
            for half in range(2):
                head = 2 * pair + half
                query, dout = queries[t * 8 + head], outs[t * 8 + head]
                scores = jnp.where(visible, SCORE_SCALE * mul(query, keys, NT), NEGATIVE)
                total_log = jnp.sum(jnp.where(lane == head, lse_in[t], 0.0), axis=1, keepdims=True)
                probs = jnp.exp(scores - total_log)
                dprobs = mul(dout, values, NT)
                inner = jnp.sum(probs * dprobs, axis=1, keepdims=True)
                dscores = (probs * (dprobs - inner)).astype(low)
                dquery = SCORE_SCALE * mul(dscores, keys, NN)
                if half == 0:
                    joined = jnp.where(half_lane, dquery[:block], pltpu.roll(dquery[block:], 64, 1))
                else:
                    joined = jnp.where(half_lane, pltpu.roll(dquery[:block], 64, 1), dquery[block:])
                dq[block * t:block * (t + 1), pl.ds(pl.multiple_of(128 * head, 128), 128)] = joined
                dk += SCORE_SCALE * mul(dscores, query, TN)
                dv += mul(probs.astype(low), dout, TN)
            for slot in range(slots):
                kv[slot, t, :, lanes] = dk[block * slot:block * (slot + 1)].astype(low)
                kv[slot, t, :, value_lanes] = dv[block * slot:block * (slot + 1)].astype(low)

            @pl.when(core == 0)
            def _():
                dkv_own[t, :, lanes] = dk[:block]
                dkv_own[t, :, value_lanes] = dv[:block]

            @pl.when(core == 1)
            def _():
                dkv_own[t, :, lanes] = dk[block:2 * block]
                dkv_own[t, :, value_lanes] = dv[block:2 * block]

            return carry

        lax.fori_loop(0, 4, attend, 0)

    def kd_copy(hop):
        return remote(kv.at[hop * 2 + (1 - core)], dkv_core.at[hop], kd_send.at[hop], kd_recv.at[hop], sibling)

    def k_copy(hop):
        return remote(kv.at[hop * 2 + core], dkv_deep.at[hop], k_send.at[hop], k_recv.at[hop], (row, seq - 2 * hop))

    for hop in range(back, -1, -1):
        @pl.when(deep >= hop)
        def _():
            kd_copy(hop).start()

    for hop in range(back, 0, -1):
        @pl.when(deep >= hop)
        def _():
            kd_copy(hop).wait_recv()
            both = kv[hop * 2 + core].astype(full) + dkv_core[hop].astype(full)
            kv[hop * 2 + core] = both.astype(low)
            k_copy(hop).start()

    cosine, sine = cos_in[...], sin_in[...]

    def turn_back(value):
        return value * cosine - jnp.where(lane % 64 < 32, pltpu.roll(value, 96, 1), pltpu.roll(value, 32, 1)) * sine

    for head in range(8):
        lanes = slice(128 * head, 128 * (head + 1))
        dqkv[:, lanes] = turn_back(dq[:, lanes]).astype(low)
    for lo in range(0, width, 256):
        grads[lo:lo + 256, :1024] = mul(normed_in[:, lo:lo + 256], dqkv[:, :1024], TN).astype(low)

    kd_copy(0).wait_recv()
    dkv_own[...] += dkv_core[0].astype(full)
    for hop in range(1, back + 1):
        @pl.when(deep + hop < n_deep)
        def _():
            remote(kv.at[0], dkv_deep.at[hop], k_send.at[hop], k_recv.at[hop], sibling).wait_recv()
            dkv_own[...] += dkv_deep[hop].astype(full)

    for pair in range(4):
        lanes = slice(128 * pair, 128 * (pair + 1))
        value_lanes = slice(512 + 128 * pair, 640 + 128 * pair)
        dkey = jnp.concatenate([dkv_own[0, :, lanes], dkv_own[1, :, lanes]], axis=0)
        dqkv[:, 1024 + 128 * pair:1152 + 128 * pair] = turn_back(dkey).astype(low)
        dvalue = jnp.concatenate([dkv_own[0, :, value_lanes], dkv_own[1, :, value_lanes]], axis=0)
        dqkv[:, 1536 + 128 * pair:1664 + 128 * pair] = dvalue.astype(low)
    for lo in range(0, width, 256):
        grads[lo:lo + 256, 1024:2048] = mul(normed_in[:, lo:lo + 256], dqkv[:, 1024:], TN).astype(low)
    x = x_in[...].astype(full)
    scale_one = norm_scale(x)
    for lo in range(0, width, 256):
        dq[:, lo:lo + 256] = mul(dqkv[...], wall[lo:lo + 256, :2048], NT)
    dxone = dq[...]
    weighted = gain_one * dxone
    dgain_one = jnp.sum(dxone * x * scale_one, axis=0, keepdims=True)
    input_out[...] = (
        input_out[...]
        + scale_one * weighted
        - x * (scale_one * scale_one * scale_one) * jnp.mean(weighted * x, axis=1, keepdims=True)
    )
    wide = lax.broadcasted_iota(jnp.int32, (width, 128), 1)
    grads[:, 3072:] = jnp.where(
        wide == 16, column(dgain_one), jnp.where(wide == 17, column(dgain_two), drouter)
    ).astype(low)

    def part(of_row, of_deep, of_core):
        return pl.ds(pl.multiple_of((of_row * n_seq + of_deep * 2 + of_core) * rows, rows), rows)

    def d_copy(step, hop):
        there = part(row_of(row, step), (deep + hop) % n_deep, 1 - core)
        return remote(grads.at[there], from_core.at[hop, step], d_send.at[hop, step], d_recv.at[hop, step], sibling)

    def p_copy(step, hop):
        there = part(row_of(row, step), (deep + hop) % n_deep, core)
        return remote(grads.at[there], from_plane.at[hop, step - 1], p_send.at[hop, step], p_recv.at[hop, step],
                      (row_of(row, step), seq))

    def z_copy(hop):
        there = part(row, (deep + hop) % n_deep, core)
        return remote(grads.at[there], from_deep.at[hop], z_send.at[hop], z_recv.at[hop],
                      (row, (deep + hop) % n_deep * 2 + core))

    def start_d(index, carry):
        d_copy(3 - index % 4, n_deep - 1 - index // 4).start()
        return carry

    lax.fori_loop(0, 4 * n_deep, start_d, 0)

    def sum_cores(index, carry):
        step, hop = 3 - index % 4, n_deep - 1 - index // 4
        d_copy(step, hop).wait_recv()
        there = part(row_of(row, step), (deep + hop) % n_deep, core)
        grads[there] = (grads[there].astype(full) + from_core[hop, step].astype(full)).astype(low)

        @pl.when(step > 0)
        def _():
            p_copy(step, hop).start()

        return carry

    lax.fori_loop(0, 4 * n_deep, sum_cores, 0)

    def sum_plane(index, carry):
        hop = n_deep - 1 - index
        there = part(row, (deep + hop) % n_deep, core)
        for step in range(1, 4):
            p_copy(step, hop).wait_recv()
        value = grads[there].astype(full)
        for step in range(1, 4):
            value += from_plane[hop, step - 1].astype(full)
        grads[there] = value.astype(low)

        @pl.when(hop > 0)
        def _():
            z_copy(hop).start()

        return carry

    lax.fori_loop(0, n_deep, sum_plane, 0)

    def settle_y(step, carry):
        y_copy(step).wait()
        return carry

    lax.fori_loop(1, 8, settle_y, 0)
    total_grad = grads[part(row, deep, core)].astype(full)
    for hop in range(1, n_deep):
        z_copy(hop).wait_recv()
        total_grad += from_deep[hop].astype(full)
    q_out[...] = total_grad[:, :1024]
    k_out[...] = total_grad[:, 1024:1536]
    v_out[...] = total_grad[:, 1536:2048]
    o_out[...] = total_grad[:, 2048:3072]
    small_out[...] = total_grad[:, 3072:]

    def settle_d(index, carry):
        hop, step = index // 4, index % 4
        d_copy(step, hop).wait_send()

        @pl.when(step > 0)
        def _():
            p_copy(step, hop).wait_send()

        return carry

    lax.fori_loop(0, 4 * n_deep, settle_d, 0)

    def settle_z(hop, carry):
        z_copy(hop).wait_send()
        return carry

    lax.fori_loop(1, n_deep, settle_z, 0)
    for hop in range(back + 1):
        @pl.when(deep >= hop)
        def _():
            kd_copy(hop).wait_send()
            if hop > 0:
                k_copy(hop).wait_send()

    for copy in expert_own:
        copy.wait()

    def settle_experts(step, carry):
        other = (me + total - step) % total
        for kind in range(3):
            expert_copy(kind, step).wait_send()
            there = held.at[kind, other % n_seq // 4, other // n_seq * 4 + other % 4]
            remote(there, there, e_send.at[kind, step], e_recv.at[kind, step], sibling).wait_recv()
        return carry

    lax.fori_loop(1, total, settle_experts, 0)


def window_of(length, block, n_deep):
    return min((length // 2 + 2 * block - 1) // (2 * block), n_deep - 1)


def run_backward(n_row, n_seq, length, dense, kv, queries, normed, mixed, x, g, cosine, sine, start,
                 hidden, xtwo, gates, dgates, dx, lse, y_made, expert_grads):
    tokens, width = x.shape
    total, n_deep = n_row * n_seq, n_seq // 2
    rows, block = width // total, tokens // 2
    back = window_of(length, block, n_deep)
    slots, columns = kv.shape[0], dense.shape[1]
    low, full = jnp.bfloat16, jnp.float32
    dma, shape = pltpu.SemaphoreType.DMA, jax.ShapeDtypeStruct
    ff = expert_grads.shape[2]
    return pl.pallas_call(
        functools.partial(backward_kernel, n_row, n_seq, back),
        out_shape=(
            shape((8, tokens, width), low),
            shape((tokens, width), full),
            shape((rows, 1024), full),
            shape((rows, 512), full),
            shape((rows, 512), full),
            shape((rows, 1024), full),
            shape((rows, 128), full),
            shape((3, n_seq // 4, n_row * 4, rows, ff), low),
        ),
        in_specs=[ANY] * 3 + [VMEM] * 13 + [ANY] * 2,
        out_specs=(ANY,) + (VMEM,) * 6 + (ANY,),
        scratch_shapes=[
            pltpu.VMEM((width, columns), low),
            pltpu.VMEM(kv.shape, low),
            pltpu.VMEM((16, tokens, 128), low),
            pltpu.VMEM((16, tokens, 128), low),
            pltpu.VMEM((tokens, 1024), full),
            pltpu.VMEM((tokens, 2048), low),
            pltpu.VMEM(kv.shape[1:], full),
            pltpu.VMEM((back + 1,) + kv.shape[1:], low),
            pltpu.VMEM((back + 1,) + kv.shape[1:], low),
            pltpu.VMEM((width, columns), low),
            pltpu.VMEM((n_deep, 4, rows, columns), low),
            pltpu.VMEM((n_deep, 3, rows, columns), low),
            pltpu.VMEM((n_deep, rows, columns), low),
            dma((3,)),
            dma((back + 1,)), dma((back + 1,)), dma((back + 1,)), dma((back + 1,)),
            dma((8,)), dma((8,)),
            dma((3, total)), dma((3, total)), dma((3,)),
            dma((n_deep, 4)), dma((n_deep, 4)), dma((n_deep, 4)), dma((n_deep, 4)),
            dma((n_deep,)), dma((n_deep,)),
        ],
        compiler_params=pltpu.CompilerParams(
            collective_id=2, has_side_effects=True, vmem_limit_bytes=62 << 20
        ),
        name="backward",
    )(dense, kv, queries, normed, mixed, x, g, cosine, sine, start, hidden, xtwo, gates, dgates, dx, lse,
      y_made, expert_grads)


def body(
    n_row,
    n_seq,
    tokens,
    segment_ids,
    expert_ids,
    norm1_gain,
    w_query,
    w_key,
    w_value,
    w_out,
    norm2_gain,
    w_router,
    w_gate,
    w_up,
    w_down,
    out_grad,
):
    row_count, block_len, width = tokens.shape
    token_count = row_count * block_len
    length = segment_ids.shape[1]
    rows = w_query.shape[0]
    first = lax.axis_index("seq") * block_len
    low, full = jnp.bfloat16, jnp.float32

    routes = expert_ids.reshape(token_count, TOPK)
    picks = jnp.sum(
        (routes[:, :, None] == jnp.arange(128, dtype=jnp.int32)[None, None, :]).astype(full), axis=1
    )
    counts = jnp.concatenate([jnp.sum(picks, axis=0)[None, :EXPERTS], jnp.zeros((rows - 1, EXPERTS), full)])
    packed = jnp.concatenate(
        [w_query, w_key, w_value, w_out.T, w_router, norm1_gain[:, None], norm2_gain[:, None],
         jnp.zeros((rows, 14), low), counts.astype(low), jnp.zeros((rows, 80), low)],
        axis=1,
    )
    local_segments = lax.dynamic_slice_in_dim(segment_ids, first, block_len, axis=1)
    start = jnp.sum(
        (segment_ids[:, None, :] < local_segments[:, :, None]).astype(jnp.int32), axis=2
    ).reshape(token_count)
    positions = jnp.tile(first + jnp.arange(block_len, dtype=jnp.int32), row_count) - start
    cosine, sine = rope_tables(positions, HEAD)
    cosine = jnp.concatenate([cosine, cosine], axis=1)
    sine = jnp.concatenate([-sine[:, :32], sine[:, 32:]] * 2, axis=1)
    start = jnp.broadcast_to(start[:, None], (token_count, 128))

    x = tokens.reshape(token_count, width)
    g = out_grad.reshape(token_count, width)
    (xtwo, gates, count_rows, hidden, mixed, lse, normed, queries, kv, dense, group_g, expert_weights) = run_forward(
        n_row, n_seq, length, packed, x, g, cosine, sine, start, picks, w_gate, w_up, jnp.swapaxes(w_down, 1, 2)
    )
    expert_counts = count_rows[0, 32:32 + EXPERTS].astype(jnp.int32)
    y_made, dx, dgates, expert_grads = run_experts(n_row, n_seq, xtwo, gates, group_g, expert_weights)
    y_got, input_grad, dq, dk, dv, do, small, held = run_backward(
        n_row, n_seq, length, dense, kv, queries, normed, mixed, x, g, cosine, sine, start,
        hidden, xtwo, gates, dgates, dx, lse, y_made, expert_grads,
    )
    mixture = y_made[0].astype(full) + jnp.sum(y_got[1:].astype(full), axis=0)
    layer_out = (hidden + RESIDUAL * mixture).astype(low)
    grads = jnp.sum(held.astype(full), axis=1)
    return (
        layer_out.reshape(row_count, block_len, width),
        input_grad.reshape(row_count, block_len, width),
        small[:, 16],
        dq,
        dk,
        dv,
        do.T,
        small[:, 17],
        small[:, :EXPERTS],
        grads[0],
        grads[1],
        jnp.swapaxes(grads[2], 1, 2),
        expert_counts,
    )


def solution(mesh):
    in_specs = (
        P("row", "seq", None),
        P("row", None),
        P("seq", "row", None, None),
        P(("row", "seq")),
        P(("row", "seq"), None),
        P(("row", "seq"), None),
        P(("row", "seq"), None),
        P(None, ("row", "seq")),
        P(("row", "seq")),
        P(("row", "seq"), None),
        P(None, ("row", "seq"), None),
        P(None, ("row", "seq"), None),
        P(None, None, ("row", "seq")),
        P("row", "seq", None),
    )
    out_specs = (
        P("row", "seq", None),
        P("row", "seq", None),
        P(("row", "seq")),
        P(("row", "seq"), None),
        P(("row", "seq"), None),
        P(("row", "seq"), None),
        P(None, ("row", "seq")),
        P(("row", "seq")),
        P(("row", "seq"), None),
        P(None, ("row", "seq"), None),
        P(None, ("row", "seq"), None),
        P(None, None, ("row", "seq")),
        P(),
    )
    return jax.shard_map(
        functools.partial(body, mesh.shape["row"], mesh.shape["seq"]),
        mesh=mesh,
        in_specs=in_specs,
        out_specs=out_specs,
        check_vma=False,
    )
```

time: 1460 us -> 503 us (0.34)
  waiting for transfers between devices: 726 us -> 0 us
  blocking collectives: 158 us -> 0 us
  Pallas kernels: 403 us -> 471 us
  matrix products: 58.4 us -> 0 us
  local copies, waits for them, and re-layouts: 71.3 us -> 12.9 us
  other arithmetic: 26.8 us -> 10.8 us
    reduce_scatter x6 -> x0, waiting for transfers between devices: 594 us -> none  [the longest x1 142 us: body(): lax.psum_scatter(delta_out_weight, ('row', 'seq'), scatter_dimension=1, t...]
    all_gather x6 -> x0, waiting for transfers between devices: 117 us -> none  [the longest x1 52.5 us: body(): lax.all_gather(w_value, ('row', 'seq'), axis=0, tiled=True)]
    unnamed x2 -> x0, blocking collectives: 79.6 us -> none
    pallas_call x3, Pallas kernels: 403 us -> 471 us  [the longest x1 182 us: run_backward(): pl.pallas_call(functools.partial(backward_kernel, n_row, n_seq, back), ou...]
    dot_general x28 -> x0, matrix products: 57.3 us -> none  [the longest x2 13.5 us: attend_backward(): jnp.einsum('kgcl,ckgd->lkd', probs.astype(jnp.bfloat16), delta_row, prefe...]
    all_gather x1 -> x0, blocking collectives: 40.2 us -> none  [body(): lax.all_gather(w_router, ('row', 'seq'), axis=0, tiled=True)]
    psum x1 -> x0, blocking collectives: 37.9 us -> none  [body(): expert_counts = lax.psum(jnp.sum(picks, axis=0), ('row', 'seq'))]
    dynamic_update_slice x12 -> x0, local copies, waits for them, and re-layouts: 18.6 us -> none  [the longest x8 18.3 us: body(): lax.scan(attend_backward, None, (query, key_rows, value_rows, segment_ids...]
  transfers between devices with their start and end apart: 13 -> 0, of which waited for: 11 -> 0; matrix products, arithmetic and copies ran while one was open for 5% -> 0% of each run, Pallas kernels for 12% -> 0%
where the time goes in v2:
time: 503 us; the launch traced here: 496 us
  Pallas kernels  471 us (94%)
  local copies, waits for them, and re-layouts  12.9 us (3%)
  other arithmetic  10.8 us (2%)
    pallas_call x1, Pallas kernels, run_backward(): pl.pallas_call(functools.partial(backward_kernel, n_row, n_seq, back), ou...  182 us
    pallas_call x1, Pallas kernels, run_forward(): pl.pallas_call(functools.partial(forward_kernel, n_row, n_seq, back), out...  170 us
    pallas_call x1, Pallas kernels, run_experts(): pl.pallas_call(functools.partial(experts_kernel, n_seq), out_shape=(shape...  119 us

profile of v2, /device:TPU:0, one launch (start us, length us, event | category | flops | bytes accessed | tf_op | source)
XLA Modules:
  0.0 496.0 jit_solution(9588743187393353333)
XLA Ops:
  0.7 0.7 constant_dynamic-slice_fusion
  1.3 0.9 convert_reduce_fusion.4
  2.3 0.8 copy.38
  3.1 0.8 copy.39
  3.8 0.8 copy.37
  4.6 0.1 broadcast_multiply_fusion
  4.7 0.8 broadcast_in_dim.32.start_in
  5.5 0.8 copy.36
  6.3 1.1 convert_reduce_fusion.2
  7.4 0.5 fusion.3
  7.9 0.1 slice_negate_fusion
  8.0 0.9 pad_maximum_fusion.1
  8.9 1.7 concatenate.16.packed
  10.6 170.2 %forward.1 = (bf16[256,1024]{1,0:T(8,128)(2,1)}, f32[16,256]{1,0:T(8,128)}, f32[8,128]{1,0:T(8,128)}, f32[256,1024]{1,0:T(8,128)}, bf16[256,1024]{1,0:T(8,128)(2...) custom-call(bf16[32,3200]{1,0:T(8,128)(2,1)} %concatenate.16.packed,, ...), custom_call_target="tpu_custom_call" | custom-call | tf_op jit(solution)/shard_map/forward/pallas_call | solution.py:399
  180.8 119.4 %experts.1 = (bf16[8,256,1024]{2,1,0:T(8,128)(2,1)}, f32[256,1024]{1,0:T(8,128)}, f32[16,256]{1,0:T(8,128)}, bf16[3,1024,512]{2,1,0:T(8,128)(2,1)}) custom-call(bf16[256,1024]{1,0:T(8,128)(2,1)} %get-tuple-element.38.x_in.xtwo_in, f32[16,256]{1,0:T(8,128)} %get-tuple-element.39.gates_in, bf16[8,256,1024]{2,1,0:T(8,128)(2,1)} %get-tuple-element.40.g_in, ...), custom_call_target="tpu_custom_call" | custom-call | tf_op jit(solution)/shard_map/experts/pallas_call | solution.py:587
  300.2 181.9 %backward.1 = (bf16[8,256,1024]{2,1,0:T(8,128)(2,1)}, f32[256,1024]{1,0:T(8,128)}, f32[32,1024]{1,0:T(8,128)}, f32[32,512]{1,0:T(8,128)}, f32[32,512]{1,0:T(8,12...) custom-call(bf16[1024,3200]{1,0:T(8,128)(2,1)} %get-tuple-element.43.dense, ...), custom_call_target="tpu_custom_call" | custom-call | tf_op jit(solution)/shard_map/backward/pallas_call | solution.py:958
  482.0 0.0 copy-start
  482.0 0.0 copy-start.3
  482.1 0.0 copy-start.1
  482.1 3.0 convert_reduce_fusion
  485.1 0.0 copy-done
  485.1 2.1 fusion.2
  487.2 1.3 convert_bitcast_fusion
  488.5 0.0 copy-done.3
  488.5 0.7 slice_reduce_fusion
  489.2 0.7 copy.40
  489.9 0.0 copy-done.1
  489.9 0.7 convert_reduce_fusion.1
  490.6 0.0 copy-start.2
  490.6 0.0 copy-start.5
  490.6 0.0 copy-start.7
  490.6 0.0 copy-start.6
  490.7 0.0 copy-start.4
  490.7 1.8 slice_bitcast_fusion
  492.4 0.0 copy-done.2
  492.4 1.0 copy.46
  493.4 0.0 copy-done.5
  493.4 0.7 copy.47
  494.1 0.0 copy-done.7
  494.1 0.6 copy.48
  494.7 0.0 copy-done.6
  494.7 0.6 copy.49
  495.3 0.0 copy-done.4
  495.3 0.7 copy.50
  (7 shorter events, 0.0 us)
Async XLA Ops:
  482.0 3.1 copy-start
  482.0 6.5 %copy-start.3 = (f32[32,128]{1,0:T(8,128)S(1)}, f32[32,128]{1,0:T(8,128)}, u32[]{:S(2)}) copy-start(f32[32,128]{1,0:T(8,128)} %get-tuple-element.54) | copy-start | bytes 49156
  482.1 7.8 %copy-start.1 = (bf16[3,2,16,32,512]{4,3,2,1,0:T(8,128)(2,1)S(1)}, bf16[3,2,16,32,512]{4,3,2,1,0:T(8,128)(2,1)}, u32[]{:S(2)}) copy-start(bf16[3,2,16,32,512]{4,3,2,1,0:T(8,128)(2,1)} %get-tuple-element.59) | copy-start | bytes 9437188
  490.6 1.8 copy-start.2
  490.6 2.8 copy-start.5
  490.6 3.4 copy-start.7
  490.6 4.0 copy-start.6
  490.7 4.7 copy-start.4

commit v3 on v2

v3 whole, which is shorter than its diff:
```python
import functools

import jax
import jax.numpy as jnp
from jax import lax
from jax.experimental import pallas as pl
from jax.experimental.pallas import tpu as pltpu
from jax.sharding import PartitionSpec as P

HEAD = 64
EXPERTS = 16
TOPK = 8

EPSILON = 1e-06
SCORE_SCALE = 0.015625
RESIDUAL = 0.22
THETA = 10000.0
NEGATIVE = -1e30

MESH = pl.DeviceIdType.MESH
STRIDE = 11
ANY = pl.BlockSpec(memory_space=pl.ANY)
VMEM = pl.BlockSpec(memory_space=pltpu.VMEM)


def norm_scale(value):
    return lax.rsqrt(jnp.mean(value * value, axis=-1, keepdims=True) + EPSILON)


def rope_tables(positions, width):
    half = width // 2
    frequency = THETA ** (-2.0 * jnp.arange(half, dtype=jnp.float32) / width)
    angle = positions.astype(jnp.float32)[..., None] * frequency
    angle = jnp.concatenate([angle, angle], axis=-1)
    return (jnp.cos(angle), jnp.sin(angle))


def greet_all(n_row, n_seq):
    row, seq = lax.axis_index("row"), lax.axis_index("seq")
    me, total = row * n_seq + seq, n_row * n_seq
    barrier = pltpu.get_barrier_semaphore()

    def greet(step, carry):
        other = (me + step) % total
        pl.semaphore_signal(
            barrier, inc=1, device_id=(other // n_seq, other % n_seq), device_id_type=MESH
        )
        return carry

    lax.fori_loop(1, total, greet, 0)
    pl.semaphore_wait(barrier, total - 1)


NN = (((1,), (0,)), ((), ()))
NT = (((1,), (1,)), ((), ()))
TN = (((0,), (0,)), ((), ()))


def mul(a, b, dims):
    return lax.dot_general(a, b, dims, preferred_element_type=jnp.float32)


def column(row_values):
    return jnp.broadcast_to(row_values, (128, row_values.shape[1])).T


def peer_of(row, seq, step):
    other_row = (row // 2 + step // 4) % 2 * 2 + (row % 2 + step // 2 % 2) % 2
    other_seq = seq // 4 * 4 + (seq // 2 % 2 + step % 2) % 2 * 2 + seq % 2
    return (other_row, other_seq)


def row_of(row, step):
    return (row // 2 + step // 2) % 2 * 2 + (row % 2 + step % 2) % 2


def remote(source, target, send, recv, device):
    return pltpu.make_async_remote_copy(
        src_ref=source, dst_ref=target, send_sem=send, recv_sem=recv, device_id=device,
        device_id_type=MESH,
    )


def thirds_of(rows):
    cut = rows * 3 // 8
    rest = (rows - cut) // 2
    return ((0, cut), (cut, rest), (cut + rest, rest))


def tree_rounds(row, seq, own, slots, send, recv):
    thirds = thirds_of(own.shape[0])

    def hop(source, slot, toward, index):
        return remote(source, slot, send.at[index], recv.at[index], peer_of(row, seq, toward))

    def piece(slot, third):
        return slots.at[slot, pl.ds(*thirds[third])]

    first = lambda i: hop(own, slots.at[(1, 2, 4)[i]], (1, 2, 4)[i], i)
    second = lambda i: hop(slots.at[(2, 4, 1)[i]], slots.at[(3, 6, 5)[i]], (1, 2, 4)[i], 3 + i)
    third = lambda i: hop(piece((6, 5, 3)[i], i), piece(7, i), (1, 2, 4)[i], 6 + i)

    def start(make):
        for i in range(3):
            make(i).start()

    def landed(make):
        for i in range(3):
            make(i).wait_recv()

    def round_one():
        start(first)

    def round_two():
        landed(first)
        start(second)

    def round_three():
        landed(second)
        start(third)

    def last():
        landed(third)

    def sent():
        for make in (first, second, third):
            for i in range(3):
                make(i).wait_send()

    return round_one, round_two, round_three, last, sent


def forward_kernel(
    n_row, n_seq, back,
    pack_kv, pack_qo, x_in, g_in, cos_in, sin_in, start_in, picks_in, gate, up, down,
    xtwo_out, gates_out, counts_out, hidden_out, mixed_out, lse_out, normed_out, queries_out, kv_out,
    w_kv_out, w_qo_out, g_out, xs_out, gates_all, held,
    w_kv, w_qo, kv, queries, normed, mixed, hidden, lse,
    z_send, z_recv, p_send, p_recv, d_send, d_recv, kv_send, kv_recv, kvd_send, kvd_recv,
    g_send, g_recv, x_send, x_recv, gate_send, gate_recv, group_local, e_send, e_recv, e_local, pass_send, pass_recv, local, store,
):
    row, seq = lax.axis_index("row"), lax.axis_index("seq")
    core, deep, n_deep = seq % 2, seq // 2, n_seq // 2
    me, total = row * n_seq + seq, n_row * n_seq
    sibling = (row, deep * 2 + (1 - core))
    rows = pack_kv.shape[0]
    tokens, width = x_in.shape
    block = tokens // 2
    low, full = jnp.bfloat16, jnp.float32
    slots = kv.shape[0]
    packs, walls = (pack_kv, pack_qo), (w_kv, w_qo)
    greet_all(n_row, n_seq)

    def part(kind, of_row, of_deep, of_core):
        start = (of_row * n_seq + of_deep * 2 + of_core) * rows
        return walls[kind].at[pl.ds(pl.multiple_of(start, rows), rows)]

    own_copies = [
        pltpu.make_async_copy(packs[kind], part(kind, row, deep, core), local.at[kind]) for kind in range(2)
    ]
    for copy in own_copies:
        copy.start()

    def z_copy(kind, step):
        return remote(packs[kind], part(kind, row, deep, core), z_send.at[kind, step], z_recv.at[kind, step],
                      (row, (deep + step) % n_deep * 2 + core))

    def plane_copy(kind, step, hop, source):
        here = part(kind, row, (deep + n_deep - hop) % n_deep, core)
        return remote(here if source is None else source, here, p_send.at[kind, hop, step], p_recv.at[kind, hop, step],
                      (row_of(row, step), seq))

    def core_copy(kind, step, hop, source):
        here = part(kind, row_of(row, step), (deep + n_deep - hop) % n_deep, core)
        return remote(here if source is None else source, here, d_send.at[kind, hop, step], d_recv.at[kind, hop, step],
                      sibling)

    def dense_start(kind):
        def start_z(step, carry):
            z_copy(kind, step).start()
            return carry

        lax.fori_loop(1, n_deep, start_z, 0)
        for step in range(1, 4):
            plane_copy(kind, step, 0, packs[kind]).start()
        core_copy(kind, 0, 0, packs[kind]).start()

    def dense_relay(kind):
        def relay(hop, carry):
            there = part(kind, row, (deep + n_deep - hop) % n_deep, core)
            remote(there, there, z_send.at[kind, hop], z_recv.at[kind, hop], sibling).wait_recv()
            for step in range(1, 4):
                plane_copy(kind, step, hop, None).start()
            core_copy(kind, 0, hop, None).start()
            return carry

        lax.fori_loop(1, n_deep, relay, 0)

    def dense_finish(kind):
        def spread(index, carry):
            hop, step = index // 3, index % 3 + 1
            there = part(kind, row_of(row, step), (deep + n_deep - hop) % n_deep, core)
            remote(there, there, p_send.at[kind, hop, step], p_recv.at[kind, hop, step], sibling).wait_recv()
            core_copy(kind, step, hop, None).start()
            return carry

        lax.fori_loop(0, n_deep * 3, spread, 0)
        own_copies[kind].wait()

        def gathered(index, carry):
            hop, step = index // 4, index % 4
            there = part(kind, row_of(row, step), (deep + n_deep - hop) % n_deep, 1 - core)
            remote(there, there, d_send.at[kind, hop, step], d_recv.at[kind, hop, step], sibling).wait_recv()
            return carry

        lax.fori_loop(0, n_deep * 4, gathered, 0)

    def expert_copy(kind, source, step):
        other = (me + step) % total
        other_row, other_seq = other // n_seq, other % n_seq
        return remote(
            source.at[other_row * 4 + other_seq % 4],
            held.at[other_seq % 2, kind, pl.ds(pl.multiple_of(me * rows, rows), rows)],
            e_send.at[kind, step], e_recv.at[kind, step], (other_row, other_seq),
        )

    sources = (gate, up, down)
    expert_own = [
        pltpu.make_async_copy(
            source.at[row * 4 + seq % 4],
            held.at[core, kind, pl.ds(pl.multiple_of(me * rows, rows), rows)],
            e_local.at[kind],
        )
        for kind, source in enumerate(sources)
    ]

    def experts_start(*kinds):
        def start_experts(index, carry):
            for kind in kinds:
                expert_copy(kind, sources[kind], index * STRIDE % total).start()
            return carry

        lax.fori_loop(1, total, start_experts, 0)

    g_one, g_two, g_three, g_last, g_sent = tree_rounds(row, seq, g_in, g_out, g_send, g_recv)
    g_own = pltpu.make_async_copy(g_in, g_out.at[0], group_local.at[0])

    dense_start(0)
    dense_start(1)
    for copy in expert_own:
        copy.start()
    g_own.start()
    experts_start(0, 1, 2)
    x = x_in[...].astype(full)
    scale_one = norm_scale(x)
    dense_relay(0)
    dense_finish(0)
    small = w_kv[:, 1024:].astype(full)
    counts_out[...] = jnp.broadcast_to(jnp.sum(small, axis=0, keepdims=True), (8, 128))
    small = small.T
    gain_one, gain_two = small[16:17], small[17:18]
    normed[...] = (x * scale_one * gain_one).astype(low)

    lane = lax.broadcasted_iota(jnp.int32, (tokens, 128), 1)
    cosine, sine = cos_in[...], sin_in[...]

    def turn(value):
        return value * cosine + jnp.where(lane % 64 < 32, pltpu.roll(value, 96, 1), pltpu.roll(value, 32, 1)) * sine

    for pair in range(4):
        lanes = slice(128 * pair, 128 * (pair + 1))
        value_lanes = slice(512 + 128 * pair, 640 + 128 * pair)
        key = turn(mul(normed[...], w_kv[:, lanes], NN)).astype(low)
        value = mul(normed[...], w_kv[:, value_lanes], NN).astype(low)
        for t in range(2):
            here = slice(block * t, block * (t + 1))
            kv[core, t, :, lanes] = key[here]
            kv[core, t, :, value_lanes] = value[here]

    def kv_copy(hop):
        return remote(kv.at[(hop - 1) * 2 + core], kv.at[hop * 2 + core], kv_send.at[hop], kv_recv.at[hop],
                      (row, seq + 2))

    def kv_pass(hop, of_core):
        there = kv.at[hop * 2 + of_core]
        return remote(there, there, kvd_send.at[hop], kvd_recv.at[hop], sibling)

    @pl.when(deep + 1 < n_deep)
    def _():
        kv_copy(1).start()

    for hop in range(1, back + 1):
        @pl.when(deep < hop)
        def _():
            kv[2 * hop] = jnp.zeros(kv.shape[1:], low)
            kv[2 * hop + 1] = jnp.zeros(kv.shape[1:], low)

    kv_pass(0, core).start()
    dense_relay(1)
    g_one()
    dense_finish(1)
    half_lane = lax.broadcasted_iota(jnp.int32, (block, 128), 1) < 64
    for head in range(8):
        both = turn(mul(normed[...], w_qo[:, 128 * head:128 * (head + 1)], NN))
        for t in range(2):
            value = both[block * t:block * (t + 1)]
            other = pltpu.roll(value, 64, 1)
            if head % 2 == 0:
                first, second = jnp.where(half_lane, value, 0.0), jnp.where(half_lane, other, 0.0)
            else:
                first, second = jnp.where(half_lane, 0.0, other), jnp.where(half_lane, 0.0, value)
            queries[t * 8 + head, :block] = first.astype(low)
            queries[t * 8 + head, block:] = second.astype(low)

    for hop in range(1, back + 1):
        @pl.when(deep >= hop)
        def _():
            kv_copy(hop).wait_recv()
            if hop < back:
                @pl.when(deep + 1 < n_deep)
                def _():
                    kv_copy(hop + 1).start()

            kv_pass(hop, core).start()


    kv_pass(0, 1 - core).wait_recv()
    for hop in range(1, back + 1):
        @pl.when(deep >= hop)
        def _():
            kv_pass(hop, 1 - core).wait_recv()

    g_two()
    for t in range(2):
        visible = visibility(deep, seq, slots, block, start_in[block * t:block * (t + 1)])

        def attend(pair, carry):
            lanes = pl.ds(pl.multiple_of(128 * pair, 128), 128)
            value_lanes = pl.ds(pl.multiple_of(512 + 128 * pair, 128), 128)
            values = jnp.concatenate([kv[slot, t, :, value_lanes] for slot in range(slots)], axis=0)
            for half in range(2):
                head = 2 * pair + half
                query = queries[t * 8 + head]
                scores = jnp.concatenate(
                    [mul(query, kv[slot, t, :, lanes], NT) for slot in range(slots)], axis=1
                )
                scores = jnp.where(visible, SCORE_SCALE * scores, NEGATIVE)
                peak = jnp.max(scores, axis=1, keepdims=True)
                raised = jnp.exp(scores - peak)
                denominator = jnp.sum(raised, axis=1, keepdims=True)
                probs = (raised / denominator).astype(low)
                out = mul(probs, values, NN)
                if half == 0:
                    joined = jnp.where(half_lane, out[:block], pltpu.roll(out[block:], 64, 1))
                else:
                    joined = jnp.where(half_lane, pltpu.roll(out[:block], 64, 1), out[block:])
                mixed[block * t:block * (t + 1), pl.ds(pl.multiple_of(128 * head, 128), 128)] = joined.astype(low)
                lse[t] = jnp.where(lane == head, peak + jnp.log(denominator), lse[t])
            return carry

        lax.fori_loop(0, 4, attend, 0)

    g_three()
    for lo in range(0, width, 256):
        branch = mul(mixed[...], w_qo[lo:lo + 256, 1024:], NT)
        hidden[:, lo:lo + 256] = x_in[:, lo:lo + 256].astype(full) + RESIDUAL * branch
    scale_two = norm_scale(hidden[...])
    xtwo_out[...] = (hidden[...] * scale_two * gain_two).astype(low)
    x_one, x_two, x_three, x_last, x_sent = tree_rounds(row, seq, xtwo_out, xs_out, x_send, x_recv)
    x_one()
    logits = mul(xtwo_out[...], w_kv[:, 1024:], NN)
    picked = picks_in[...] > 0
    logits = jnp.where(picked, logits, NEGATIVE)
    raised = jnp.where(picked, jnp.exp(logits - jnp.max(logits, axis=1, keepdims=True)), 0.0)
    gates = raised / jnp.sum(raised, axis=1, keepdims=True)
    gates_out[...] = gates.T[:EXPERTS]

    def gate_copy(step):
        return remote(gates_out, gates_all.at[step], gate_send.at[step], gate_recv.at[step], peer_of(row, seq, step))

    def send_gates(step, carry):
        gate_copy(step).start()
        return carry

    lax.fori_loop(1, 8, send_gates, 0)
    group_own = [
        g_own,
        pltpu.make_async_copy(xtwo_out, xs_out.at[0], group_local.at[1]),
        pltpu.make_async_copy(gates_out, gates_all.at[0], group_local.at[2]),
    ]
    for copy in group_own[1:]:
        copy.start()

    stores = [
        pltpu.make_async_copy(source, target, store.at[i])
        for i, (source, target) in enumerate((
            (w_kv, w_kv_out), (w_qo, w_qo_out), (kv, kv_out), (queries, queries_out), (normed, normed_out),
            (mixed, mixed_out), (hidden, hidden_out), (lse, lse_out),
        ))
    ]
    for copy in stores:
        copy.start()

    x_two()
    x_three()

    def arrived(step, carry):
        other = (me + total - step) % total
        for kind in range(3):
            there = held.at[core, kind, pl.ds(pl.multiple_of(other * rows, rows), rows)]
            remote(there, there, e_send.at[kind, step], e_recv.at[kind, step], sibling).wait_recv()
        return carry

    lax.fori_loop(1, total, arrived, 0)
    for copy in expert_own:
        copy.wait()
    remote(held.at[core], held.at[core], pass_send, pass_recv, sibling).start()

    def settle_experts(step, carry):
        for kind, source in enumerate(sources):
            expert_copy(kind, source, step).wait_send()
        return carry

    lax.fori_loop(1, total, settle_experts, 0)
    g_last()
    g_sent()
    x_last()
    x_sent()
    for copy in group_own:
        copy.wait()

    def settle_gates(step, carry):
        gate_copy(step).wait()
        return carry

    lax.fori_loop(1, 8, settle_gates, 0)
    for kind in range(2):
        def settle_z(step, carry):
            z_copy(kind, step).wait_send()
            return carry

        lax.fori_loop(1, n_deep, settle_z, 0)

        def settle_plane(index, carry):
            hop, step = index // 4, index % 4
            core_copy(kind, step, hop, None).wait_send()

            @pl.when(step > 0)
            def _():
                plane_copy(kind, step, hop, None).wait_send()

            return carry

        lax.fori_loop(0, n_deep * 4, settle_plane, 0)

    kv_pass(0, core).wait_send()
    for hop in range(1, back + 1):
        @pl.when((deep + 1 < n_deep) & (deep >= hop - 1))
        def _():
            kv_copy(hop).wait_send()

        @pl.when(deep >= hop)
        def _():
            kv_pass(hop, core).wait_send()

    for copy in stores:
        copy.wait()
    share = remote(held.at[core], held.at[1 - core], pass_send, pass_recv, sibling)
    share.wait_recv()
    remote(held.at[core], held.at[core], pass_send, pass_recv, sibling).wait_send()


def visibility(deep, seq, slots, block, start):
    key = lax.broadcasted_iota(jnp.int32, (block, block), 1)
    query = lax.broadcasted_iota(jnp.int32, (block, block), 0) + seq * block
    tiles = []
    for slot in range(slots):
        position = key + ((deep - slot // 2) * 2 + slot % 2) * block
        seen = jnp.where((position >= start) & (position <= query), 1.0, 0.0)
        tiles.append(jnp.concatenate([seen, seen], axis=0))
    return jnp.concatenate(tiles, axis=1) > 0.5


def run_forward(n_row, n_seq, length, pack_kv, pack_qo, x, g, cosine, sine, start, picks, gate, up, down):
    tokens, width = x.shape
    experts, rows, hidden = gate.shape
    total, n_deep = n_row * n_seq, n_seq // 2
    block = tokens // 2
    back = window_of(length, block, n_deep)
    slots = 2 * (back + 1)
    low, full = jnp.bfloat16, jnp.float32
    dma = pltpu.SemaphoreType.DMA
    kv = (slots, 2, block, 1024)
    shape = jax.ShapeDtypeStruct
    return pl.pallas_call(
        functools.partial(forward_kernel, n_row, n_seq, back),
        out_shape=(
            shape((tokens, width), low),
            shape((EXPERTS, tokens), full),
            shape((8, 128), full),
            shape((tokens, width), full),
            shape((tokens, 1024), low),
            shape((2, 2 * block, 128), full),
            shape((tokens, width), low),
            shape((16, 2 * block, 128), low),
            shape(kv, low),
            shape((width, pack_kv.shape[1]), low),
            shape((width, pack_qo.shape[1]), low),
            shape((8, tokens, width), low),
            shape((8, tokens, width), low),
            shape((8, EXPERTS, tokens), full),
            shape((2, 3, width, hidden), low),
        ),
        in_specs=[ANY, ANY, VMEM, ANY, VMEM, VMEM, VMEM, VMEM, ANY, ANY, ANY],
        out_specs=(VMEM, VMEM, VMEM) + (ANY,) * 12,
        scratch_shapes=[
            pltpu.VMEM((width, pack_kv.shape[1]), low),
            pltpu.VMEM((width, pack_qo.shape[1]), low),
            pltpu.VMEM(kv, low),
            pltpu.VMEM((16, 2 * block, 128), low),
            pltpu.VMEM((tokens, width), low),
            pltpu.VMEM((tokens, 1024), low),
            pltpu.VMEM((tokens, width), full),
            pltpu.VMEM((2, 2 * block, 128), full),
            dma((2, n_deep)), dma((2, n_deep)),
            dma((2, n_deep, 4)), dma((2, n_deep, 4)),
            dma((2, n_deep, 4)), dma((2, n_deep, 4)),
            dma((back + 1,)), dma((back + 1,)),
            dma((back + 1,)), dma((back + 1,)),
            dma((9,)), dma((9,)), dma((9,)), dma((9,)), dma((8,)), dma((8,)), dma((3,)),
            dma((3, total)), dma((3, total)), dma((3,)),
            dma, dma, dma((2,)), dma((8,)),
        ],
        compiler_params=pltpu.CompilerParams(
            collective_id=1, has_side_effects=True, vmem_limit_bytes=60 << 20
        ),
        name="forward",
    )(pack_kv, pack_qo, x, g, cosine, sine, start, picks, gate, up, down)


def experts_kernel(
    n_seq, xs_in, gs_in, gates_in, w_in, hidden_in, layer_out, dx_out, dg_out, grad_out,
    xs, gs, gates, w, acc, mids, thirds_got, second_got, last_got, dg_made, dg_got, half_made, half_got,
    t_send, t_recv, s_send, s_recv, l_send, l_recv, dg_send, dg_recv, load, half_send, half_recv, done_sem,
):
    row, seq = lax.axis_index("row"), lax.axis_index("seq")
    core, chip_z = seq % 2, seq // 2 % 2
    tokens, width = hidden_in.shape
    ff = w.shape[1] // 6
    mine = (row * 2 + chip_z) * 2
    low, full = jnp.bfloat16, jnp.float32
    sibling = (row, seq // 2 * 2 + (1 - core))
    thirds = thirds_of(tokens)
    columns = ((0, 0), (0, 1), (1, 0), (1, 1), (0, 2), (1, 2))
    loads = [
        pltpu.make_async_copy(w_in.at[j, kind], w.at[:, pl.ds(col * ff, ff)], load.at[col])
        for col, (j, kind) in enumerate(columns)
    ]
    loads += [
        pltpu.make_async_copy(source, target, load.at[6 + i])
        for i, (source, target) in enumerate(((xs_in, xs), (gs_in, gs), (gates_in, gates)))
    ]
    for copy in loads:
        copy.start()
    barrier = pltpu.get_barrier_semaphore()

    def greet(step, carry):
        pl.semaphore_signal(barrier, inc=1, device_id=peer_of(row, seq, step), device_id_type=MESH)
        return carry

    lax.fori_loop(1, 8, greet, 0)
    pl.semaphore_signal(barrier, inc=1, device_id=sibling, device_id_type=MESH)
    acc[...] = jnp.zeros_like(acc)
    pl.semaphore_wait(barrier, 8)
    for copy in loads:
        copy.wait()

    def dg_copy(step):
        return remote(dg_made.at[step], dg_got.at[step], dg_send.at[step], dg_recv.at[step], peer_of(row, seq, step))

    results = (xs, gs)

    def third_copy(i, which):
        rows = pl.ds(*thirds[i])
        return remote(results[which].at[7, rows], thirds_got.at[which, rows], t_send.at[which, i], t_recv.at[which, i],
                      peer_of(row, seq, (1, 2, 4)[i]))

    def second_copy(i, which):
        return remote(results[which].at[(6, 5, 3)[i]], second_got.at[which, i], s_send.at[which, i], s_recv.at[which, i],
                      peer_of(row, seq, (2, 4, 1)[i]))

    def last_copy(i, which):
        slot = (4, 1, 2)[i]
        return remote(results[which].at[slot], last_got.at[which, i], l_send.at[which, i], l_recv.at[which, i],
                      peer_of(row, seq, slot))

    def relay_third(i):
        for which in range(2):
            rows, slot = pl.ds(*thirds[i]), (6, 5, 3)[i]
            third_copy(i, which).wait_recv()
            results[which][slot, rows] = (
                results[which][slot, rows].astype(full) + thirds_got[which, rows].astype(full)
            ).astype(low)
            second_copy(i, which).start()

    def relay_second(i):
        for which in range(2):
            slot = (4, 1, 2)[i]
            second_copy(i, which).wait_recv()
            results[which][slot] = (
                results[which][slot].astype(full) + second_got[which, i].astype(full)
            ).astype(low)
            last_copy(i, which).start()

    def block(index, carry):
        step = 7 - index + jnp.where(index == 3, -1, 0) + jnp.where(index == 4, 1, 0)
        step = jnp.where(index == 5, 1, jnp.where(index == 6, 2, step))
        x, g = xs[step], gs[step]
        for j in range(2):
            gate = column(gates[step, pl.ds(mine + j, 1)])[:, :1]
            a = mul(x, w[:, 2 * j * ff:(2 * j + 1) * ff], NN)
            b = mul(x, w[:, (2 * j + 1) * ff:(2 * j + 2) * ff], NN)
            back = RESIDUAL * mul(g, w[:, (4 + j) * ff:(5 + j) * ff], NN)
            sigma = jax.nn.sigmoid(a)
            smooth = a * sigma
            inner = smooth * b
            dgate = jnp.sum(inner * back, axis=1, keepdims=True)
            back = gate * back
            mids[:, (4 + j) * ff:(5 + j) * ff] = (gate * inner).astype(low)
            mids[:, 2 * j * ff:(2 * j + 1) * ff] = (back * b * (sigma + smooth * (1.0 - sigma))).astype(low)
            mids[:, (2 * j + 1) * ff:(2 * j + 2) * ff] = (back * smooth).astype(low)
            dg_made[step, j] = jnp.broadcast_to(dgate, (tokens, 128)).T[:8]
        for lo in range(0, width, 256):
            part = slice(lo, lo + 256)
            acc[part, :4 * ff] += mul(xs[step, :, part], mids[:, :4 * ff], TN)
            acc[part, 4 * ff:] += mul(gs[step, :, part], mids[:, 4 * ff:], TN)
        for lo in range(0, width, 256):
            part = slice(lo, lo + 256)
            xs[step, :, part] = mul(mids[:, 4 * ff:], w[part, 4 * ff:], NT).astype(low)
            gs[step, :, part] = mul(mids[:, :4 * ff], w[part, :4 * ff], NT).astype(low)

        @pl.when(index < 7)
        def _():
            dg_copy(step).start()

        @pl.when(index == 0)
        def _():
            for i in range(3):
                for which in range(2):
                    third_copy(i, which).start()

        for i in range(3):
            @pl.when(index == 1 + i)
            def _():
                relay_third(i)

            @pl.when(index == 5 + i)
            def _():
                relay_second(i)

        return carry

    lax.fori_loop(0, 8, block, 0)

    def share_of(j):
        wide = acc[:, pl.ds(pl.multiple_of(j * 2 * ff, 128), 2 * ff)]
        thin = RESIDUAL * acc[:, pl.ds(pl.multiple_of((4 + j) * ff, 128), ff)]
        return wide, thin

    wide, thin = share_of(1 - core)
    half_made[:, :2 * ff] = wide.astype(low)
    half_made[:, 2 * ff:] = thin.astype(low)
    half = remote(half_made, half_got, half_send, half_recv, sibling)
    half.start()
    dg_got[0] = dg_made[0]
    half.wait_recv()
    wide, thin = share_of(core)
    half_got[:, :2 * ff] = (wide + half_got[:, :2 * ff].astype(full)).astype(low)
    half_got[:, 2 * ff:] = (thin + half_got[:, 2 * ff:].astype(full)).astype(low)
    store = pltpu.make_async_copy(half_got, grad_out, done_sem)
    store.start()

    def settle(step, carry):
        dg_copy(step).wait()
        return carry

    lax.fori_loop(1, 8, settle, 0)

    def place(step, carry):
        other_row, other_seq = peer_of(row, seq, step)
        chip = other_row * 2 + other_seq // 2 % 2
        for j in range(2):
            dg_out[pl.ds(chip * 2 + j, 1)] = dg_got[step, j, :1]
        return carry

    lax.fori_loop(0, 8, place, 0)
    for i in range(3):
        for which in range(2):
            last_copy(i, which).wait_recv()
    dx_out[...] = gs[0].astype(full) + sum(last_got[1, i].astype(full) for i in range(3))
    mixture = xs[0].astype(full) + sum(last_got[0, i].astype(full) for i in range(3))
    layer_out[...] = (hidden_in[...] + RESIDUAL * mixture).astype(low)
    for i in range(3):
        for which in range(2):
            third_copy(i, which).wait_send()
            second_copy(i, which).wait_send()
            last_copy(i, which).wait_send()
    half.wait_send()
    store.wait()


def run_experts(n_row, n_seq, xs, gs, gates, w, hidden):
    _, tokens, width = xs.shape
    ff = w.shape[3]
    low, full = jnp.bfloat16, jnp.float32
    dma, shape = pltpu.SemaphoreType.DMA, jax.ShapeDtypeStruct
    return pl.pallas_call(
        functools.partial(experts_kernel, n_seq),
        out_shape=(
            shape((tokens, width), low),
            shape((tokens, width), full),
            shape((EXPERTS, tokens), full),
            shape((width, 3 * ff), low),
        ),
        in_specs=[ANY, ANY, ANY, ANY, VMEM],
        out_specs=(VMEM, VMEM, VMEM, ANY),
        scratch_shapes=[
            pltpu.VMEM((8, tokens, width), low),
            pltpu.VMEM((8, tokens, width), low),
            pltpu.VMEM((8, EXPERTS, tokens), full),
            pltpu.VMEM((width, 6 * ff), low),
            pltpu.VMEM((width, 6 * ff), full),
            pltpu.VMEM((tokens, 6 * ff), low),
            pltpu.VMEM((2, tokens, width), low),
            pltpu.VMEM((2, 3, tokens, width), low),
            pltpu.VMEM((2, 3, tokens, width), low),
            pltpu.VMEM((8, 2, 8, tokens), full),
            pltpu.VMEM((8, 2, 8, tokens), full),
            pltpu.VMEM((width, 3 * ff), low),
            pltpu.VMEM((width, 3 * ff), low),
            dma((2, 3)), dma((2, 3)), dma((2, 3)), dma((2, 3)), dma((2, 3)), dma((2, 3)),
            dma((8,)), dma((8,)), dma((9,)),
            dma, dma, dma,
        ],
        compiler_params=pltpu.CompilerParams(
            collective_id=3, has_side_effects=True, vmem_limit_bytes=60 << 20
        ),
        name="experts",
    )(xs, gs, gates, w, hidden)


def backward_kernel(
    n_row, n_seq, back,
    w_kv_in, w_qo_in, kv_in, queries_in, normed_in, mixed_in, x_in, g_in, cos_in, sin_in, start_in,
    hidden_in, xtwo_in, gates_in, dgates_in, dx_in, lse_in, expert_grads,
    input_out, q_out, k_out, v_out, o_out, small_out, held,
    w_kv, w_qo, kv, queries, outs, dq, dqkv, dkv_own, dkv_core, dkv_deep,
    grads_o, grads_q, grads_k, core_o, core_q, core_k, plane_o, plane_q, plane_k, deep_o, deep_q, deep_k,
    load, k_send, k_recv, kd_send, kd_recv, e_send, e_recv, e_local,
    d_send, d_recv, p_send, p_recv, z_send, z_recv,
):
    row, seq = lax.axis_index("row"), lax.axis_index("seq")
    core, deep, n_deep = seq % 2, seq // 2, n_seq // 2
    me, total = row * n_seq + seq, n_row * n_seq
    sibling = (row, deep * 2 + (1 - core))
    rows = q_out.shape[0]
    tokens, width = x_in.shape
    block = tokens // 2
    low, full = jnp.bfloat16, jnp.float32
    slots = kv.shape[0]
    loads = [
        pltpu.make_async_copy(source, target, load.at[i])
        for i, (source, target) in enumerate(((w_kv_in, w_kv), (w_qo_in, w_qo), (kv_in, kv), (queries_in, queries)))
    ]
    for copy in loads:
        copy.start()
    greet_all(n_row, n_seq)

    def expert_copy(step):
        other = (me + step) % total
        return remote(
            expert_grads.at[pl.ds(pl.multiple_of(other * rows, rows), rows)],
            held.at[seq // 4, row * 4 + seq % 4],
            e_send.at[step], e_recv.at[step], (other // n_seq, other % n_seq),
        )

    expert_own = pltpu.make_async_copy(
        expert_grads.at[pl.ds(pl.multiple_of(me * rows, rows), rows)],
        held.at[seq // 4, row * 4 + seq % 4], e_local,
    )
    expert_own.start()

    def experts_start(lo, hi):
        def start_experts(index, carry):
            expert_copy(index * STRIDE % total).start()
            return carry

        lax.fori_loop(lo, hi, start_experts, 0)

    experts_start(1, total * 5 // 8)
    for copy in loads:
        copy.wait()

    made, from_core = (grads_o, grads_q, grads_k), (core_o, core_q, core_k)
    from_plane, from_deep = (plane_o, plane_q, plane_k), (deep_o, deep_q, deep_k)

    def part(of_row, of_deep, of_core):
        return pl.ds(pl.multiple_of((of_row * n_seq + of_deep * 2 + of_core) * rows, rows), rows)

    def d_copy(kind, step, hop):
        there = part(row_of(row, step), (deep + hop) % n_deep, 1 - core)
        return remote(made[kind].at[there], from_core[kind].at[hop, step], d_send.at[kind, hop, step],
                      d_recv.at[kind, hop, step], sibling)

    def p_copy(kind, step, hop):
        there = part(row_of(row, step), (deep + hop) % n_deep, core)
        return remote(made[kind].at[there], from_plane[kind].at[hop, step - 1], p_send.at[kind, hop, step],
                      p_recv.at[kind, hop, step], (row_of(row, step), seq))

    def z_copy(kind, hop):
        there = part(row, (deep + hop) % n_deep, core)
        return remote(made[kind].at[there], from_deep[kind].at[hop], z_send.at[kind, hop], z_recv.at[kind, hop],
                      (row, (deep + hop) % n_deep * 2 + core))

    def dense_start(kind):
        def start_d(index, carry):
            d_copy(kind, 3 - index % 4, n_deep - 1 - index // 4).start()
            return carry

        lax.fori_loop(0, 4 * n_deep, start_d, 0)

    def dense_cores(kind):
        def sum_cores(index, carry):
            step, hop = 3 - index % 4, n_deep - 1 - index // 4
            d_copy(kind, step, hop).wait_recv()
            there = part(row_of(row, step), (deep + hop) % n_deep, core)
            made[kind][there] = (made[kind][there].astype(full) + from_core[kind][hop, step].astype(full)).astype(low)

            @pl.when(step > 0)
            def _():
                p_copy(kind, step, hop).start()

            return carry

        lax.fori_loop(0, 4 * n_deep, sum_cores, 0)

    def dense_plane(kind):
        def sum_plane(index, carry):
            hop = n_deep - 1 - index
            there = part(row, (deep + hop) % n_deep, core)
            for step in range(1, 4):
                p_copy(kind, step, hop).wait_recv()
            value = made[kind][there].astype(full)
            for step in range(1, 4):
                value += from_plane[kind][hop, step - 1].astype(full)
            made[kind][there] = value.astype(low)

            @pl.when(hop > 0)
            def _():
                z_copy(kind, hop).start()

            return carry

        lax.fori_loop(0, n_deep, sum_plane, 0)

    def dense_end(kind):
        value = made[kind][part(row, deep, core)].astype(full)
        for hop in range(1, n_deep):
            z_copy(kind, hop).wait_recv()
            value += from_deep[kind][hop].astype(full)
        return value


    def upright(value):
        return jnp.concatenate([value, jnp.zeros((128 - value.shape[0], tokens), full)], axis=0).T

    small = w_kv[:, 1024:].astype(full).T
    gain_one, gain_two = small[16:17], small[17:18]
    gates, dgates = upright(gates_in[...]), upright(dgates_in[...])
    dlogits = (gates * (dgates - jnp.sum(gates * dgates, axis=1, keepdims=True))).astype(low)
    dxtwo = dx_in[...] + mul(dlogits, w_kv[:, 1024:], NT)
    h = hidden_in[...]
    scale_two = norm_scale(h)
    weighted = gain_two * dxtwo
    dgain_two = jnp.sum(dxtwo * h * scale_two, axis=0, keepdims=True)
    input_out[...] = (
        g_in[...].astype(full)
        + scale_two * weighted
        - h * (scale_two * scale_two * scale_two) * jnp.mean(weighted * h, axis=1, keepdims=True)
    )
    dbranch = (RESIDUAL * input_out[...]).astype(low)
    drouter = mul(xtwo_in[...], dlogits, TN)
    for lo in range(0, width, 256):
        grads_o[lo:lo + 256] = mul(dbranch[:, lo:lo + 256], mixed_in[...], TN).astype(low)
    dense_start(0)

    half_lane = lax.broadcasted_iota(jnp.int32, (block, 128), 1) < 64
    for head in range(8):
        both = mul(dbranch, w_qo[:, 1024 + 128 * head:1152 + 128 * head], NN)
        for t in range(2):
            value = both[block * t:block * (t + 1)]
            other = pltpu.roll(value, 64, 1)
            if head % 2 == 0:
                first, second = jnp.where(half_lane, value, 0.0), jnp.where(half_lane, other, 0.0)
            else:
                first, second = jnp.where(half_lane, 0.0, other), jnp.where(half_lane, 0.0, value)
            outs[t * 8 + head, :block] = first.astype(low)
            outs[t * 8 + head, block:] = second.astype(low)

    dense_cores(0)

    lane = lax.broadcasted_iota(jnp.int32, (tokens, 128), 1)
    for t in range(2):
        visible = visibility(deep, seq, slots, block, start_in[block * t:block * (t + 1)])

        def attend(pair, carry):
            lanes = pl.ds(pl.multiple_of(128 * pair, 128), 128)
            value_lanes = pl.ds(pl.multiple_of(512 + 128 * pair, 128), 128)
            keys = jnp.concatenate([kv[slot, t, :, lanes] for slot in range(slots)], axis=0)
            values = jnp.concatenate([kv[slot, t, :, value_lanes] for slot in range(slots)], axis=0)
            dk, dv = 0.0, 0.0
            for half in range(2):
                head = 2 * pair + half
                query, dout = queries[t * 8 + head], outs[t * 8 + head]
                scores = jnp.where(visible, SCORE_SCALE * mul(query, keys, NT), NEGATIVE)
                total_log = jnp.sum(jnp.where(lane == head, lse_in[t], 0.0), axis=1, keepdims=True)
                probs = jnp.exp(scores - total_log)
                dprobs = mul(dout, values, NT)
                inner = jnp.sum(probs * dprobs, axis=1, keepdims=True)
                dscores = (probs * (dprobs - inner)).astype(low)
                dquery = SCORE_SCALE * mul(dscores, keys, NN)
                if half == 0:
                    joined = jnp.where(half_lane, dquery[:block], pltpu.roll(dquery[block:], 64, 1))
                else:
                    joined = jnp.where(half_lane, pltpu.roll(dquery[:block], 64, 1), dquery[block:])
                dq[block * t:block * (t + 1), pl.ds(pl.multiple_of(128 * head, 128), 128)] = joined
                dk += SCORE_SCALE * mul(dscores, query, TN)
                dv += mul(probs.astype(low), dout, TN)
            for slot in range(slots):
                kv[slot, t, :, lanes] = dk[block * slot:block * (slot + 1)].astype(low)
                kv[slot, t, :, value_lanes] = dv[block * slot:block * (slot + 1)].astype(low)

            @pl.when(core == 0)
            def _():
                dkv_own[t, :, lanes] = dk[:block]
                dkv_own[t, :, value_lanes] = dv[:block]

            @pl.when(core == 1)
            def _():
                dkv_own[t, :, lanes] = dk[block:2 * block]
                dkv_own[t, :, value_lanes] = dv[block:2 * block]

            return carry

        lax.fori_loop(0, 4, attend, 0)
        if t == 0:
            dense_plane(0)

    def kd_copy(hop):
        return remote(kv.at[hop * 2 + (1 - core)], dkv_core.at[hop], kd_send.at[hop], kd_recv.at[hop], sibling)

    def k_copy(hop):
        return remote(kv.at[hop * 2 + core], dkv_deep.at[hop - 1], k_send.at[hop], k_recv.at[hop], (row, seq - 2))

    def k_sum(hop):
        kd_copy(hop).wait_recv()
        kv[hop * 2 + core] = (kv[hop * 2 + core].astype(full) + dkv_core[hop].astype(full)).astype(low)
        if hop < back:
            @pl.when(deep + 1 < n_deep)
            def _():
                k_copy(hop + 1).wait_recv()
                kv[hop * 2 + core] = (kv[hop * 2 + core].astype(full) + dkv_deep[hop].astype(full)).astype(low)

        k_copy(hop).start()

    for hop in range(back, -1, -1):
        @pl.when(deep >= hop)
        def _():
            kd_copy(hop).start()

    @pl.when(deep >= back)
    def _():
        k_sum(back)

    cosine, sine = cos_in[...], sin_in[...]

    def turn_back(value):
        return value * cosine - jnp.where(lane % 64 < 32, pltpu.roll(value, 96, 1), pltpu.roll(value, 32, 1)) * sine

    for head in range(8):
        lanes = slice(128 * head, 128 * (head + 1))
        dqkv[:, lanes] = turn_back(dq[:, lanes]).astype(low)
    for lo in range(0, width, 256):
        grads_q[lo:lo + 256] = mul(normed_in[:, lo:lo + 256], dqkv[:, :1024], TN).astype(low)
    dense_start(1)
    for hop in range(back - 1, 0, -1):
        @pl.when(deep >= hop)
        def _():
            k_sum(hop)

    for lo in range(0, width, 256):
        part_q = slice(lo, lo + 256)
        dq[:, part_q] = mul(dqkv[:, :1024], w_qo[part_q, :1024], NT)
    dense_cores(1)
    experts_start(total * 5 // 8, total)
    kd_copy(0).wait_recv()
    dkv_own[...] += dkv_core[0].astype(full)

    @pl.when(deep + 1 < n_deep)
    def _():
        k_copy(1).wait_recv()
        dkv_own[...] += dkv_deep[0].astype(full)

    for pair in range(4):
        lanes = slice(128 * pair, 128 * (pair + 1))
        value_lanes = slice(512 + 128 * pair, 640 + 128 * pair)
        dkey = jnp.concatenate([dkv_own[0, :, lanes], dkv_own[1, :, lanes]], axis=0)
        dqkv[:, 1024 + 128 * pair:1152 + 128 * pair] = turn_back(dkey).astype(low)
        dvalue = jnp.concatenate([dkv_own[0, :, value_lanes], dkv_own[1, :, value_lanes]], axis=0)
        dqkv[:, 1536 + 128 * pair:1664 + 128 * pair] = dvalue.astype(low)
    for lo in range(0, width, 256):
        grads_k[lo:lo + 256, :1024] = mul(normed_in[:, lo:lo + 256], dqkv[:, 1024:], TN).astype(low)
    x = x_in[...].astype(full)
    scale_one = norm_scale(x)
    for lo in range(0, width, 256):
        part_k = slice(lo, lo + 256)
        dq[:, part_k] += mul(dqkv[:, 1024:], w_kv[part_k, :1024], NT)
    dxone = dq[...]
    weighted = gain_one * dxone
    dgain_one = jnp.sum(dxone * x * scale_one, axis=0, keepdims=True)
    wide = lax.broadcasted_iota(jnp.int32, (width, 128), 1)
    grads_k[:, 1024:] = jnp.where(
        wide == 16, column(dgain_one), jnp.where(wide == 17, column(dgain_two), drouter)
    ).astype(low)
    dense_start(2)
    dense_plane(1)
    input_out[...] = (
        input_out[...]
        + scale_one * weighted
        - x * (scale_one * scale_one * scale_one) * jnp.mean(weighted * x, axis=1, keepdims=True)
    )
    dense_cores(2)
    dense_plane(2)
    o_out[...] = dense_end(0)
    q_out[...] = dense_end(1)
    last = dense_end(2)
    k_out[...] = last[:, :512]
    v_out[...] = last[:, 512:1024]
    small_out[...] = last[:, 1024:]
    for kind in range(3):
        def settle_d(index, carry):
            hop, step = index // 4, index % 4
            d_copy(kind, step, hop).wait_send()

            @pl.when(step > 0)
            def _():
                p_copy(kind, step, hop).wait_send()

            return carry

        lax.fori_loop(0, 4 * n_deep, settle_d, 0)

        def settle_z(hop, carry):
            z_copy(kind, hop).wait_send()
            return carry

        lax.fori_loop(1, n_deep, settle_z, 0)

    for hop in range(back + 1):
        @pl.when(deep >= hop)
        def _():
            kd_copy(hop).wait_send()
            if hop > 0:
                k_copy(hop).wait_send()

    expert_own.wait()

    def settle_experts(step, carry):
        other = (me + total - step) % total
        expert_copy(step).wait_send()
        there = held.at[other % n_seq // 4, other // n_seq * 4 + other % 4]
        remote(there, there, e_send.at[step], e_recv.at[step], sibling).wait_recv()
        return carry

    lax.fori_loop(1, total, settle_experts, 0)


def window_of(length, block, n_deep):
    return min((length // 2 + 2 * block - 1) // (2 * block), n_deep - 1)


def run_backward(n_row, n_seq, length, w_kv, w_qo, kv, queries, normed, mixed, x, g, cosine, sine, start,
                 hidden, xtwo, gates, dgates, dx, lse, expert_grads):
    tokens, width = x.shape
    total, n_deep = n_row * n_seq, n_seq // 2
    rows, block = width // total, tokens // 2
    back = window_of(length, block, n_deep)
    columns = (1024, 1024, w_kv.shape[1])
    low, full = jnp.bfloat16, jnp.float32
    dma, shape = pltpu.SemaphoreType.DMA, jax.ShapeDtypeStruct
    return pl.pallas_call(
        functools.partial(backward_kernel, n_row, n_seq, back),
        out_shape=(
            shape((tokens, width), full),
            shape((rows, 1024), full),
            shape((rows, 512), full),
            shape((rows, 512), full),
            shape((rows, 1024), full),
            shape((rows, 128), full),
            shape((n_seq // 4, n_row * 4, rows, expert_grads.shape[1]), low),
        ),
        in_specs=[ANY] * 4 + [VMEM] * 13 + [ANY],
        out_specs=(VMEM,) * 6 + (ANY,),
        scratch_shapes=[
            pltpu.VMEM(w_kv.shape, low),
            pltpu.VMEM(w_qo.shape, low),
            pltpu.VMEM(kv.shape, low),
            pltpu.VMEM((16, tokens, 128), low),
            pltpu.VMEM((16, tokens, 128), low),
            pltpu.VMEM((tokens, 1024), full),
            pltpu.VMEM((tokens, 2048), low),
            pltpu.VMEM(kv.shape[1:], full),
            pltpu.VMEM((back + 1,) + kv.shape[1:], low),
            pltpu.VMEM((back,) + kv.shape[1:], low),
        ]
        + [pltpu.VMEM((width, c), low) for c in columns]
        + [pltpu.VMEM((n_deep, 4, rows, c), low) for c in columns]
        + [pltpu.VMEM((n_deep, 3, rows, c), low) for c in columns]
        + [pltpu.VMEM((n_deep, rows, c), low) for c in columns]
        + [
            dma((4,)),
            dma((back + 1,)), dma((back + 1,)), dma((back + 1,)), dma((back + 1,)),
            dma((total,)), dma((total,)), dma,
            dma((3, n_deep, 4)), dma((3, n_deep, 4)), dma((3, n_deep, 4)), dma((3, n_deep, 4)),
            dma((3, n_deep)), dma((3, n_deep)),
        ],
        compiler_params=pltpu.CompilerParams(
            collective_id=2, has_side_effects=True, vmem_limit_bytes=62 << 20
        ),
        name="backward",
    )(w_kv, w_qo, kv, queries, normed, mixed, x, g, cosine, sine, start, hidden, xtwo, gates, dgates, dx, lse,
      expert_grads)


def body(
    n_row,
    n_seq,
    tokens,
    segment_ids,
    expert_ids,
    norm1_gain,
    w_query,
    w_key,
    w_value,
    w_out,
    norm2_gain,
    w_router,
    w_gate,
    w_up,
    w_down,
    out_grad,
):
    row_count, block_len, width = tokens.shape
    token_count = row_count * block_len
    length = segment_ids.shape[1]
    rows, ff = w_query.shape[0], w_gate.shape[2]
    first = lax.axis_index("seq") * block_len
    low, full = jnp.bfloat16, jnp.float32

    routes = expert_ids.reshape(token_count, TOPK)
    picks = jnp.sum(
        (routes[:, :, None] == jnp.arange(128, dtype=jnp.int32)[None, None, :]).astype(full), axis=1
    )
    counts = jnp.concatenate([jnp.sum(picks, axis=0)[None, :EXPERTS], jnp.zeros((rows - 1, EXPERTS), full)])
    pack_kv = jnp.concatenate(
        [w_key, w_value, w_router, norm1_gain[:, None], norm2_gain[:, None],
         jnp.zeros((rows, 14), low), counts.astype(low), jnp.zeros((rows, 80), low)],
        axis=1,
    )
    pack_qo = jnp.concatenate([w_query, w_out.T], axis=1)
    local_segments = lax.dynamic_slice_in_dim(segment_ids, first, block_len, axis=1)
    start = jnp.sum(
        (segment_ids[:, None, :] < local_segments[:, :, None]).astype(jnp.int32), axis=2
    ).reshape(token_count)
    positions = jnp.tile(first + jnp.arange(block_len, dtype=jnp.int32), row_count) - start
    cosine, sine = rope_tables(positions, HEAD)
    cosine = jnp.concatenate([cosine, cosine], axis=1)
    sine = jnp.concatenate([-sine[:, :32], sine[:, 32:]] * 2, axis=1)
    start = jnp.broadcast_to(start[:, None], (token_count, 128))

    x = tokens.reshape(token_count, width)
    g = out_grad.reshape(token_count, width)
    (xtwo, gates, count_rows, hidden, mixed, lse, normed, queries, kv, w_kv, w_qo, group_g, group_x, group_gates, expert_weights) = run_forward(
        n_row, n_seq, length, pack_kv, pack_qo, x, g, cosine, sine, start, picks, w_gate, w_up, jnp.swapaxes(w_down, 1, 2)
    )
    expert_counts = count_rows[0, 32:32 + EXPERTS].astype(jnp.int32)
    layer_out, dx, dgates, expert_grads = run_experts(
        n_row, n_seq, group_x, group_g, group_gates, expert_weights, hidden
    )
    input_grad, dq, dk, dv, do, small, held = run_backward(
        n_row, n_seq, length, w_kv, w_qo, kv, queries, normed, mixed, x, g, cosine, sine, start,
        hidden, xtwo, gates, dgates, dx, lse, expert_grads,
    )
    grads = jnp.sum(held.astype(full), axis=0)
    return (
        layer_out.reshape(row_count, block_len, width),
        input_grad.reshape(row_count, block_len, width),
        small[:, 16],
        dq,
        dk,
        dv,
        do.T,
        small[:, 17],
        small[:, :EXPERTS],
        grads[:, :, :ff],
        grads[:, :, ff:2 * ff],
        jnp.swapaxes(grads[:, :, 2 * ff:], 1, 2),
        expert_counts,
    )


def solution(mesh):
    in_specs = (
        P("row", "seq", None),
        P("row", None),
        P("seq", "row", None, None),
        P(("row", "seq")),
        P(("row", "seq"), None),
        P(("row", "seq"), None),
        P(("row", "seq"), None),
        P(None, ("row", "seq")),
        P(("row", "seq")),
        P(("row", "seq"), None),
        P(None, ("row", "seq"), None),
        P(None, ("row", "seq"), None),
        P(None, None, ("row", "seq")),
        P("row", "seq", None),
    )
    out_specs = (
        P("row", "seq", None),
        P("row", "seq", None),
        P(("row", "seq")),
        P(("row", "seq"), None),
        P(("row", "seq"), None),
        P(("row", "seq"), None),
        P(None, ("row", "seq")),
        P(("row", "seq")),
        P(("row", "seq"), None),
        P(None, ("row", "seq"), None),
        P(None, ("row", "seq"), None),
        P(None, None, ("row", "seq")),
        P(),
    )
    return jax.shard_map(
        functools.partial(body, mesh.shape["row"], mesh.shape["seq"]),
        mesh=mesh,
        in_specs=in_specs,
        out_specs=out_specs,
        check_vma=False,
    )
```

time: 503 us -> 405 us (0.81); the launches traced: 496 us -> 404 us
  Pallas kernels: 471 us -> 379 us
    pallas_call x1, Pallas kernels: 182 us -> 142 us  [run_backward(): pl.pallas_call(functools.partial(backward_kernel, n_row, n_seq, back), ou...]
    pallas_call x1, Pallas kernels: 119 us -> 84.1 us  [run_experts(): pl.pallas_call(functools.partial(experts_kernel, n_seq), out_shape=(shape...]
    pallas_call x1, Pallas kernels: 170 us -> 153 us  [run_forward(): pl.pallas_call(functools.partial(forward_kernel, n_row, n_seq, back), out...]
where the time goes in v3:
time: 405 us; the launch traced here: 404 us
  Pallas kernels  379 us (94%)
  local copies, waits for them, and re-layouts  15 us (4%)
  other arithmetic  9.27 us (2%)
    pallas_call x1, Pallas kernels, run_forward(): pl.pallas_call(functools.partial(forward_kernel, n_row, n_seq, back), out...  153 us
    pallas_call x1, Pallas kernels, run_backward(): pl.pallas_call(functools.partial(backward_kernel, n_row, n_seq, back), ou...  142 us
    pallas_call x1, Pallas kernels, run_experts(): pl.pallas_call(functools.partial(experts_kernel, n_seq), out_shape=(shape...  84.1 us

profile of v3, /device:TPU:0, one launch (start us, length us, event | category | flops | bytes accessed | tf_op | source)
XLA Modules:
  0.0 403.9 jit_solution(8081890565291965049)
XLA Ops:
  0.7 0.7 constant_dynamic-slice_fusion
  1.3 0.9 convert_reduce_fusion.3
  2.3 0.8 copy.38
  3.1 0.8 copy.39
  3.8 0.8 copy.37
  4.6 0.1 broadcast_multiply_fusion
  4.7 0.8 broadcast_in_dim.32.start_in
  5.5 0.8 copy.36
  6.3 1.1 convert_reduce_fusion.1
  7.4 1.5 concatenate.19.pack_kv
  8.9 1.5 pad_maximum_fusion.pack_qo
  10.4 0.5 fusion
  11.0 0.1 slice_negate_fusion
  11.1 0.9 pad_maximum_fusion.2
  12.0 152.8 %forward.1 = (bf16[256,1024]{1,0:T(8,128)(2,1)}, f32[16,256]{1,0:T(8,128)}, f32[8,128]{1,0:T(8,128)}, f32[256,1024]{1,0:T(8,128)}, bf16[256,1024]{1,0:T(8,128)(2...) custom-call(bf16[32,1152]{1,0:T(8,128)(2,1)} %concatenate.19.pack_kv, ...), custom_call_target="tpu_custom_call" | custom-call | tf_op jit(solution)/shard_map/forward/pallas_call | solution.py:495
  164.7 84.1 %experts.1 = (bf16[256,1024]{1,0:T(8,128)(2,1)}, f32[256,1024]{1,0:T(8,128)}, f32[16,256]{1,0:T(8,128)}, bf16[1024,1536]{1,0:T(8,128)(2,1)}) custom-call(bf16[8,256,1024]{2,1,0:T(8,128)(2,1)} %get-tuple-element.39.xs_in, bf16[8,256,1024]{2,1,0:T(8,128)(2,1)} %get-tuple-element.40.gs_in, f32[8,16,256]{2,1,0:T(8,128)} %get-tuple-element.41.gates_in, ...), custom_call_target="tpu_custom_call" | custom-call | tf_op jit(solution)/shard_map/experts/pallas_call | solution.py:717
  248.8 141.9 %backward.1 = (f32[256,1024]{1,0:T(8,128)}, f32[32,1024]{1,0:T(8,128)}, f32[32,512]{1,0:T(8,128)}, f32[32,512]{1,0:T(8,128)}, f32[32,1024]{1,0:T(8,128)}, /*inde...) custom-call(bf16[1024,1152]{1,0:T(8,128)(2,1)} %get-tuple-element.45.w_kv_in, ...), custom_call_target="tpu_custom_call" | custom-call | tf_op jit(solution)/shard_map/backward/pallas_call | solution.py:1101
  390.8 1.3 convert_bitcast_fusion
  392.0 1.5 slice_reduce_fusion
  393.5 1.4 copy.40
  394.9 2.8 convert_reduce_fusion
  397.7 0.0 copy-start.1
  397.7 0.0 copy-start
  397.7 1.8 slice_bitcast_fusion
  399.5 0.0 copy-start.3
  399.5 0.0 copy-start.5
  399.5 0.0 copy-start.4
  399.5 0.0 copy-start.2
  399.5 0.0 copy-done.1
  399.5 0.8 copy.47
  400.3 0.0 copy-done
  400.3 1.0 copy.48
  401.3 0.0 copy-done.3
  401.3 0.7 copy.49
  401.9 0.0 copy-done.5
  402.0 0.6 copy.50
  402.6 0.0 copy-done.4
  402.6 0.6 copy.51
  403.2 0.0 copy-done.2
  403.2 0.7 copy.52
  (7 shorter events, 0.0 us)
Async XLA Ops:
  397.7 1.8 copy-start.1
  397.7 2.6 copy-start
  399.5 1.8 copy-start.3
  399.5 2.4 copy-start.5
  399.5 3.1 copy-start.4
  399.5 3.7 copy-start.2

commit v4 on v3

--- a/solution.py
+++ b/solution.py
@@ -2,6 +2,7 @@
 
 import jax
 import jax.numpy as jnp
+import numpy as np
 from jax import lax
 from jax.experimental import pallas as pl
 from jax.experimental.pallas import tpu as pltpu
@@ -27,15 +28,7 @@
     return lax.rsqrt(jnp.mean(value * value, axis=-1, keepdims=True) + EPSILON)
 
 
-def rope_tables(positions, width):
-    half = width // 2
-    frequency = THETA ** (-2.0 * jnp.arange(half, dtype=jnp.float32) / width)
-    angle = positions.astype(jnp.float32)[..., None] * frequency
-    angle = jnp.concatenate([angle, angle], axis=-1)
-    return (jnp.cos(angle), jnp.sin(angle))
-
-
-def greet_all(n_row, n_seq):
+def greet_all(n_row, n_seq, wait=True):
     row, seq = lax.axis_index("row"), lax.axis_index("seq")
     me, total = row * n_seq + seq, n_row * n_seq
     barrier = pltpu.get_barrier_semaphore()
@@ -48,7 +41,8 @@
         return carry
 
     lax.fori_loop(1, total, greet, 0)
-    pl.semaphore_wait(barrier, total - 1)
+    if wait:
+        pl.semaphore_wait(barrier, total - 1)
 
 
 NN = (((1,), (0,)), ((), ()))
@@ -132,10 +126,10 @@
 
 def forward_kernel(
     n_row, n_seq, back,
-    pack_kv, pack_qo, x_in, g_in, cos_in, sin_in, start_in, picks_in, gate, up, down,
-    xtwo_out, gates_out, counts_out, hidden_out, mixed_out, lse_out, normed_out, queries_out, kv_out,
+    key_in, value_in, query_in, out_in, small_in, turns_in, segments_in, ids_in, x_in, g_in, gate, up, down,
+    cos_in, sin_in, start_in, xtwo_out, gates_out, counts_out, hidden_out, mixed_out, lse_out, normed_out, queries_out, kv_out,
     w_kv_out, w_qo_out, g_out, xs_out, gates_all, held,
-    w_kv, w_qo, kv, queries, normed, mixed, hidden, lse,
+    pack_kv, pack_qo, upright, picks_in, w_kv, w_qo, kv, queries, normed, mixed, hidden, lse,
     z_send, z_recv, p_send, p_recv, d_send, d_recv, kv_send, kv_recv, kvd_send, kvd_recv,
     g_send, g_recv, x_send, x_recv, gate_send, gate_recv, group_local, e_send, e_recv, e_local, pass_send, pass_recv, local, store,
 ):
@@ -143,13 +137,31 @@
     core, deep, n_deep = seq % 2, seq // 2, n_seq // 2
     me, total = row * n_seq + seq, n_row * n_seq
     sibling = (row, deep * 2 + (1 - core))
-    rows = pack_kv.shape[0]
+    rows = key_in.shape[0]
     tokens, width = x_in.shape
     block = tokens // 2
     low, full = jnp.bfloat16, jnp.float32
     slots = kv.shape[0]
     packs, walls = (pack_kv, pack_qo), (w_kv, w_qo)
-    greet_all(n_row, n_seq)
+    greet_all(n_row, n_seq, False)
+
+    sublane = lax.broadcasted_iota(jnp.int32, (128, 128), 0)
+    for t in range(2):
+        chosen = jnp.zeros((128, block), full)
+        for choice in range(TOPK):
+            chosen += jnp.where(ids_in[t, choice:choice + 1] == sublane, 1.0, 0.0)
+        picks_in[block * t:block * (t + 1)] = chosen.T
+    count = jnp.broadcast_to(jnp.sum(picks_in[...], axis=0, keepdims=True), (8, 128))
+    upright[...] = jnp.zeros_like(upright)
+    upright[:small_in.shape[0], :rows] = small_in[...]
+    small = upright[...].T[:rows]
+    counts = jnp.where(sublane[:rows] == 0, pltpu.roll(count, 32, 1)[:1], 0.0)
+    pack_kv[:, :512] = key_in[...]
+    pack_kv[:, 512:1024] = value_in[...]
+    pack_kv[:, 1024:] = (small + counts).astype(low)
+    pack_qo[:, :1024] = query_in[...]
+    pack_qo[:, 1024:] = out_in[...]
+    pl.semaphore_wait(pltpu.get_barrier_semaphore(), total - 1)
 
     def part(kind, of_row, of_deep, of_core):
         start = (of_row * n_seq + of_deep * 2 + of_core) * rows
@@ -234,13 +246,13 @@
         for kind, source in enumerate(sources)
     ]
 
-    def experts_start(*kinds):
+    def experts_start(lo, hi):
         def start_experts(index, carry):
-            for kind in kinds:
+            for kind in range(3):
                 expert_copy(kind, sources[kind], index * STRIDE % total).start()
             return carry
 
-        lax.fori_loop(1, total, start_experts, 0)
+        lax.fori_loop(lo, hi, start_experts, 0)
 
     g_one, g_two, g_three, g_last, g_sent = tree_rounds(row, seq, g_in, g_out, g_send, g_recv)
     g_own = pltpu.make_async_copy(g_in, g_out.at[0], group_local.at[0])
@@ -250,9 +262,22 @@
     for copy in expert_own:
         copy.start()
     g_own.start()
-    experts_start(0, 1, 2)
+    experts_start(1, total * 5 // 8)
     x = x_in[...].astype(full)
     scale_one = norm_scale(x)
+    for t in range(2):
+        own = segments_in[t:t + 1, pl.ds(pl.multiple_of(seq * block, block), block)].astype(full)
+        own = column(own)
+        smaller = jnp.zeros((block, 128), full)
+        for lo in range(0, segments_in.shape[1], 128):
+            smaller += jnp.where(segments_in[t:t + 1, lo:lo + 128].astype(full) < own, 1.0, 0.0)
+        begin = jnp.broadcast_to(jnp.sum(smaller, axis=1, keepdims=True), (block, 128))
+        start_in[block * t:block * (t + 1)] = begin.astype(jnp.int32)
+        place = lax.broadcasted_iota(jnp.int32, (block, 128), 0) + seq * block
+        angle = (place.astype(full) - begin) * turns_in[:1]
+        cos_in[block * t:block * (t + 1)] = jnp.cos(angle)
+        sin_in[block * t:block * (t + 1)] = jnp.sin(angle) * turns_in[1:2]
+
     dense_relay(0)
     dense_finish(0)
     small = w_kv[:, 1024:].astype(full)
@@ -331,6 +356,7 @@
             kv_pass(hop, 1 - core).wait_recv()
 
     g_two()
+    experts_start(total * 5 // 8, total)
     for t in range(2):
         visible = visibility(deep, seq, slots, block, start_in[block * t:block * (t + 1)])
 
@@ -481,7 +507,7 @@
     return jnp.concatenate(tiles, axis=1) > 0.5
 
 
-def run_forward(n_row, n_seq, length, pack_kv, pack_qo, x, g, cosine, sine, start, picks, gate, up, down):
+def run_forward(n_row, n_seq, length, key, value, query, out, small, turns, segments, ids, x, g, gate, up, down):
     tokens, width = x.shape
     experts, rows, hidden = gate.shape
     total, n_deep = n_row * n_seq, n_seq // 2
@@ -495,6 +521,9 @@
     return pl.pallas_call(
         functools.partial(forward_kernel, n_row, n_seq, back),
         out_shape=(
+            shape((tokens, 128), full),
+            shape((tokens, 128), full),
+            shape((tokens, 128), jnp.int32),
             shape((tokens, width), low),
             shape((EXPERTS, tokens), full),
             shape((8, 128), full),
@@ -504,18 +533,22 @@
             shape((tokens, width), low),
             shape((16, 2 * block, 128), low),
             shape(kv, low),
-            shape((width, pack_kv.shape[1]), low),
-            shape((width, pack_qo.shape[1]), low),
+            shape((width, 1152), low),
+            shape((width, 2048), low),
             shape((8, tokens, width), low),
             shape((8, tokens, width), low),
             shape((8, EXPERTS, tokens), full),
             shape((2, 3, width, hidden), low),
         ),
-        in_specs=[ANY, ANY, VMEM, ANY, VMEM, VMEM, VMEM, VMEM, ANY, ANY, ANY],
-        out_specs=(VMEM, VMEM, VMEM) + (ANY,) * 12,
+        in_specs=[VMEM] * 9 + [ANY] * 4,
+        out_specs=(VMEM,) * 6 + (ANY,) * 12,
         scratch_shapes=[
-            pltpu.VMEM((width, pack_kv.shape[1]), low),
-            pltpu.VMEM((width, pack_qo.shape[1]), low),
+            pltpu.VMEM((rows, 1152), low),
+            pltpu.VMEM((rows, 2048), low),
+            pltpu.VMEM((128, 128), full),
+            pltpu.VMEM((tokens, 128), full),
+            pltpu.VMEM((width, 1152), low),
+            pltpu.VMEM((width, 2048), low),
             pltpu.VMEM(kv, low),
             pltpu.VMEM((16, 2 * block, 128), low),
             pltpu.VMEM((tokens, width), low),
@@ -535,7 +568,7 @@
             collective_id=1, has_side_effects=True, vmem_limit_bytes=60 << 20
         ),
         name="forward",
-    )(pack_kv, pack_qo, x, g, cosine, sine, start, picks, gate, up, down)
+    )(key, value, query, out, small, turns, segments, ids, x, g, gate, up, down)
 
 
 def experts_kernel(
@@ -756,7 +789,7 @@
     input_out, q_out, k_out, v_out, o_out, small_out, held,
     w_kv, w_qo, kv, queries, outs, dq, dqkv, dkv_own, dkv_core, dkv_deep,
     grads_o, grads_q, grads_k, core_o, core_q, core_k, plane_o, plane_q, plane_k, deep_o, deep_q, deep_k,
-    load, k_send, k_recv, kd_send, kd_recv, e_send, e_recv, e_local,
+    spread_out, load, k_send, k_recv, kd_send, kd_recv, e_send, e_recv, e_local,
     d_send, d_recv, p_send, p_recv, z_send, z_recv,
 ):
     row, seq = lax.axis_index("row"), lax.axis_index("seq")
@@ -1046,7 +1079,8 @@
     last = dense_end(2)
     k_out[...] = last[:, :512]
     v_out[...] = last[:, 512:1024]
-    small_out[...] = last[:, 1024:]
+    spread_out[:rows] = last[:, 1024:]
+    small_out[...] = spread_out[...].T
     for kind in range(3):
         def settle_d(index, carry):
             hop, step = index // 4, index % 4
@@ -1106,7 +1140,7 @@
             shape((rows, 512), full),
             shape((rows, 512), full),
             shape((rows, 1024), full),
-            shape((rows, 128), full),
+            shape((128, 128), full),
             shape((n_seq // 4, n_row * 4, rows, expert_grads.shape[1]), low),
         ),
         in_specs=[ANY] * 4 + [VMEM] * 13 + [ANY],
@@ -1128,6 +1162,7 @@
         + [pltpu.VMEM((n_deep, 3, rows, c), low) for c in columns]
         + [pltpu.VMEM((n_deep, rows, c), low) for c in columns]
         + [
+            pltpu.VMEM((128, 128), full),
             dma((4,)),
             dma((back + 1,)), dma((back + 1,)), dma((back + 1,)), dma((back + 1,)),
             dma((total,)), dma((total,)), dma,
@@ -1140,6 +1175,67 @@
         name="backward",
     )(w_kv, w_qo, kv, queries, normed, mixed, x, g, cosine, sine, start, hidden, xtwo, gates, dgates, dx, lse,
       expert_grads)
+
+
+def results_kernel(
+    held, counts, small, *refs
+):
+    passed, copied = refs[:6], refs[6:12]
+    gate_out, up_out, down_out, router_out, one_out, two_out, counts_out = refs[12:]
+    ff = gate_out.shape[2]
+    rows = router_out.shape[1]
+    for source, target in zip(passed[:2], copied[:2]):
+        target[...] = source[...]
+
+    @pl.when(pl.program_id(0) == 0)
+    def _():
+        for source, target in zip(passed[2:], copied[2:]):
+            target[...] = source[...]
+        router_out[...] = small[:EXPERTS, :rows]
+        one_out[...] = small[EXPERTS:EXPERTS + 1, :rows]
+        two_out[...] = small[EXPERTS + 1:EXPERTS + 2, :rows]
+        counts_out[...] = pltpu.roll(counts[...], 96, 1)[:1].astype(jnp.int32)
+
+    for out, lo in ((gate_out, 0), (up_out, ff), (down_out, 2 * ff)):
+        value = held[0, :, :, lo:lo + ff].astype(jnp.float32)
+        for group in range(1, held.shape[0]):
+            value += held[group, :, :, lo:lo + ff].astype(jnp.float32)
+        out[...] = value
+
+
+def run_results(held, counts, small, *passed):
+    groups, experts, rows, wide = held.shape
+    ff, full = wide // 3, jnp.float32
+    some = experts // 4
+    shape = jax.ShapeDtypeStruct
+    whole = lambda i: (0, 0)
+    moved = [pl.BlockSpec((a.shape[0] // 4, a.shape[1]), lambda i: (i, 0)) for a in passed[:2]]
+    moved += [pl.BlockSpec(a.shape, whole) for a in passed[2:]]
+    return pl.pallas_call(
+        results_kernel,
+        grid=(4,),
+        out_shape=tuple(shape(a.shape, a.dtype) for a in passed) + (
+            shape((experts, rows, ff), full),
+            shape((experts, rows, ff), full),
+            shape((experts, rows, ff), full),
+            shape((EXPERTS, rows), full),
+            shape((1, rows), full),
+            shape((1, rows), full),
+            shape((1, 128), jnp.int32),
+        ),
+        in_specs=[
+            pl.BlockSpec((groups, some, rows, wide), lambda i: (0, i, 0, 0)),
+            pl.BlockSpec((8, 128), whole),
+            pl.BlockSpec((128, 128), whole),
+        ] + moved,
+        out_specs=tuple(moved) + (pl.BlockSpec((some, rows, ff), lambda i: (i, 0, 0)),) * 3 + (
+            pl.BlockSpec((EXPERTS, rows), whole),
+            pl.BlockSpec((1, rows), whole),
+            pl.BlockSpec((1, rows), whole),
+            pl.BlockSpec((1, 128), whole),
+        ),
+        name="results",
+    )(held, counts, small, *passed)
 
 
 def body(
@@ -1163,37 +1259,21 @@
     row_count, block_len, width = tokens.shape
     token_count = row_count * block_len
     length = segment_ids.shape[1]
-    rows, ff = w_query.shape[0], w_gate.shape[2]
-    first = lax.axis_index("seq") * block_len
-    low, full = jnp.bfloat16, jnp.float32
-
-    routes = expert_ids.reshape(token_count, TOPK)
-    picks = jnp.sum(
-        (routes[:, :, None] == jnp.arange(128, dtype=jnp.int32)[None, None, :]).astype(full), axis=1
-    )
-    counts = jnp.concatenate([jnp.sum(picks, axis=0)[None, :EXPERTS], jnp.zeros((rows - 1, EXPERTS), full)])
-    pack_kv = jnp.concatenate(
-        [w_key, w_value, w_router, norm1_gain[:, None], norm2_gain[:, None],
-         jnp.zeros((rows, 14), low), counts.astype(low), jnp.zeros((rows, 80), low)],
-        axis=1,
-    )
-    pack_qo = jnp.concatenate([w_query, w_out.T], axis=1)
-    local_segments = lax.dynamic_slice_in_dim(segment_ids, first, block_len, axis=1)
-    start = jnp.sum(
-        (segment_ids[:, None, :] < local_segments[:, :, None]).astype(jnp.int32), axis=2
-    ).reshape(token_count)
-    positions = jnp.tile(first + jnp.arange(block_len, dtype=jnp.int32), row_count) - start
-    cosine, sine = rope_tables(positions, HEAD)
-    cosine = jnp.concatenate([cosine, cosine], axis=1)
-    sine = jnp.concatenate([-sine[:, :32], sine[:, 32:]] * 2, axis=1)
-    start = jnp.broadcast_to(start[:, None], (token_count, 128))
-
+    rows = w_query.shape[0]
+    full = jnp.float32
+    small = jnp.concatenate([w_router.T, norm1_gain[None], norm2_gain[None], jnp.zeros((14, rows), norm1_gain.dtype)])
+    lanes = np.arange(128) % HEAD
+    half = HEAD // 2
+    frequency = (THETA ** (-2.0 * (lanes % half) / HEAD)).astype(np.float32)
+    turns = np.zeros((8, 128), np.float32)
+    turns[0], turns[1] = frequency, np.where(lanes < half, -1.0, 1.0)
     x = tokens.reshape(token_count, width)
     g = out_grad.reshape(token_count, width)
-    (xtwo, gates, count_rows, hidden, mixed, lse, normed, queries, kv, w_kv, w_qo, group_g, group_x, group_gates, expert_weights) = run_forward(
-        n_row, n_seq, length, pack_kv, pack_qo, x, g, cosine, sine, start, picks, w_gate, w_up, jnp.swapaxes(w_down, 1, 2)
+    (cosine, sine, start, xtwo, gates, counts, hidden, mixed, lse, normed, queries, kv, w_kv, w_qo,
+     group_g, group_x, group_gates, expert_weights) = run_forward(
+        n_row, n_seq, length, w_key, w_value, w_query, w_out.T, small.astype(full), jnp.asarray(turns), segment_ids,
+        jnp.swapaxes(expert_ids[0], 1, 2), x, g, w_gate, w_up, jnp.swapaxes(w_down, 1, 2)
     )
-    expert_counts = count_rows[0, 32:32 + EXPERTS].astype(jnp.int32)
     layer_out, dx, dgates, expert_grads = run_experts(
         n_row, n_seq, group_x, group_g, group_gates, expert_weights, hidden
     )
@@ -1201,21 +1281,23 @@
         n_row, n_seq, length, w_kv, w_qo, kv, queries, normed, mixed, x, g, cosine, sine, start,
         hidden, xtwo, gates, dgates, dx, lse, expert_grads,
     )
-    grads = jnp.sum(held.astype(full), axis=0)
+    layer_out, input_grad, dq, dk, dv, do, d_gate, d_up, d_down, router, one, two, counts = run_results(
+        held, counts, small, layer_out, input_grad, dq, dk, dv, do
+    )
     return (
         layer_out.reshape(row_count, block_len, width),
         input_grad.reshape(row_count, block_len, width),
-        small[:, 16],
+        one[0],
         dq,
         dk,
         dv,
         do.T,
-        small[:, 17],
-        small[:, :EXPERTS],
-        grads[:, :, :ff],
-        grads[:, :, ff:2 * ff],
-        jnp.swapaxes(grads[:, :, 2 * ff:], 1, 2),
-        expert_counts,
+        two[0],
+        router.T,
+        d_gate,
+        d_up,
+        jnp.swapaxes(d_down, 1, 2),
+        counts[0, :EXPERTS],
     )
 
 

time: 405 us -> 382 us (0.943)
  local copies, waits for them, and re-layouts: 15 us -> 1.27 us
  other arithmetic: 9.27 us -> 1.4 us
    pallas_call x1, Pallas kernels: 142 us -> 131 us  [run_backward(): pl.pallas_call(functools.partial(backward_kernel, n_row, n_seq, back), ou...]
    unnamed x20 -> x0, local copies, waits for them, and re-layouts: 6.51 us -> none
    pallas_call x1, Pallas kernels: 153 us -> 158 us  [run_forward(): pl.pallas_call(functools.partial(forward_kernel, n_row, n_seq, back), out...]
    pallas_call x0 -> x1, Pallas kernels: none -> 5.29 us  [run_results(): pl.pallas_call(results_kernel, grid=(4,), out_shape=tuple((shape(a.shape,...]
    reduce_sum x3 -> x0, other arithmetic: 4.82 us -> none  [the longest x1 2.81 us: body(): grads = jnp.sum(held.astype(full), axis=0)]
where the time goes in v4:
time: 382 us
  Pallas kernels  378 us (99%)
    pallas_call x1, Pallas kernels, run_forward(): pl.pallas_call(functools.partial(forward_kernel, n_row, n_seq, back), out...  158 us
    pallas_call x1, Pallas kernels, run_backward(): pl.pallas_call(functools.partial(backward_kernel, n_row, n_seq, back), ou...  131 us
    pallas_call x1, Pallas kernels, run_experts(): pl.pallas_call(functools.partial(experts_kernel, n_seq), out_shape=(shape...  83.6 us

profile of v4, /device:TPU:0, one launch (start us, length us, event | category | flops | bytes accessed | tf_op | source)
XLA Modules:
  0.0 381.6 jit_solution(133817382829661723)
XLA Ops:
  0.7 0.1 pad.3.clone
  0.7 1.4 maximum_convert_fusion.small_in
  2.1 158.4 %forward.1 = (f32[256,128]{1,0:T(8,128)}, f32[256,128]{1,0:T(8,128)}, s32[256,128]{1,0:T(8,128)}, bf16[256,1024]{1,0:T(8,128)(2,1)}, f32[16,256]{1,0:T(8,128)}, ...) custom-call(bf16[32,512]{1,0:T(8,128)(2,1)} %key_in.1, ...), custom_call_target="tpu_custom_call" | custom-call | tf_op jit(solution)/shard_map/forward/pallas_call | solution.py:521
  160.5 83.6 %experts.1 = (bf16[256,1024]{1,0:T(8,128)(2,1)}, f32[256,1024]{1,0:T(8,128)}, f32[16,256]{1,0:T(8,128)}, bf16[1024,1536]{1,0:T(8,128)(2,1)}) custom-call(bf16[8,256,1024]{2,1,0:T(8,128)(2,1)} %get-tuple-element.67.xs_in, bf16[8,256,1024]{2,1,0:T(8,128)(2,1)} %get-tuple-element.68.gs_in, f32[8,16,256]{2,1,0:T(8,128)} %get-tuple-element.69.gates_in, ...), custom_call_target="tpu_custom_call" | custom-call | tf_op jit(solution)/shard_map/experts/pallas_call | solution.py:750
  244.1 131.0 %backward.1 = (f32[256,1024]{1,0:T(8,128)}, f32[32,1024]{1,0:T(8,128)}, f32[32,512]{1,0:T(8,128)}, f32[32,512]{1,0:T(8,128)}, f32[32,1024]{1,0:T(8,128)}, /*inde...) custom-call(bf16[1024,1152]{1,0:T(8,128)(2,1)} %get-tuple-element.55.w_kv_in, ...), custom_call_target="tpu_custom_call" | custom-call | tf_op jit(solution)/shard_map/backward/pallas_call | solution.py:1135
  375.2 5.3 %results.1 = (bf16[256,1024]{1,0:T(8,128)(2,1)}, f32[256,1024]{1,0:T(8,128)}, f32[32,1024]{1,0:T(8,128)}, f32[32,512]{1,0:T(8,128)}, f32[32,512]{1,0:T(8,128)}, ...) custom-call(bf16[2,16,32,1536]{3,2,1,0:T(8,128)(2,1)} %get-tuple-ele, ...), custom_call_target="tpu_custom_call" | custom-call | tf_op jit(solution)/shard_map/results/pallas_call | solution.py:1214
  380.4 1.2 slice_bitcast_fusion
  (1 shorter events, 0.0 us)

commit v5 on v4

--- a/solution.py
+++ b/solution.py
@@ -182,6 +182,10 @@
         return remote(here if source is None else source, here, p_send.at[kind, hop, step], p_recv.at[kind, hop, step],
                       (row_of(row, step), seq))
 
+    def corner_copy(kind, step, hop):
+        here = part(kind, row_of(row, step), (deep + n_deep - hop) % n_deep, core)
+        return remote(here, here, p_send.at[kind, hop, 3], p_recv.at[kind, hop, 3], (row_of(row, 3 - step), seq))
+
     def core_copy(kind, step, hop, source):
         here = part(kind, row_of(row, step), (deep + n_deep - hop) % n_deep, core)
         return remote(here if source is None else source, here, d_send.at[kind, hop, step], d_recv.at[kind, hop, step],
@@ -193,7 +197,7 @@
             return carry
 
         lax.fori_loop(1, n_deep, start_z, 0)
-        for step in range(1, 4):
+        for step in range(1, 3):
             plane_copy(kind, step, 0, packs[kind]).start()
         core_copy(kind, 0, 0, packs[kind]).start()
 
@@ -201,7 +205,7 @@
         def relay(hop, carry):
             there = part(kind, row, (deep + n_deep - hop) % n_deep, core)
             remote(there, there, z_send.at[kind, hop], z_recv.at[kind, hop], sibling).wait_recv()
-            for step in range(1, 4):
+            for step in range(1, 3):
                 plane_copy(kind, step, hop, None).start()
             core_copy(kind, 0, hop, None).start()
             return carry
@@ -209,14 +213,28 @@
         lax.fori_loop(1, n_deep, relay, 0)
 
     def dense_finish(kind):
-        def spread(index, carry):
-            hop, step = index // 3, index % 3 + 1
+        def landed(hop, step):
             there = part(kind, row_of(row, step), (deep + n_deep - hop) % n_deep, core)
             remote(there, there, p_send.at[kind, hop, step], p_recv.at[kind, hop, step], sibling).wait_recv()
             core_copy(kind, step, hop, None).start()
-            return carry
-
-        lax.fori_loop(0, n_deep * 3, spread, 0)
+
+        def spread(hop, carry):
+            for step in range(1, 3):
+                landed(hop, step)
+
+                @pl.when(hop % 2 == step - 1)
+                def _():
+                    corner_copy(kind, step, hop).start()
+
+            return carry
+
+        lax.fori_loop(0, n_deep, spread, 0)
+
+        def corner(hop, carry):
+            landed(hop, 3)
+            return carry
+
+        lax.fori_loop(0, n_deep, corner, 0)
         own_copies[kind].wait()
 
         def gathered(index, carry):
@@ -324,6 +342,7 @@
     dense_relay(1)
     g_one()
     dense_finish(1)
+    g_two()
     half_lane = lax.broadcasted_iota(jnp.int32, (block, 128), 1) < 64
     for head in range(8):
         both = turn(mul(normed[...], w_qo[:, 128 * head:128 * (head + 1)], NN))
@@ -348,6 +367,8 @@
 
             kv_pass(hop, core).start()
 
+        if hop == 1:
+            experts_start(total * 5 // 8, total)
 
     kv_pass(0, 1 - core).wait_recv()
     for hop in range(1, back + 1):
@@ -355,20 +376,20 @@
         def _():
             kv_pass(hop, 1 - core).wait_recv()
 
-    g_two()
-    experts_start(total * 5 // 8, total)
+    g_three()
+    places = window_slots(core, slots)
     for t in range(2):
-        visible = visibility(deep, seq, slots, block, start_in[block * t:block * (t + 1)])
+        visible = visibility(seq, slots, block, start_in[block * t:block * (t + 1)])
 
         def attend(pair, carry):
             lanes = pl.ds(pl.multiple_of(128 * pair, 128), 128)
             value_lanes = pl.ds(pl.multiple_of(512 + 128 * pair, 128), 128)
-            values = jnp.concatenate([kv[slot, t, :, value_lanes] for slot in range(slots)], axis=0)
+            values = jnp.concatenate([kv[slot, t, :, value_lanes] for slot in places], axis=0)
             for half in range(2):
                 head = 2 * pair + half
                 query = queries[t * 8 + head]
                 scores = jnp.concatenate(
-                    [mul(query, kv[slot, t, :, lanes], NT) for slot in range(slots)], axis=1
+                    [mul(query, kv[slot, t, :, lanes], NT) for slot in places], axis=1
                 )
                 scores = jnp.where(visible, SCORE_SCALE * scores, NEGATIVE)
                 peak = jnp.max(scores, axis=1, keepdims=True)
@@ -386,7 +407,6 @@
 
         lax.fori_loop(0, 4, attend, 0)
 
-    g_three()
     for lo in range(0, width, 256):
         branch = mul(mixed[...], w_qo[lo:lo + 256, 1024:], NT)
         hidden[:, lo:lo + 256] = x_in[:, lo:lo + 256].astype(full) + RESIDUAL * branch
@@ -427,9 +447,6 @@
     for copy in stores:
         copy.start()
 
-    x_two()
-    x_three()
-
     def arrived(step, carry):
         other = (me + total - step) % total
         for kind in range(3):
@@ -450,6 +467,8 @@
     lax.fori_loop(1, total, settle_experts, 0)
     g_last()
     g_sent()
+    x_two()
+    x_three()
     x_last()
     x_sent()
     for copy in group_own:
@@ -471,9 +490,13 @@
             hop, step = index // 4, index % 4
             core_copy(kind, step, hop, None).wait_send()
 
-            @pl.when(step > 0)
+            @pl.when((step > 0) & (step < 3))
             def _():
                 plane_copy(kind, step, hop, None).wait_send()
+
+            @pl.when((step > 0) & (step < 3) & (hop % 2 == step - 1))
+            def _():
+                corner_copy(kind, step, hop).wait_send()
 
             return carry
 
@@ -496,12 +519,16 @@
     remote(held.at[core], held.at[core], pass_send, pass_recv, sibling).wait_send()
 
 
-def visibility(deep, seq, slots, block, start):
+def window_slots(core, slots):
+    return [(d + 1 - core) // 2 * 2 + (core + d) % 2 for d in range(slots - 1)]
+
+
+def visibility(seq, slots, block, start):
     key = lax.broadcasted_iota(jnp.int32, (block, block), 1)
     query = lax.broadcasted_iota(jnp.int32, (block, block), 0) + seq * block
     tiles = []
-    for slot in range(slots):
-        position = key + ((deep - slot // 2) * 2 + slot % 2) * block
+    for d in range(slots - 1):
+        position = key + (seq - d) * block
         seen = jnp.where((position >= start) & (position <= query), 1.0, 0.0)
         tiles.append(jnp.concatenate([seen, seen], axis=0))
     return jnp.concatenate(tiles, axis=1) > 0.5
@@ -589,11 +616,16 @@
         pltpu.make_async_copy(w_in.at[j, kind], w.at[:, pl.ds(col * ff, ff)], load.at[col])
         for col, (j, kind) in enumerate(columns)
     ]
+    loads.append(pltpu.make_async_copy(gates_in, gates, load.at[6]))
     loads += [
-        pltpu.make_async_copy(source, target, load.at[6 + i])
-        for i, (source, target) in enumerate(((xs_in, xs), (gs_in, gs), (gates_in, gates)))
+        pltpu.make_async_copy(source.at[7], target.at[7], load.at[7 + i])
+        for i, (source, target) in enumerate(((xs_in, xs), (gs_in, gs)))
     ]
-    for copy in loads:
+    others = [
+        pltpu.make_async_copy(source.at[pl.ds(0, 7)], target.at[pl.ds(0, 7)], load.at[9 + i])
+        for i, (source, target) in enumerate(((xs_in, xs), (gs_in, gs)))
+    ]
+    for copy in loads + others:
         copy.start()
     barrier = pltpu.get_barrier_semaphore()
 
@@ -648,6 +680,11 @@
     def block(index, carry):
         step = 7 - index + jnp.where(index == 3, -1, 0) + jnp.where(index == 4, 1, 0)
         step = jnp.where(index == 5, 1, jnp.where(index == 6, 2, step))
+        @pl.when(index == 1)
+        def _():
+            for copy in others:
+                copy.wait()
+
         x, g = xs[step], gs[step]
         for j in range(2):
             gate = column(gates[step, pl.ds(mine + j, 1)])[:, :1]
@@ -772,7 +809,7 @@
             pltpu.VMEM((width, 3 * ff), low),
             pltpu.VMEM((width, 3 * ff), low),
             dma((2, 3)), dma((2, 3)), dma((2, 3)), dma((2, 3)), dma((2, 3)), dma((2, 3)),
-            dma((8,)), dma((8,)), dma((9,)),
+            dma((8,)), dma((8,)), dma((11,)),
             dma, dma, dma,
         ],
         compiler_params=pltpu.CompilerParams(
@@ -831,8 +868,7 @@
         lax.fori_loop(lo, hi, start_experts, 0)
 
     experts_start(1, total * 5 // 8)
-    for copy in loads:
-        copy.wait()
+    loads[0].wait()
 
     made, from_core = (grads_o, grads_q, grads_k), (core_o, core_q, core_k)
     from_plane, from_deep = (plane_o, plane_q, plane_k), (deep_o, deep_q, deep_k)
@@ -927,6 +963,7 @@
         grads_o[lo:lo + 256] = mul(dbranch[:, lo:lo + 256], mixed_in[...], TN).astype(low)
     dense_start(0)
 
+    loads[1].wait()
     half_lane = lax.broadcasted_iota(jnp.int32, (block, 128), 1) < 64
     for head in range(8):
         both = mul(dbranch, w_qo[:, 1024 + 128 * head:1152 + 128 * head], NN)
@@ -942,15 +979,44 @@
 
     dense_cores(0)
 
+    def kd_copy(hop, t):
+        return remote(kv.at[hop * 2 + (1 - core), t], dkv_core.at[hop, t], kd_send.at[hop, t], kd_recv.at[hop, t], sibling)
+
+    def k_copy(hop, t):
+        return remote(kv.at[hop * 2 + core, t], dkv_deep.at[hop - 1, t], k_send.at[hop, t], k_recv.at[hop, t], (row, seq - 2))
+
+    def k_start(t):
+        for hop in range(back, -1, -1):
+            @pl.when(deep >= hop)
+            def _():
+                kd_copy(hop, t).start()
+
+    def k_sum(hop, t):
+        @pl.when(deep >= hop)
+        def _():
+            kd_copy(hop, t).wait_recv()
+            kv[hop * 2 + core, t] = (kv[hop * 2 + core, t].astype(full) + dkv_core[hop, t].astype(full)).astype(low)
+            if hop < back:
+                @pl.when(deep + 1 < n_deep)
+                def _():
+                    k_copy(hop + 1, t).wait_recv()
+                    kv[hop * 2 + core, t] = (kv[hop * 2 + core, t].astype(full) + dkv_deep[hop, t].astype(full)).astype(low)
+
+            k_copy(hop, t).start()
+
     lane = lax.broadcasted_iota(jnp.int32, (tokens, 128), 1)
+    for copy in loads[2:]:
+        copy.wait()
+    places = window_slots(core, slots)
+    kv[jnp.where(core == 0, 1, 2 * back)] = jnp.zeros(kv.shape[1:], low)
     for t in range(2):
-        visible = visibility(deep, seq, slots, block, start_in[block * t:block * (t + 1)])
+        visible = visibility(seq, slots, block, start_in[block * t:block * (t + 1)])
 
         def attend(pair, carry):
             lanes = pl.ds(pl.multiple_of(128 * pair, 128), 128)
             value_lanes = pl.ds(pl.multiple_of(512 + 128 * pair, 128), 128)
-            keys = jnp.concatenate([kv[slot, t, :, lanes] for slot in range(slots)], axis=0)
-            values = jnp.concatenate([kv[slot, t, :, value_lanes] for slot in range(slots)], axis=0)
+            keys = jnp.concatenate([kv[slot, t, :, lanes] for slot in places], axis=0)
+            values = jnp.concatenate([kv[slot, t, :, value_lanes] for slot in places], axis=0)
             dk, dv = 0.0, 0.0
             for half in range(2):
                 head = 2 * pair + half
@@ -969,52 +1035,23 @@
                 dq[block * t:block * (t + 1), pl.ds(pl.multiple_of(128 * head, 128), 128)] = joined
                 dk += SCORE_SCALE * mul(dscores, query, TN)
                 dv += mul(probs.astype(low), dout, TN)
-            for slot in range(slots):
-                kv[slot, t, :, lanes] = dk[block * slot:block * (slot + 1)].astype(low)
-                kv[slot, t, :, value_lanes] = dv[block * slot:block * (slot + 1)].astype(low)
-
-            @pl.when(core == 0)
-            def _():
-                dkv_own[t, :, lanes] = dk[:block]
-                dkv_own[t, :, value_lanes] = dv[:block]
-
-            @pl.when(core == 1)
-            def _():
-                dkv_own[t, :, lanes] = dk[block:2 * block]
-                dkv_own[t, :, value_lanes] = dv[block:2 * block]
-
+            for d, slot in enumerate(places[1:], 1):
+                kv[slot, t, :, lanes] = dk[block * d:block * (d + 1)].astype(low)
+                kv[slot, t, :, value_lanes] = dv[block * d:block * (d + 1)].astype(low)
+            dkv_own[t, :, lanes] = dk[:block]
+            dkv_own[t, :, value_lanes] = dv[:block]
             return carry
 
         lax.fori_loop(0, 4, attend, 0)
+        k_start(t)
         if t == 0:
             dense_plane(0)
-
-    def kd_copy(hop):
-        return remote(kv.at[hop * 2 + (1 - core)], dkv_core.at[hop], kd_send.at[hop], kd_recv.at[hop], sibling)
-
-    def k_copy(hop):
-        return remote(kv.at[hop * 2 + core], dkv_deep.at[hop - 1], k_send.at[hop], k_recv.at[hop], (row, seq - 2))
-
-    def k_sum(hop):
-        kd_copy(hop).wait_recv()
-        kv[hop * 2 + core] = (kv[hop * 2 + core].astype(full) + dkv_core[hop].astype(full)).astype(low)
-        if hop < back:
-            @pl.when(deep + 1 < n_deep)
-            def _():
-                k_copy(hop + 1).wait_recv()
-                kv[hop * 2 + core] = (kv[hop * 2 + core].astype(full) + dkv_deep[hop].astype(full)).astype(low)
-
-        k_copy(hop).start()
-
-    for hop in range(back, -1, -1):
-        @pl.when(deep >= hop)
-        def _():
-            kd_copy(hop).start()
-
-    @pl.when(deep >= back)
-    def _():
-        k_sum(back)
-
+            k_sum(back, 0)
+
+
+    for hop in range(back - 1, 0, -1):
+        k_sum(hop, 0)
+    k_sum(back, 1)
     cosine, sine = cos_in[...], sin_in[...]
 
     def turn_back(value):
@@ -1027,22 +1064,21 @@
         grads_q[lo:lo + 256] = mul(normed_in[:, lo:lo + 256], dqkv[:, :1024], TN).astype(low)
     dense_start(1)
     for hop in range(back - 1, 0, -1):
-        @pl.when(deep >= hop)
-        def _():
-            k_sum(hop)
+        k_sum(hop, 1)
 
     for lo in range(0, width, 256):
         part_q = slice(lo, lo + 256)
         dq[:, part_q] = mul(dqkv[:, :1024], w_qo[part_q, :1024], NT)
     dense_cores(1)
     experts_start(total * 5 // 8, total)
-    kd_copy(0).wait_recv()
-    dkv_own[...] += dkv_core[0].astype(full)
-
-    @pl.when(deep + 1 < n_deep)
-    def _():
-        k_copy(1).wait_recv()
-        dkv_own[...] += dkv_deep[0].astype(full)
+    for t in range(2):
+        kd_copy(0, t).wait_recv()
+        dkv_own[t] += dkv_core[0, t].astype(full)
+
+        @pl.when(deep + 1 < n_deep)
+        def _():
+            k_copy(1, t).wait_recv()
+            dkv_own[t] += dkv_deep[0, t].astype(full)
 
     for pair in range(4):
         lanes = slice(128 * pair, 128 * (pair + 1))
@@ -1101,11 +1137,12 @@
         lax.fori_loop(1, n_deep, settle_z, 0)
 
     for hop in range(back + 1):
-        @pl.when(deep >= hop)
-        def _():
-            kd_copy(hop).wait_send()
-            if hop > 0:
-                k_copy(hop).wait_send()
+        for t in range(2):
+            @pl.when(deep >= hop)
+            def _():
+                kd_copy(hop, t).wait_send()
+                if hop > 0:
+                    k_copy(hop, t).wait_send()
 
     expert_own.wait()
 
@@ -1120,7 +1157,9 @@
 
 
 def window_of(length, block, n_deep):
-    return min((length // 2 + 2 * block - 1) // (2 * block), n_deep - 1)
+    back = length // 2 // (2 * block)
+    assert back * 4 * block == length and 0 < back < n_deep
+    return back
 
 
 def run_backward(n_row, n_seq, length, w_kv, w_qo, kv, queries, normed, mixed, x, g, cosine, sine, start,
@@ -1164,7 +1203,7 @@
         + [
             pltpu.VMEM((128, 128), full),
             dma((4,)),
-            dma((back + 1,)), dma((back + 1,)), dma((back + 1,)), dma((back + 1,)),
+            dma((back + 1, 2)), dma((back + 1, 2)), dma((back + 1, 2)), dma((back + 1, 2)),
             dma((total,)), dma((total,)), dma,
             dma((3, n_deep, 4)), dma((3, n_deep, 4)), dma((3, n_deep, 4)), dma((3, n_deep, 4)),
             dma((3, n_deep)), dma((3, n_deep)),

time: 382 us -> 367 us (0.961)
  Pallas kernels: 378 us -> 363 us
    pallas_call x1, Pallas kernels: 158 us -> 151 us  [run_forward(): pl.pallas_call(functools.partial(forward_kernel, n_row, n_seq, back), out...]
    pallas_call x1, Pallas kernels: 83.6 us -> 77.4 us  [run_experts(): pl.pallas_call(functools.partial(experts_kernel, n_seq), out_shape=(shape...]
where the time goes in v5:
time: 367 us; the launch traced here: 366 us
  Pallas kernels  363 us (99%)
    pallas_call x1, Pallas kernels, run_forward(): pl.pallas_call(functools.partial(forward_kernel, n_row, n_seq, back), out...  151 us
    pallas_call x1, Pallas kernels, run_backward(): pl.pallas_call(functools.partial(backward_kernel, n_row, n_seq, back), ou...  129 us
    pallas_call x1, Pallas kernels, run_experts(): pl.pallas_call(functools.partial(experts_kernel, n_seq), out_shape=(shape...  77.4 us

profile of v5, /device:TPU:0, one launch (start us, length us, event | category | flops | bytes accessed | tf_op | source)
XLA Modules:
  0.0 366.5 jit_solution(10033237285920003233)
XLA Ops:
  0.7 0.1 pad.3.clone
  0.7 1.4 maximum_convert_fusion.small_in
  2.1 151.5 %forward.1 = (f32[256,128]{1,0:T(8,128)}, f32[256,128]{1,0:T(8,128)}, s32[256,128]{1,0:T(8,128)}, bf16[256,1024]{1,0:T(8,128)(2,1)}, f32[16,256]{1,0:T(8,128)}, ...) custom-call(bf16[32,512]{1,0:T(8,128)(2,1)} %key_in.1, ...), custom_call_target="tpu_custom_call" | custom-call | tf_op jit(solution)/shard_map/forward/pallas_call | solution.py:548
  153.6 77.4 %experts.1 = (bf16[256,1024]{1,0:T(8,128)(2,1)}, f32[256,1024]{1,0:T(8,128)}, f32[16,256]{1,0:T(8,128)}, bf16[1024,1536]{1,0:T(8,128)(2,1)}) custom-call(bf16[8,256,1024]{2,1,0:T(8,128)(2,1)} %get-tuple-element.67.xs_in, bf16[8,256,1024]{2,1,0:T(8,128)(2,1)} %get-tuple-element.68.gs_in, f32[8,16,256]{2,1,0:T(8,128)} %get-tuple-element.69.gates_in, ...), custom_call_target="tpu_custom_call" | custom-call | tf_op jit(solution)/shard_map/experts/pallas_call | solution.py:787
  231.1 128.9 %backward.1 = (f32[256,1024]{1,0:T(8,128)}, f32[32,1024]{1,0:T(8,128)}, f32[32,512]{1,0:T(8,128)}, f32[32,512]{1,0:T(8,128)}, f32[32,1024]{1,0:T(8,128)}, /*inde...) custom-call(bf16[1024,1152]{1,0:T(8,128)(2,1)} %get-tuple-element.55.w_kv_in, ...), custom_call_target="tpu_custom_call" | custom-call | tf_op jit(solution)/shard_map/backward/pallas_call | solution.py:1174
  360.0 5.3 %results.1 = (bf16[256,1024]{1,0:T(8,128)(2,1)}, f32[256,1024]{1,0:T(8,128)}, f32[32,1024]{1,0:T(8,128)}, f32[32,512]{1,0:T(8,128)}, f32[32,512]{1,0:T(8,128)}, ...) custom-call(bf16[2,16,32,1536]{3,2,1,0:T(8,128)(2,1)} %get-tuple-ele, ...), custom_call_target="tpu_custom_call" | custom-call | tf_op jit(solution)/shard_map/results/pallas_call | solution.py:1253
  365.3 1.2 slice_bitcast_fusion
  (1 shorter events, 0.0 us)

commit v6 on v5

--- a/solution.py
+++ b/solution.py
@@ -265,12 +265,12 @@
     ]
 
     def experts_start(lo, hi):
-        def start_experts(index, carry):
-            for kind in range(3):
+        for kind in range(3):
+            def start_experts(index, carry):
                 expert_copy(kind, sources[kind], index * STRIDE % total).start()
-            return carry
-
-        lax.fori_loop(lo, hi, start_experts, 0)
+                return carry
+
+            lax.fori_loop(lo, hi, start_experts, 0)
 
     g_one, g_two, g_three, g_last, g_sent = tree_rounds(row, seq, g_in, g_out, g_send, g_recv)
     g_own = pltpu.make_async_copy(g_in, g_out.at[0], group_local.at[0])
@@ -447,17 +447,20 @@
     for copy in stores:
         copy.start()
 
-    def arrived(step, carry):
-        other = (me + total - step) % total
-        for kind in range(3):
+    def share(kind, of_core):
+        there = held.at[of_core, kind]
+        return remote(there, there, pass_send.at[kind], pass_recv.at[kind], sibling)
+
+    for kind in range(3):
+        def arrived(step, carry):
+            other = (me + total - step) % total
             there = held.at[core, kind, pl.ds(pl.multiple_of(other * rows, rows), rows)]
             remote(there, there, e_send.at[kind, step], e_recv.at[kind, step], sibling).wait_recv()
-        return carry
-
-    lax.fori_loop(1, total, arrived, 0)
-    for copy in expert_own:
-        copy.wait()
-    remote(held.at[core], held.at[core], pass_send, pass_recv, sibling).start()
+            return carry
+
+        lax.fori_loop(1, total, arrived, 0)
+        expert_own[kind].wait()
+        share(kind, core).start()
 
     def settle_experts(step, carry):
         for kind, source in enumerate(sources):
@@ -514,9 +517,9 @@
 
     for copy in stores:
         copy.wait()
-    share = remote(held.at[core], held.at[1 - core], pass_send, pass_recv, sibling)
-    share.wait_recv()
-    remote(held.at[core], held.at[core], pass_send, pass_recv, sibling).wait_send()
+    for kind in range(3):
+        share(kind, core).wait_send()
+        share(kind, 1 - core).wait_recv()
 
 
 def window_slots(core, slots):
@@ -589,7 +592,7 @@
             dma((back + 1,)), dma((back + 1,)),
             dma((9,)), dma((9,)), dma((9,)), dma((9,)), dma((8,)), dma((8,)), dma((3,)),
             dma((3, total)), dma((3, total)), dma((3,)),
-            dma, dma, dma((2,)), dma((8,)),
+            dma((3,)), dma((3,)), dma((2,)), dma((8,)),
         ],
         compiler_params=pltpu.CompilerParams(
             collective_id=1, has_side_effects=True, vmem_limit_bytes=60 << 20
@@ -600,7 +603,7 @@
 
 def experts_kernel(
     n_seq, xs_in, gs_in, gates_in, w_in, hidden_in, layer_out, dx_out, dg_out, grad_out,
-    xs, gs, gates, w, acc, mids, thirds_got, second_got, last_got, dg_made, dg_got, half_made, half_got,
+    xs, gs, gates, w, acc, mids, far, thirds_got, second_got, last_got, dg_made, dg_got, half_made, half_got,
     t_send, t_recv, s_send, s_recv, l_send, l_recv, dg_send, dg_recv, load, half_send, half_recv, done_sem,
 ):
     row, seq = lax.axis_index("row"), lax.axis_index("seq")
@@ -647,11 +650,11 @@
 
     def third_copy(i, which):
         rows = pl.ds(*thirds[i])
-        return remote(results[which].at[7, rows], thirds_got.at[which, rows], t_send.at[which, i], t_recv.at[which, i],
+        return remote(far.at[which, 0, rows], thirds_got.at[which, rows], t_send.at[which, i], t_recv.at[which, i],
                       peer_of(row, seq, (1, 2, 4)[i]))
 
     def second_copy(i, which):
-        return remote(results[which].at[(6, 5, 3)[i]], second_got.at[which, i], s_send.at[which, i], s_recv.at[which, i],
+        return remote(far.at[which, 1 + i], second_got.at[which, i], s_send.at[which, i], s_recv.at[which, i],
                       peer_of(row, seq, (2, 4, 1)[i]))
 
     def last_copy(i, which):
@@ -661,10 +664,10 @@
 
     def relay_third(i):
         for which in range(2):
-            rows, slot = pl.ds(*thirds[i]), (6, 5, 3)[i]
+            rows = pl.ds(*thirds[i])
             third_copy(i, which).wait_recv()
-            results[which][slot, rows] = (
-                results[which][slot, rows].astype(full) + thirds_got[which, rows].astype(full)
+            far[which, 1 + i, rows] = (
+                far[which, 1 + i, rows].astype(full) + thirds_got[which, rows].astype(full)
             ).astype(low)
             second_copy(i, which).start()
 
@@ -677,9 +680,19 @@
             ).astype(low)
             last_copy(i, which).start()
 
-    def block(index, carry):
+    def order(index):
         step = 7 - index + jnp.where(index == 3, -1, 0) + jnp.where(index == 4, 1, 0)
-        step = jnp.where(index == 5, 1, jnp.where(index == 6, 2, step))
+        return jnp.where(index == 5, 1, jnp.where(index == 6, 2, step))
+
+    def weigh(step, kept):
+        for lo in range(0, width, 256):
+            part = slice(lo, lo + 256)
+            acc[part, :4 * ff] += mul(xs[step, :, part], mids[kept, :, :4 * ff], TN)
+            acc[part, 4 * ff:] += mul(gs[step, :, part], mids[kept, :, 4 * ff:], TN)
+
+    def block(is_far, index, carry):
+        step, kept = order(index), index if is_far else 4
+
         @pl.when(index == 1)
         def _():
             for copy in others:
@@ -696,18 +709,22 @@
             inner = smooth * b
             dgate = jnp.sum(inner * back, axis=1, keepdims=True)
             back = gate * back
-            mids[:, (4 + j) * ff:(5 + j) * ff] = (gate * inner).astype(low)
-            mids[:, 2 * j * ff:(2 * j + 1) * ff] = (back * b * (sigma + smooth * (1.0 - sigma))).astype(low)
-            mids[:, (2 * j + 1) * ff:(2 * j + 2) * ff] = (back * smooth).astype(low)
+            mids[kept, :, (4 + j) * ff:(5 + j) * ff] = (gate * inner).astype(low)
+            mids[kept, :, 2 * j * ff:(2 * j + 1) * ff] = (back * b * (sigma + smooth * (1.0 - sigma))).astype(low)
+            mids[kept, :, (2 * j + 1) * ff:(2 * j + 2) * ff] = (back * smooth).astype(low)
             dg_made[step, j] = jnp.broadcast_to(dgate, (tokens, 128)).T[:8]
+        if not is_far:
+            weigh(step, kept)
         for lo in range(0, width, 256):
             part = slice(lo, lo + 256)
-            acc[part, :4 * ff] += mul(xs[step, :, part], mids[:, :4 * ff], TN)
-            acc[part, 4 * ff:] += mul(gs[step, :, part], mids[:, 4 * ff:], TN)
-        for lo in range(0, width, 256):
-            part = slice(lo, lo + 256)
-            xs[step, :, part] = mul(mids[:, 4 * ff:], w[part, 4 * ff:], NT).astype(low)
-            gs[step, :, part] = mul(mids[:, :4 * ff], w[part, :4 * ff], NT).astype(low)
+            y = mul(mids[kept, :, 4 * ff:], w[part, 4 * ff:], NT).astype(low)
+            dx = mul(mids[kept, :, :4 * ff], w[part, :4 * ff], NT).astype(low)
+            if is_far:
+                far[0, index, :, part] = y
+                far[1, index, :, part] = dx
+            else:
+                xs[step, :, part] = y
+                gs[step, :, part] = dx
 
         @pl.when(index < 7)
         def _():
@@ -724,13 +741,20 @@
             def _():
                 relay_third(i)
 
-            @pl.when(index == 5 + i)
+            @pl.when(index == (6, 7, 7)[i])
             def _():
                 relay_second(i)
 
         return carry
 
-    lax.fori_loop(0, 8, block, 0)
+    lax.fori_loop(0, 4, functools.partial(block, True), 0)
+    lax.fori_loop(4, 8, functools.partial(block, False), 0)
+
+    def weigh_far(index, carry):
+        weigh(order(index), index)
+        return carry
+
+    lax.fori_loop(0, 4, weigh_far, 0)
 
     def share_of(j):
         wide = acc[:, pl.ds(pl.multiple_of(j * 2 * ff, 128), 2 * ff)]
@@ -800,7 +824,8 @@
             pltpu.VMEM((8, EXPERTS, tokens), full),
             pltpu.VMEM((width, 6 * ff), low),
             pltpu.VMEM((width, 6 * ff), full),
-            pltpu.VMEM((tokens, 6 * ff), low),
+            pltpu.VMEM((5, tokens, 6 * ff), low),
+            pltpu.VMEM((2, 4, tokens, width), low),
             pltpu.VMEM((2, tokens, width), low),
             pltpu.VMEM((2, 3, tokens, width), low),
             pltpu.VMEM((2, 3, tokens, width), low),
@@ -813,7 +838,7 @@
             dma, dma, dma,
         ],
         compiler_params=pltpu.CompilerParams(
-            collective_id=3, has_side_effects=True, vmem_limit_bytes=60 << 20
+            collective_id=3, has_side_effects=True, vmem_limit_bytes=62 << 20
         ),
         name="experts",
     )(xs, gs, gates, w, hidden)

time: 367 us -> 366 us (level)
  Pallas kernels: 363 us -> 359 us
    pallas_call x1, Pallas kernels: 77.4 us -> 73.6 us  [run_experts(): pl.pallas_call(functools.partial(experts_kernel, n_seq), out_shape=(shape...]
where the time goes in v6:
time: 366 us; the launch traced here: 363 us
  Pallas kernels  359 us (98%)
    pallas_call x1, Pallas kernels, run_forward(): pl.pallas_call(functools.partial(forward_kernel, n_row, n_seq, back), out...  151 us
    pallas_call x1, Pallas kernels, run_backward(): pl.pallas_call(functools.partial(backward_kernel, n_row, n_seq, back), ou...  129 us
    pallas_call x1, Pallas kernels, run_experts(): pl.pallas_call(functools.partial(experts_kernel, n_seq), out_shape=(shape...  73.6 us

profile of v6, /device:TPU:0, one launch (start us, length us, event | category | flops | bytes accessed | tf_op | source)
XLA Modules:
  0.0 362.8 jit_solution(9676436804205053968)
XLA Ops:
  0.7 0.1 pad.3.clone
  0.7 1.4 maximum_convert_fusion.small_in
  2.1 150.9 %forward.1 = (f32[256,128]{1,0:T(8,128)}, f32[256,128]{1,0:T(8,128)}, s32[256,128]{1,0:T(8,128)}, bf16[256,1024]{1,0:T(8,128)(2,1)}, f32[16,256]{1,0:T(8,128)}, ...) custom-call(bf16[32,512]{1,0:T(8,128)(2,1)} %key_in.1, ...), custom_call_target="tpu_custom_call" | custom-call | tf_op jit(solution)/shard_map/forward/pallas_call | solution.py:551
  153.0 73.6 %experts.1 = (bf16[256,1024]{1,0:T(8,128)(2,1)}, f32[256,1024]{1,0:T(8,128)}, f32[16,256]{1,0:T(8,128)}, bf16[1024,1536]{1,0:T(8,128)(2,1)}) custom-call(bf16[8,256,1024]{2,1,0:T(8,128)(2,1)} %get-tuple-element.67.xs_in, bf16[8,256,1024]{2,1,0:T(8,128)(2,1)} %get-tuple-element.68.gs_in, f32[8,16,256]{2,1,0:T(8,128)} %get-tuple-element.69.gates_in, ...), custom_call_target="tpu_custom_call" | custom-call | tf_op jit(solution)/shard_map/experts/pallas_call | solution.py:811
  226.6 129.3 %backward.1 = (f32[256,1024]{1,0:T(8,128)}, f32[32,1024]{1,0:T(8,128)}, f32[32,512]{1,0:T(8,128)}, f32[32,512]{1,0:T(8,128)}, f32[32,1024]{1,0:T(8,128)}, /*inde...) custom-call(bf16[1024,1152]{1,0:T(8,128)(2,1)} %get-tuple-element.55.w_kv_in, ...), custom_call_target="tpu_custom_call" | custom-call | tf_op jit(solution)/shard_map/backward/pallas_call | solution.py:1199
  355.8 5.3 %results.1 = (bf16[256,1024]{1,0:T(8,128)(2,1)}, f32[256,1024]{1,0:T(8,128)}, f32[32,1024]{1,0:T(8,128)}, f32[32,512]{1,0:T(8,128)}, f32[32,512]{1,0:T(8,128)}, ...) custom-call(bf16[2,16,32,1536]{3,2,1,0:T(8,128)(2,1)} %get-tuple-ele, ...), custom_call_target="tpu_custom_call" | custom-call | tf_op jit(solution)/shard_map/results/pallas_call | solution.py:1278
  361.1 1.2 slice_bitcast_fusion
  (1 shorter events, 0.0 us)

commit v7 on v6

--- a/solution.py
+++ b/solution.py
@@ -693,10 +693,11 @@
     def block(is_far, index, carry):
         step, kept = order(index), index if is_far else 4
 
-        @pl.when(index == 1)
-        def _():
-            for copy in others:
-                copy.wait()
+        if is_far:
+            @pl.when(index == 1)
+            def _():
+                for copy in others:
+                    copy.wait()
 
         x, g = xs[step], gs[step]
         for j in range(2):
@@ -730,20 +731,23 @@
         def _():
             dg_copy(step).start()
 
-        @pl.when(index == 0)
-        def _():
+        if is_far:
+            @pl.when(index == 0)
+            def _():
+                for i in range(3):
+                    for which in range(2):
+                        third_copy(i, which).start()
+
             for i in range(3):
-                for which in range(2):
-                    third_copy(i, which).start()
-
-        for i in range(3):
-            @pl.when(index == 1 + i)
-            def _():
-                relay_third(i)
-
-            @pl.when(index == (6, 7, 7)[i])
-            def _():
-                relay_second(i)
+                @pl.when(index == 1 + i)
+                def _():
+                    relay_third(i)
+
+        else:
+            for i in range(3):
+                @pl.when(index == (6, 7, 7)[i])
+                def _():
+                    relay_second(i)
 
         return carry
 

time: 366 us -> 363 us (level)
  no operation moved by 1% of the time
where the time goes in v7:
time: 363 us; the launch traced here: 362 us
  Pallas kernels  359 us (99%)
    pallas_call x1, Pallas kernels, run_forward(): pl.pallas_call(functools.partial(forward_kernel, n_row, n_seq, back), out...  151 us
    pallas_call x1, Pallas kernels, run_backward(): pl.pallas_call(functools.partial(backward_kernel, n_row, n_seq, back), ou...  129 us
    pallas_call x1, Pallas kernels, run_experts(): pl.pallas_call(functools.partial(experts_kernel, n_seq), out_shape=(shape...  73.6 us

profile of v7, /device:TPU:0, one launch (start us, length us, event | category | flops | bytes accessed | tf_op | source)
XLA Modules:
  0.0 362.3 jit_solution(12995759212802268464)
XLA Ops:
  0.7 0.1 pad.3.clone
  0.7 1.4 maximum_convert_fusion.small_in
  2.1 150.9 %forward.1 = (f32[256,128]{1,0:T(8,128)}, f32[256,128]{1,0:T(8,128)}, s32[256,128]{1,0:T(8,128)}, bf16[256,1024]{1,0:T(8,128)(2,1)}, f32[16,256]{1,0:T(8,128)}, ...) custom-call(bf16[32,512]{1,0:T(8,128)(2,1)} %key_in.1, ...), custom_call_target="tpu_custom_call" | custom-call | tf_op jit(solution)/shard_map/forward/pallas_call | solution.py:551
  153.0 73.6 %experts.1 = (bf16[256,1024]{1,0:T(8,128)(2,1)}, f32[256,1024]{1,0:T(8,128)}, f32[16,256]{1,0:T(8,128)}, bf16[1024,1536]{1,0:T(8,128)(2,1)}) custom-call(bf16[8,256,1024]{2,1,0:T(8,128)(2,1)} %get-tuple-element.67.xs_in, bf16[8,256,1024]{2,1,0:T(8,128)(2,1)} %get-tuple-element.68.gs_in, f32[8,16,256]{2,1,0:T(8,128)} %get-tuple-element.69.gates_in, ...), custom_call_target="tpu_custom_call" | custom-call | tf_op jit(solution)/shard_map/experts/pallas_call | solution.py:815
  226.6 129.2 %backward.1 = (f32[256,1024]{1,0:T(8,128)}, f32[32,1024]{1,0:T(8,128)}, f32[32,512]{1,0:T(8,128)}, f32[32,512]{1,0:T(8,128)}, f32[32,1024]{1,0:T(8,128)}, /*inde...) custom-call(bf16[1024,1152]{1,0:T(8,128)(2,1)} %get-tuple-element.55.w_kv_in, ...), custom_call_target="tpu_custom_call" | custom-call | tf_op jit(solution)/shard_map/backward/pallas_call | solution.py:1203
  355.8 5.3 %results.1 = (bf16[256,1024]{1,0:T(8,128)(2,1)}, f32[256,1024]{1,0:T(8,128)}, f32[32,1024]{1,0:T(8,128)}, f32[32,512]{1,0:T(8,128)}, f32[32,512]{1,0:T(8,128)}, ...) custom-call(bf16[2,16,32,1536]{3,2,1,0:T(8,128)(2,1)} %get-tuple-ele, ...), custom_call_target="tpu_custom_call" | custom-call | tf_op jit(solution)/shard_map/results/pallas_call | solution.py:1282
  361.1 1.2 slice_bitcast_fusion
  (1 shorter events, 0.0 us)
